TPU v7x, 32 devices: a whole 2x2x4 slice. The times are simulated.
32 devices in a mesh: grp: 2 (over y), ctx: 4 (over z), ch: 4 (over x, core).
Axes of the slice: x: 2, y: 2, z: 4, core: 2. Of those that a mesh axis runs over, the one named last changes fastest.
Arguments:
- fwd_hidden: bfloat16 [4096, 2048], P(('grp', 'ctx'), 'ch'), parts along dimension 0, may hold values from -6 to 6
- rev_hidden: bfloat16 [4096, 2048], P(('grp', 'ctx'), 'ch'), parts along dimension 0, may hold values from -6 to 6
- bases: int32 [4096], P(('grp', 'ctx')), parts along dimension 0, may hold values from 0 to 3
- complement: int32 [4], replicated, may hold values from 0 to 3, each once
- offsets: int32 [32], P('grp'), parts along dimension 0, may hold values from 0 to 2047, as said below
- base_embed: bfloat16 [4, 2048], P(None, 'ch'), may hold values from -6 to 6
- norm_gain: float32 [2048], replicated, may hold values from 0.1 to 1.9
- in_weight: bfloat16 [4, 2048, 2048], P(None, 'ctx', 'ch'), may hold values from -0.125 to 0.125
- filters: float32 [3, 16, 128], P(None, 'ch'), may hold values from -0.5 to 0.5
- out_weight: bfloat16 [2048, 2048], P('ctx', 'ch'), may hold values from -0.125 to 0.125
Outputs:
- block_out: bfloat16 [4096, 2048], P(('grp', 'ctx'), 'ch'), parts along dimension 0
There are 2 independent parts, one for each index of `grp`. A program takes and returns all parts, laid end to end along the dimension named above; an argument that names none is the same for every part. Nothing has to cross between parts.
Inputs may be any that keep to these rules, and one draw needn't show every extreme that they name: The first offset is 0, the last is 2047, and the offsets rise strictly; each is the first position of a document. `complement`: A permutation of the 4 letters.
All inputs are finite; a program needn't handle non-finite values.
Results may differ from a plain program's by a relative error of at most 0.012.
Values may be sent and summed in bfloat16 or wider, within the bound.
No kernel may reach another device: no remote copies, remote signals or barrier semaphores. Data moves between devices by JAX's collectives and lax.ppermute only.
A program may use at most 64 MiB of HBM per device.

v0:
```python
import jax
import jax.numpy as jnp
from jax import lax
from jax.sharding import PartitionSpec as P


def partner(block, axis, apart):
    count = lax.axis_size(axis)
    route = []
    for low in range(count):
        high = low | 1 << apart
        if high != low and high < count:
            route += [(low, high), (high, low)]
    return lax.ppermute(block, axis, route)


def shifted(value, axis, by):
    count = lax.axis_size(axis)
    pairs = [(i, i + by) for i in range(count) if 0 <= i + by < count]
    return lax.ppermute(value, axis, pairs)


def doc_of(positions, offsets, seq_len):
    count = jnp.sum((offsets[None, :] <= positions[:, None]).astype(jnp.int32), axis=1) - 1
    inside = (positions >= 0) & (positions < seq_len)
    return jnp.where(inside, count, -1)


def toeplitz(taps):
    heads, block = taps.shape
    pattern = jnp.concatenate(
        [jnp.zeros((heads, 1), taps.dtype), taps[:, ::-1], jnp.zeros((heads, block), taps.dtype)],
        axis=1,
    )
    repeated = jnp.tile(pattern, (1, block))
    return repeated[:, : block * 2 * block].reshape(heads, block, 2 * block)


def rms_norm(values, gain):
    floats = values.astype(jnp.float32)
    scale = lax.rsqrt(jnp.mean(floats * floats, axis=-1, keepdims=True) + 1e-05)
    return (floats * scale * gain).astype(jnp.bfloat16)


def blockwise_conv(conv_in, rim, taps, ext_docs):
    rows, width = conv_in.shape
    heads, block = taps.shape
    head_dim = width // heads
    blocks = rows // block
    extended = jnp.concatenate([rim, conv_in], axis=0)
    target_docs = ext_docs[block:].reshape(blocks, block)
    window = jnp.concatenate(
        [
            extended[:rows].reshape(blocks, block, width),
            extended[block:].reshape(blocks, block, width),
        ],
        axis=1,
    )
    window = window.reshape(blocks, 2 * block, heads, head_dim)
    window_docs = jnp.concatenate(
        [ext_docs[:rows].reshape(blocks, block), ext_docs[block:].reshape(blocks, block)], axis=1
    )
    mask = (target_docs[:, :, None] == window_docs[:, None, :]).astype(jnp.bfloat16)
    kernel = toeplitz(taps)[None] * mask[:, None]
    result = jnp.einsum("nhts,nshd->nthd", kernel, window, preferred_element_type=jnp.float32)
    return result.reshape(rows, width)


def local(
    fwd_hidden,
    rev_hidden,
    bases,
    complement,
    offsets,
    base_embed,
    norm_gain,
    in_weight,
    filters,
    out_weight,
):
    rows, width_local = fwd_hidden.shape
    ctx_count = lax.axis_size("ctx")
    here = lax.axis_index("ctx")
    seq_len = rows * ctx_count
    letters = base_embed.shape[0]
    alphabet = jnp.arange(letters, dtype=jnp.int32)
    onehot = (bases[:, None] == alphabet[None, :]).astype(jnp.bfloat16)
    swap_table = (complement[:, None] == alphabet[None, :]).astype(jnp.bfloat16)
    onehot_rev = jnp.dot(onehot, swap_table, preferred_element_type=jnp.float32).astype(
        jnp.bfloat16
    )
    embed_fwd = jnp.dot(onehot, base_embed, preferred_element_type=jnp.float32)
    embed_rev = jnp.dot(onehot_rev, base_embed, preferred_element_type=jnp.float32)
    fwd_input = (fwd_hidden.astype(jnp.float32) + embed_fwd).astype(jnp.bfloat16)
    rev_input = (rev_hidden.astype(jnp.float32) + embed_rev).astype(jnp.bfloat16)
    levels = ctx_count.bit_length() - 1
    for level in range(levels):
        rev_input = partner(rev_input, "ctx", level)
    rev_input = rev_input[::-1]
    full_fwd, full_rev = (
        lax.all_gather(fwd_input, "ch", axis=1, tiled=True),
        lax.all_gather(rev_input, "ch", axis=1, tiled=True),
    )
    normed_fwd = rms_norm(full_fwd, norm_gain)
    normed_rev = rms_norm(full_rev, norm_gain)
    piece = lax.all_gather(in_weight, "ctx", axis=1, tiled=True)
    add_fwd = jnp.einsum("rd,bdc->brc", normed_fwd, piece, preferred_element_type=jnp.float32)
    add_rev = jnp.einsum("rd,bdc->brc", normed_rev, piece, preferred_element_type=jnp.float32)
    taps_all = filters.astype(jnp.bfloat16)
    block = filters.shape[-1]
    before = here * rows - block + jnp.arange(rows + block, dtype=jnp.int32)
    docs_fwd = doc_of(before, offsets, seq_len)
    docs_rev = doc_of(seq_len - 1 - before, offsets, seq_len)
    state_fwd = add_fwd[0]
    state_rev = add_rev[0]
    for section in range(filters.shape[0]):
        in_fwd = state_fwd.astype(jnp.bfloat16)
        in_rev = state_rev.astype(jnp.bfloat16)
        rim_fwd, rim_rev = shifted((in_fwd[-block:], in_rev[-block:]), "ctx", 1)
        conv_rev = blockwise_conv(in_rev, rim_rev, taps_all[section], docs_rev)
        conv_fwd = blockwise_conv(in_fwd, rim_fwd, taps_all[section], docs_fwd)
        state_fwd = add_fwd[section + 1] * conv_fwd
        state_rev = add_rev[section + 1] * conv_rev
    mixed_fwd = state_fwd.astype(jnp.bfloat16)
    mixed_rev = state_rev.astype(jnp.bfloat16)
    for level in range(levels):
        mixed_rev = partner(mixed_rev, "ctx", level)
    mixed_rev = mixed_rev[::-1]
    mixed_sum = (mixed_fwd.astype(jnp.float32) + mixed_rev.astype(jnp.float32)).astype(jnp.bfloat16)
    whole_sum = lax.all_gather(mixed_sum, "ch", axis=1, tiled=True)
    total = jnp.dot(
        whole_sum,
        lax.all_gather(out_weight, "ctx", axis=0, tiled=True),
        preferred_element_type=jnp.float32,
    )
    return total.astype(jnp.bfloat16)


def solution(mesh):
    in_specs = (
        P(("grp", "ctx"), "ch"),
        P(("grp", "ctx"), "ch"),
        P(("grp", "ctx")),
        P(),
        P("grp"),
        P(None, "ch"),
        P(),
        P(None, "ctx", "ch"),
        P(None, "ch", None),
        P("ctx", "ch"),
    )
    out_specs = P(("grp", "ctx"), "ch")
    return jax.shard_map(local, mesh=mesh, in_specs=in_specs, out_specs=out_specs, check_vma=False)
```

profile of v0, /device:TPU:0, one launch (start us, length us, event | category | flops | bytes accessed | tf_op | source)
XLA Modules:
  0.0 390.4 jit_solution(10410948972962377146)
XLA Ops:
  7.2 2.2 fusion.14
  9.5 1.7 fusion.15
  11.2 3.1 collective-permute-start.3
  14.3 11.9 %collective-permute-done.3 = bf16[512,512]{1,0:T(8,128)(2,1)S(1)} collective-permute-done((bf16[512,512]{1,0:T(8,128)(2,1)S(1)}, bf16[512,512]{1,0:T(8,128)(2,1)S(1)}, u32[]{:S(2)}, u32[]{:S(2)}) %collective-permute-start.3) | collective-permute-done | bytes 524320 | tf_op jit(solution)/shard_map/ppermute | solution.py:14
  26.2 2.8 collective-permute-start.4
  28.9 22.6 %collective-permute-done.4 = bf16[512,512]{1,0:T(8,128)(2,1)S(1)} collective-permute-done((bf16[512,512]{1,0:T(8,128)(2,1)S(1)}, bf16[512,512]{1,0:T(8,128)(2,1)S(1)}, u32[]{:S(2)}, u32[]{:S(2)}) %collective-permute-start.4) | collective-permute-done | bytes 524320 | tf_op jit(solution)/shard_map/ppermute | solution.py:14
  51.5 5.1 %rev.21 = bf16[512,512]{1,0:T(8,128)(2,1)} reverse(bf16[512,512]{1,0:T(8,128)(2,1)S(1)} %collective-permute-done.4), dimensions={0} | reverse | bytes 1048576 | tf_op jit(solution)/shard_map/rev | solution.py:99
  64.7 2.4 fusion
  67.1 13.3 %all-gather.10.cloned.1.call-done = bf16[512,2048]{1,0:T(8,128)(2,1)} async-done(((bf16[512,512]{1,0:T(8,128)(2,1)}), bf16[512,2048]{1,0:T(8,128)(2,1)}) %all-gather.10.cloned.1.call-update) | async-done | bytes 2097168 | tf_op jit(solution)/shard_map/all_gather | solution.py:102
  80.4 2.2 fusion.3
  82.6 149.0 %all-gather.8.cloned.1.call-done = bf16[4,2048,512]{2,1,0:T(8,128)(2,1)} async-done(((bf16[4,512,512]{2,1,0:T(8,128)(2,1)}), bf16[4,2048,512]{2,1,0:T(8,128)(2,1)}) %all-gather.8.cloned.1.call-update) | async-done | bytes 8388624 | tf_op jit(solution)/shard_map/all_gather | solution.py:106
  231.7 7.1 %convolution_bitcast_fusion = f32[4,512,512]{2,1,0:T(8,128)S(1)} fusion(bf16[4,2048,512]{2,1,0:T(8,128)(2,1)} %all-gather.8.cloned.1.call-done, bf16[512,2048]{1,0:T(8,128)(2,1)S(1)} %copy-done.10, f32[512]{0:T(512)S(1)} %add_rsqrt_fusion, f32[2048]{0:T(1024)S(1)} %copy-done.14), kind=kOutput, calls=%fused_computation.10 | convolution fusion | flops 4299161600 | bytes 14690304 | tf_op jit(solution)/shard_map/rd,bdc->brc/dot_general | solution.py:108
  243.5 7.7 %convolution_bitcast_fusion.1 = f32[4,512,512]{2,1,0:T(8,128)S(1)} fusion(bf16[4,2048,512]{2,1,0:T(8,128)(2,1)} %all-gather.8.cloned.1.call-done, bf16[512,2048]{1,0:T(8,128)(2,1)} %all-gather.6.cloned.1.call-done, f32[2048]{0:T(1024)S(1)} %copy-done.14, f32[512]{0:T(512)S(1)} %add_rsqrt_fusion.1), kind=kOutput, calls=%fused_computation.11 | convolution fusion | flops 4299161600 | bytes 14690304 | tf_op jit(solution)/shard_map/rd,bdc->brc/dot_general | solution.py:107
  254.6 1.6 squeeze.52
  256.2 1.4 squeeze.51
  257.5 2.0 copy.62
  259.5 1.9 collective-permute-start.5
  261.4 1.6 squeeze.44
  263.0 2.0 convert_element_type.130
  264.9 1.9 copy.52
  266.9 1.6 slice_bitcast_fusion.3
  268.4 3.3 collective-permute-start
  271.7 1.9 pad_maximum_fusion.2
  273.6 2.0 concatenate.90
  276.7 2.8 fusion.41
  280.2 1.4 fusion.18
  283.0 2.7 collective-permute-start.6
  286.5 2.0 concatenate.77
  289.7 2.4 fusion.43
  293.1 1.8 pad_maximum_fusion.1
  294.9 1.9 concatenate.94
  298.0 2.5 fusion.40
  301.1 1.4 fusion.17
  302.5 3.9 %collective-permute-start.7 = (bf16[128,512]{1,0:T(8,128)(2,1)S(1)}, bf16[128,512]{1,0:T(8,128)(2,1)S(1)}, u32[]{:S(2)}, u32[]{:S(2)}) collective-permute-start(bf16[128,512]{1,0:T(8,128)(2,1)S(1)} %slice.179), channel_id=1, source_target_pairs={{0,4},{4,8},{8,12},{1,5},{5,9},{9,13},{2,6},{6,10},{10,14},{3,7},{... | collective-permute-start | bytes 393224 | tf_op jit(solution)/shard_map/ppermute | solution.py:20
  306.5 1.4 fusion.21
  308.5 3.0 collective-permute-start.1
  311.8 1.6 convolution_bitcast_fusion.6
  313.9 2.2 fusion.16
  317.4 2.3 fusion.42
  320.4 7.7 %collective-permute-done.8 = bf16[512,512]{1,0:T(8,128)(2,1)} collective-permute-done((bf16[512,512]{1,0:T(8,128)(2,1)}, bf16[512,512]{1,0:T(8,128)(2,1)}, u32[]{:S(2)}, u32[]{:S(2)}) %collective-permute-start.8) | collective-permute-done | bytes 524320 | tf_op jit(solution)/shard_map/ppermute | solution.py:14
  328.1 1.4 fusion.20
  329.5 2.3 collective-permute-start.2
  331.8 8.1 %collective-permute-done.2 = bf16[128,512]{1,0:T(8,128)(2,1)S(1)} collective-permute-done((bf16[128,512]{1,0:T(8,128)(2,1)S(1)}, bf16[128,512]{1,0:T(8,128)(2,1)S(1)}, u32[]{:S(2)}, u32[]{:S(2)}) %collective-permute-start.2) | collective-permute-done | bytes 131104 | tf_op jit(solution)/shard_map/ppermute | solution.py:20
  340.1 1.6 convolution_bitcast_fusion.7
  342.2 9.0 %collective-permute-done.9 = bf16[512,512]{1,0:T(8,128)(2,1)S(1)} collective-permute-done((bf16[512,512]{1,0:T(8,128)(2,1)}, bf16[512,512]{1,0:T(8,128)(2,1)S(1)}, u32[]{:S(2)}, u32[]{:S(2)}) %collective-permute-start.9) | collective-permute-done | bytes 524320 | tf_op jit(solution)/shard_map/ppermute | solution.py:14
  351.8 2.3 add_convert_fusion
  354.2 25.4 %all-gather.12.cloned.1.call-done = bf16[512,2048]{1,0:T(8,128)(2,1)} async-done(((bf16[512,512]{1,0:T(8,128)(2,1)}), bf16[512,2048]{1,0:T(8,128)(2,1)}) %all-gather.12.cloned.1.call-update) | async-done | bytes 2097168 | tf_op jit(solution)/shard_map/all_gather | solution.py:130
  379.6 4.3 %convolution_convert_fusion = bf16[512,512]{1,0:T(8,128)(2,1)} fusion(bf16[512,2048]{1,0:T(8,128)(2,1)} %all-gather.12.cloned.1.call-done, bf16[2048,512]{1,0:T(8,128)(2,1)} %all-gather.14.cloned.1.call-done), kind=kOutput, calls=%fused_computation.28 | convolution fusion | flops 1074003968 | bytes 4718592 | tf_op jit(solution)/shard_map/dot_general | solution.py:131
  (118 shorter events, 29.5 us)
Async XLA Ops:
  6.5 0.7 copy-start
  6.5 58.2 %all-gather.6.cloned.1.call-start = ((), (), s32[]{:S(2)}) async-start(), calls=%async_computation | async-start | bytes 2621440 | tf_op jit(solution)/shard_map/all_gather | solution.py:101
  9.4 71.0 %all-gather.10.cloned.1.call-start = ((), (), s32[]{:S(2)}) async-start(), calls=%async_computation.2 | async-start | bytes 2621440 | tf_op jit(solution)/shard_map/all_gather | solution.py:102
  11.2 46.9 %copy-start.13 = (s32[16]{0:T(128)S(1)}, s32[16]{0:T(128)}, u32[]{:S(2)}) copy-start(s32[16]{0:T(128)} %param.14) | copy-start | bytes 196
  11.2 47.1 %copy-start.12 = (f32[3,4,128]{2,1,0:T(4,128)S(1)}, f32[3,4,128]{2,1,0:T(4,128)}, u32[]{:S(2)}) copy-start(f32[3,4,128]{2,1,0:T(4,128)} %param.18) | copy-start | bytes 18436
  11.2 15.0 %collective-permute-start.3 = (bf16[512,512]{1,0:T(8,128)(2,1)S(1)}, bf16[512,512]{1,0:T(8,128)(2,1)S(1)}, u32[]{:S(2)}, u32[]{:S(2)}) collective-permute-start(bf16[512,512]{1,0:T(8,128)(2,1)S(1)} %fusion.15), channel_id=1, source_target_pairs={{0,4},{4,0},{8,12},{12,8},{1,5},{5,1},{9,13},{13,9},{2,6},{6,2},{1... | collective-permute-start | bytes 1572872 | tf_op jit(solution)/shard_map/ppermute | solution.py:14
  26.2 25.3 %collective-permute-start.4 = (bf16[512,512]{1,0:T(8,128)(2,1)S(1)}, bf16[512,512]{1,0:T(8,128)(2,1)S(1)}, u32[]{:S(2)}, u32[]{:S(2)}) collective-permute-start(bf16[512,512]{1,0:T(8,128)(2,1)S(1)} %collective-permute-done.3), channel_id=1, source_target_pairs={{0,8},{8,0},{4,12},{12,4},{1,9},{9,1},{5,13},{13,5},{2,10},{10,2},... | collective-permute-start | bytes 1572872 | tf_op jit(solution)/shard_map/ppermute | solution.py:14
  56.7 175.0 %all-gather.8.cloned.1.call-start = ((), (), s32[]{:S(2)}) async-start(), calls=%async_computation.1 | async-start | bytes 10485760 | tf_op jit(solution)/shard_map/all_gather | solution.py:106
  57.4 296.8 %all-gather.14.cloned.1.call-start = ((), (), s32[]{:S(2)}) async-start(), calls=%async_computation.4 | async-start | bytes 2621440 | tf_op jit(solution)/shard_map/all_gather | solution.py:133
  58.0 321.6 %all-gather.12.cloned.1.call-start = ((), (), s32[]{:S(2)}) async-start(), calls=%async_computation.3 | async-start | bytes 2621440 | tf_op jit(solution)/shard_map/all_gather | solution.py:130
  64.7 167.0 %copy-start.14 = (f32[2048]{0:T(1024)S(1)}, f32[2048]{0:T(1024)}, u32[]{:S(2)}) copy-start(f32[2048]{0:T(1024)} %param.16) | copy-start | bytes 24580
  80.4 151.3 %copy-start.10 = (bf16[512,2048]{1,0:T(8,128)(2,1)S(1)}, bf16[512,2048]{1,0:T(8,128)(2,1)}, u32[]{:S(2)}) copy-start(bf16[512,2048]{1,0:T(8,128)(2,1)} %all-gather.10.cloned.1.call-done) | copy-start | bytes 6291460
  238.7 2.3 copy-start.3
  251.3 2.5 copy-start.2
  259.5 12.2 %collective-permute-start.5 = (bf16[128,512]{1,0:T(8,128)(2,1)}, bf16[128,512]{1,0:T(8,128)(2,1)}, u32[]{:S(2)}, u32[]{:S(2)}) collective-permute-start(bf16[128,512]{1,0:T(8,128)(2,1)} %slice_bitcast_fusion.2), channel_id=1, source_target_pairs={{0,4},{4,8},{8,12},{1,5},{5,9},{9,13},{2,6},{6,10},{10,14},{3,7},{... | collective-permute-start | bytes 393224 | tf_op jit(solution)/shard_map/ppermute | solution.py:20
  268.4 17.3 %collective-permute-start = (bf16[128,512]{1,0:T(8,128)(2,1)}, bf16[128,512]{1,0:T(8,128)(2,1)S(1)}, u32[]{:S(2)}, u32[]{:S(2)}) collective-permute-start(bf16[128,512]{1,0:T(8,128)(2,1)} %slice_bitcast_fusion.3), channel_id=1, source_target_pairs={{0,4},{4,8},{8,12},{1,5},{5,9},{9,13},{2,6},{6,10},{10,14},{3,7},{... | collective-permute-start | bytes 393224 | tf_op jit(solution)/shard_map/ppermute | solution.py:20
  279.5 6.2 %copy-start.11 = (bf16[512,512]{1,0:T(8,128)(2,1)S(1)}, bf16[512,512]{1,0:T(8,128)(2,1)}, u32[]{:S(2)}) copy-start(bf16[512,512]{1,0:T(8,128)(2,1)} %slice_bitcast_fusion.9) | copy-start | bytes 1572868
  281.5 0.8 copy-start.6
  283.0 9.7 %collective-permute-start.6 = (bf16[128,512]{1,0:T(8,128)(2,1)}, bf16[128,512]{1,0:T(8,128)(2,1)}, u32[]{:S(2)}, u32[]{:S(2)}) collective-permute-start(bf16[128,512]{1,0:T(8,128)(2,1)} %slice.178), channel_id=1, source_target_pairs={{0,4},{4,8},{8,12},{1,5},{5,9},{9,13},{2,6},{6,10},{10,14},{3,7},{... | collective-permute-start | bytes 393224 | tf_op jit(solution)/shard_map/ppermute | solution.py:20
  292.1 1.0 copy-start.7
  302.5 9.0 %collective-permute-start.7 = (bf16[128,512]{1,0:T(8,128)(2,1)S(1)}, bf16[128,512]{1,0:T(8,128)(2,1)S(1)}, u32[]{:S(2)}, u32[]{:S(2)}) collective-permute-start(bf16[128,512]{1,0:T(8,128)(2,1)S(1)} %slice.179), channel_id=1, source_target_pairs={{0,4},{4,8},{8,12},{1,5},{5,9},{9,13},{2,6},{6,10},{10,14},{3,7},{... | collective-permute-start | bytes 393224 | tf_op jit(solution)/shard_map/ppermute | solution.py:20
  307.8 3.9 %copy-start.4 = (bf16[512,512]{1,0:T(8,128)(2,1)}, bf16[512,512]{1,0:T(8,128)(2,1)S(1)}, u32[]{:S(2)}) copy-start(bf16[512,512]{1,0:T(8,128)(2,1)S(1)} %fusion.21) | copy-start | bytes 1572868
  307.9 3.9 %copy-start.9 = (bf16[4,128,256]{2,1,0:T(8,128)(2,1)S(1)}, bf16[4,128,256]{2,1,0:T(8,128)(2,1)}, u32[]{:S(2)}) copy-start(bf16[4,128,256]{2,1,0:T(8,128)(2,1)} %compare_convert_fusion) | copy-start | bytes 786436
  308.5 7.9 %collective-permute-start.1 = (bf16[128,512]{1,0:T(8,128)(2,1)}, bf16[128,512]{1,0:T(8,128)(2,1)S(1)}, u32[]{:S(2)}, u32[]{:S(2)}) collective-permute-start(bf16[128,512]{1,0:T(8,128)(2,1)} %slice.169), channel_id=1, source_target_pairs={{0,4},{4,8},{8,12},{1,5},{5,9},{9,13},{2,6},{6,10},{10,14},{3,7},{... | collective-permute-start | bytes 393224 | tf_op jit(solution)/shard_map/ppermute | solution.py:20
  313.8 2.6 copy-start.5
  316.1 12.0 %collective-permute-start.8 = (bf16[512,512]{1,0:T(8,128)(2,1)}, bf16[512,512]{1,0:T(8,128)(2,1)}, u32[]{:S(2)}, u32[]{:S(2)}) collective-permute-start(bf16[512,512]{1,0:T(8,128)(2,1)} %fusion.16), channel_id=1, source_target_pairs={{0,4},{4,0},{8,12},{12,8},{1,5},{5,1},{9,13},{13,9},{2,6},{6,2},{1... | collective-permute-start | bytes 1572872 | tf_op jit(solution)/shard_map/ppermute | solution.py:14
  316.5 1.0 copy-start.8
  328.1 23.1 %collective-permute-start.9 = (bf16[512,512]{1,0:T(8,128)(2,1)}, bf16[512,512]{1,0:T(8,128)(2,1)S(1)}, u32[]{:S(2)}, u32[]{:S(2)}) collective-permute-start(bf16[512,512]{1,0:T(8,128)(2,1)} %collective-permute-done.8), channel_id=1, source_target_pairs={{0,8},{8,0},{4,12},{12,4},{1,9},{9,1},{5,13},{13,5},{2,10},{10,2},... | collective-permute-start | bytes 1572872 | tf_op jit(solution)/shard_map/ppermute | solution.py:14
  329.5 10.4 %collective-permute-start.2 = (bf16[128,512]{1,0:T(8,128)(2,1)S(1)}, bf16[128,512]{1,0:T(8,128)(2,1)S(1)}, u32[]{:S(2)}, u32[]{:S(2)}) collective-permute-start(bf16[128,512]{1,0:T(8,128)(2,1)S(1)} %slice.170), channel_id=1, source_target_pairs={{0,4},{4,8},{8,12},{1,5},{5,9},{9,13},{2,6},{6,10},{10,14},{3,7},{... | collective-permute-start | bytes 393224 | tf_op jit(solution)/shard_map/ppermute | solution.py:20
  354.2 29.7 %copy-start.1 = (bf16[4,512]{1,0:T(4,128)(2,1)S(1)}, bf16[4,512]{1,0:T(4,128)(2,1)}, u32[]{:S(2)}) copy-start(bf16[4,512]{1,0:T(4,128)(2,1)} %param.15) | copy-start | bytes 12292
Sparse Core Ops, SparseCore 0:
  9.6 25.2 all-gather.5
  56.8 23.5 all-gather.9
  82.0 149.6 all-gather.7
  233.1 46.2 all-gather.13
  354.3 25.2 all-gather.11
where the time goes:
time: 392 us; the launch traced here: 390 us
  waiting for transfers between devices  248 us (63%)
  local copies, waits for them, and re-layouts  48.7 us (12%)
  matrix products  36.2 us (9%)
  starting transfers between devices  23.1 us (6%)
  other arithmetic  20.5 us (5%)
  between operations  13.7 us (3%)
    all_gather x1, waiting for transfers between devices, local(): piece = lax.all_gather(in_weight, 'ctx', axis=1, tiled=True)  149 us
    ppermute x4, waiting for transfers between devices, partner(): return lax.ppermute(block, axis, route)  51.2 us
    all_gather x1, waiting for transfers between devices, local(): whole_sum = lax.all_gather(mixed_sum, 'ch', axis=1, tiled=True)  25.4 us
    ppermute x6, starting transfers between devices, shifted(): return lax.ppermute(value, axis, pairs)  17.1 us
    all_gather x1, waiting for transfers between devices, local(): lax.all_gather(rev_input, 'ch', axis=1, tiled=True)  13.3 us
    dot_general x6, matrix products, blockwise_conv(): jnp.einsum('nhts,nshd->nthd', kernel, window, preferred_element_type=jnp....  13.2 us
    concatenate x12, local copies, waits for them, and re-layouts, blockwise_conv(): jnp.concatenate([extended[:rows].reshape(blocks, block, width), extended[...  9.97 us
    ppermute x6, waiting for transfers between devices, shifted(): return lax.ppermute(value, axis, pairs)  8.09 us
  transfers between devices with their start and end apart: 15, of which 8 were waited for; matrix products, arithmetic and copies ran while one was open for 24% of the time, Pallas kernels for 0%

commit v1 on v0

--- a/solution.py
+++ b/solution.py
@@ -1,7 +1,13 @@
+import functools
+
 import jax
 import jax.numpy as jnp
 from jax import lax
+from jax.experimental import pallas as pl
+from jax.experimental.pallas import tpu as pltpu
 from jax.sharding import PartitionSpec as P
+
+VMEM_LIMIT = 40 * 1024 * 1024
 
 
 def partner(block, axis, apart):
@@ -136,6 +142,408 @@
     return total.astype(jnp.bfloat16)
 
 
+def flip(block, axis, bit):
+    count = lax.axis_size(axis)
+    return lax.ppermute(block, axis, [(i, i ^ bit) for i in range(count)])
+
+
+def across(block, bit):
+    groups, count = lax.axis_size("grp"), lax.axis_size("ch")
+    pairs = [
+        (g * count + k, (g ^ 1) * count + (k ^ bit)) for g in range(groups) for k in range(count)
+    ]
+    return lax.ppermute(block, ("grp", "ch"), pairs)
+
+
+def params(*semantics):
+    return pltpu.CompilerParams(
+        dimension_semantics=semantics, vmem_limit_bytes=VMEM_LIMIT
+    )
+
+
+def norm_kernel(place, gain, *refs):
+    pieces, out = refs[:-1], refs[-1]
+    strands, groups, rows, model = out.shape
+    width = pieces[0].shape[-1]
+    parts = model // width
+    for s in range(strands):
+        for g in range(groups):
+            group = pieces[(s * groups + g) * parts : (s * groups + g + 1) * parts]
+            floats = [p[...].astype(jnp.float32) for p in group]
+            total = sum(jnp.sum(f * f, axis=-1, keepdims=True) for f in floats)
+            scale = lax.rsqrt(total / model + 1e-05)
+            for j, f in enumerate(floats):
+                at = pl.multiple_of((place[0] ^ j) * width, width)
+                lanes = pl.ds(at, width)
+                out[s, g, :, lanes] = (f * scale * gain[:, lanes]).astype(jnp.bfloat16)
+
+
+def norm_all(place, gain, pieces, rows, width, parts):
+    flat = [p for strand in pieces for group in strand for p in group]
+    strands, groups = len(pieces), len(pieces[0])
+    tile = 128
+    return pl.pallas_call(
+        norm_kernel,
+        grid_spec=pltpu.PrefetchScalarGridSpec(
+            num_scalar_prefetch=1,
+            grid=(rows // tile,),
+            in_specs=[pl.BlockSpec((1, width * parts), lambda i, p: (0, 0))]
+            + [pl.BlockSpec((tile, width), lambda i, p: (i, 0)) for _ in flat],
+            out_specs=pl.BlockSpec(
+                (strands, groups, tile, width * parts), lambda i, p: (0, 0, i, 0)
+            ),
+        ),
+        out_shape=jax.ShapeDtypeStruct((strands, groups, rows, width * parts), jnp.bfloat16),
+        compiler_params=params("arbitrary"),
+        cost_estimate=pl.CostEstimate(
+            flops=6 * strands * groups * rows * width * parts,
+            bytes_accessed=4 * strands * groups * rows * width * parts,
+            transcendentals=0,
+        ),
+        name="norm",
+    )(place, gain.reshape(1, -1), *flat)
+
+
+def project(normed, weight, b):
+    count, _, depth, _ = weight.shape
+    parts = [
+        jnp.dot(
+            normed[:, z * depth : (z + 1) * depth],
+            weight[z, b],
+            preferred_element_type=jnp.float32,
+        )
+        for z in range(count)
+    ]
+    return sum(parts[1:], parts[0])
+
+
+def keep_rims(value, s, g, rim_fwd, rim_rev):
+    rows, block = value.shape[0], rim_fwd.shape[1]
+
+    @pl.when(s == 0)
+    def _():
+        rim_fwd[g] = value[rows - block :]
+
+    @pl.when(s == 1)
+    def _():
+        rim_rev[g] = value[:block]
+
+
+def first_kernel(normed, weight, state, rim_fwd, rim_rev):
+    s, g = pl.program_id(0), pl.program_id(1)
+    value = project(normed[0, 0], weight, 0).astype(jnp.bfloat16)
+    state[0, 0] = value
+    keep_rims(value, s, g, rim_fwd, rim_rev)
+
+
+def first(normed, weight, block):
+    strands, groups, rows, model = normed.shape
+    count, few, depth, width = weight.shape
+    rim = jax.ShapeDtypeStruct((groups, block, width), jnp.bfloat16)
+    rim_spec = pl.BlockSpec((groups, block, width), lambda s, g: (0, 0, 0))
+    return pl.pallas_call(
+        first_kernel,
+        grid=(strands, groups),
+        in_specs=[
+            pl.BlockSpec((1, 1, rows, model), lambda s, g: (s, g, 0, 0)),
+            pl.BlockSpec((count, 1, depth, width), lambda s, g: (0, 0, 0, 0)),
+        ],
+        out_specs=[
+            pl.BlockSpec((1, 1, rows, width), lambda s, g: (s, g, 0, 0)),
+            rim_spec,
+            rim_spec,
+        ],
+        out_shape=[
+            jax.ShapeDtypeStruct((strands, groups, rows, width), jnp.bfloat16),
+            rim,
+            rim,
+        ],
+        compiler_params=params("arbitrary", "arbitrary"),
+        cost_estimate=pl.CostEstimate(
+            flops=2 * strands * groups * rows * model * width,
+            bytes_accessed=2 * strands * groups * rows * model + 2 * model * width,
+            transcendentals=0,
+        ),
+        name="first",
+    )(normed, weight)
+
+
+def gates_kernel(normed, weight, *outs):
+    for i, out in enumerate(outs):
+        out[0, 0] = project(normed[0, 0], weight, 1 + i)
+
+
+def gates(normed, weight):
+    strands, groups, rows, model = normed.shape
+    count, few, depth, width = weight.shape
+    tile = rows // 2
+    shape = jax.ShapeDtypeStruct((strands, groups, rows, width), jnp.float32)
+    return pl.pallas_call(
+        gates_kernel,
+        grid=(strands, groups, rows // tile),
+        in_specs=[
+            pl.BlockSpec((1, 1, tile, model), lambda s, g, i: (s, g, i, 0)),
+            pl.BlockSpec((count, few, depth, width), lambda s, g, i: (0, 0, 0, 0)),
+        ],
+        out_specs=[pl.BlockSpec((1, 1, tile, width), lambda s, g, i: (s, g, i, 0))] * (few - 1),
+        out_shape=[shape] * (few - 1),
+        compiler_params=params("arbitrary", "arbitrary", "arbitrary"),
+        cost_estimate=pl.CostEstimate(
+            flops=2 * (few - 1) * strands * groups * rows * model * width,
+            bytes_accessed=2 * strands * groups * rows * model + 2 * few * model * width,
+            transcendentals=0,
+        ),
+        name="gates",
+    )(normed, weight)
+
+
+def conv_kernel(last, state, rim_fwd, rim_rev, table, mask, *refs):
+    s, g = pl.program_id(0), pl.program_id(1)
+    extended = refs[-1]
+    rows, width = state.shape[2:]
+    block = rim_fwd.shape[1]
+    heads = table.shape[2]
+    head = width // heads
+
+    @pl.when(s == 0)
+    def _():
+        extended[:block] = rim_fwd[g]
+        extended[block:] = state[0, 0]
+
+    @pl.when(s == 1)
+    def _():
+        extended[:rows] = state[0, 0]
+        extended[rows:] = rim_rev[g]
+
+    for n in range(rows // block):
+        span = slice(n * block, (n + 1) * block)
+        for h in range(heads):
+            lanes = slice(h * head, (h + 1) * head)
+            kernel = table[0, 0, h] * mask[0, 0, n]
+            conv = jnp.dot(
+                kernel,
+                extended[n * block : (n + 2) * block, lanes],
+                preferred_element_type=jnp.float32,
+            )
+            if last:
+                refs[0][0, 0, span, lanes] = conv
+            else:
+                refs[1][0, 0, span, lanes] = (refs[0][0, 0, span, lanes] * conv).astype(
+                    jnp.bfloat16
+                )
+    if not last:
+        keep_rims(refs[1][0, 0], s, g, refs[2], refs[3])
+
+
+def conv_section(state, rims, tables, mask, section, gate=None):
+    strands, groups, rows, width = state.shape
+    heads, block = tables.shape[2:4]
+    rim = jax.ShapeDtypeStruct((groups, block, width), jnp.bfloat16)
+    rim_spec = pl.BlockSpec((groups, block, width), lambda s, g: (0, 0, 0))
+    row_spec = pl.BlockSpec((1, 1, rows, width), lambda s, g: (s, g, 0, 0))
+    last = gate is None
+    in_specs = [
+        row_spec,
+        rim_spec,
+        rim_spec,
+        pl.BlockSpec((1, 1, heads, block, 2 * block), lambda s, g: (section, s, 0, 0, 0)),
+        pl.BlockSpec(
+            (1, 1, rows // block, block, 2 * block), lambda s, g: (s, g, 0, 0, 0)
+        ),
+    ]
+    args = [state, rims[0], rims[1], tables, mask]
+    if last:
+        out_specs = [row_spec]
+        out_shape = [jax.ShapeDtypeStruct(state.shape, jnp.float32)]
+    else:
+        in_specs.append(row_spec)
+        args.append(gate)
+        out_specs = [row_spec, rim_spec, rim_spec]
+        out_shape = [jax.ShapeDtypeStruct(state.shape, jnp.bfloat16), rim, rim]
+    return pl.pallas_call(
+        functools.partial(conv_kernel, last),
+        grid=(strands, groups),
+        in_specs=in_specs,
+        out_specs=out_specs,
+        out_shape=out_shape,
+        scratch_shapes=[pltpu.VMEM((rows + block, width), jnp.bfloat16)],
+        compiler_params=params("arbitrary", "arbitrary"),
+        cost_estimate=pl.CostEstimate(
+            flops=4 * strands * groups * rows * block * width,
+            bytes_accessed=10 * strands * groups * rows * width,
+            transcendentals=0,
+        ),
+        name="conv",
+    )(*args)
+
+
+def mix_kernel(normed, weight, conv, out):
+    strands = normed.shape[0]
+    total = None
+    for s in range(strands):
+        gate = project(normed[s, 0], weight, 0)
+        state = (gate * conv[s, 0]).astype(jnp.bfloat16).astype(jnp.float32)
+        total = state if total is None else total + state
+    out[...] = total.astype(jnp.bfloat16)
+
+
+def mix(normed, weight, conv, group):
+    strands, groups, rows, model = normed.shape
+    count, _, depth, width = weight.shape
+    tile = rows // 2
+    return pl.pallas_call(
+        mix_kernel,
+        grid=(rows // tile,),
+        in_specs=[
+            pl.BlockSpec((strands, 1, tile, model), lambda i: (0, group, i, 0)),
+            pl.BlockSpec((count, 1, depth, width), lambda i: (0, 0, 0, 0)),
+            pl.BlockSpec((strands, 1, tile, width), lambda i: (0, group, i, 0)),
+        ],
+        out_specs=pl.BlockSpec((tile, width), lambda i: (i, 0)),
+        out_shape=jax.ShapeDtypeStruct((rows, width), jnp.bfloat16),
+        compiler_params=params("arbitrary"),
+        cost_estimate=pl.CostEstimate(
+            flops=2 * strands * rows * model * width,
+            bytes_accessed=2 * strands * rows * model + 2 * model * width,
+            transcendentals=0,
+        ),
+        name="mix",
+    )(normed, weight, conv)
+
+
+def out_kernel(place, near, far, *refs):
+    pieces, out = refs[:-1], refs[-1]
+    half = len(pieces) // 2
+    total = None
+    for weight, group in ((near, pieces[:half]), (far, pieces[half:])):
+        for j, piece in enumerate(group):
+            term = jnp.dot(piece[...], weight[place[0] ^ j], preferred_element_type=jnp.float32)
+            total = term if total is None else total + term
+    out[...] = total.astype(jnp.bfloat16)
+
+
+def project_out(place, near, far, pieces):
+    rows, width = pieces[0].shape
+    whole = pl.BlockSpec(near.shape, lambda i, p: (0, 0, 0))
+    tile = rows // 2
+    return pl.pallas_call(
+        out_kernel,
+        grid_spec=pltpu.PrefetchScalarGridSpec(
+            num_scalar_prefetch=1,
+            grid=(rows // tile,),
+            in_specs=[whole, whole]
+            + [pl.BlockSpec((tile, width), lambda i, p: (i, 0)) for _ in pieces],
+            out_specs=pl.BlockSpec((tile, near.shape[-1]), lambda i, p: (i, 0)),
+        ),
+        out_shape=jax.ShapeDtypeStruct((rows, near.shape[-1]), jnp.bfloat16),
+        compiler_params=params("arbitrary"),
+        cost_estimate=pl.CostEstimate(
+            flops=2 * rows * width * len(pieces) * near.shape[-1],
+            bytes_accessed=2 * near.size * 2 + 2 * rows * width * len(pieces),
+            transcendentals=0,
+        ),
+        name="out",
+    )(place, near, far, *pieces)
+
+
+def conv_tables(taps):
+    sections, heads, block = taps.shape
+    zero = jnp.zeros((sections, heads, block), taps.dtype)
+    one = jnp.zeros((sections, heads, 1), taps.dtype)
+    patterns = jnp.stack(
+        [
+            jnp.concatenate([one, taps[:, :, ::-1], zero], axis=-1),
+            jnp.concatenate([taps, zero, one], axis=-1),
+        ],
+        axis=1,
+    )
+    repeated = jnp.tile(patterns, (1, 1, 1, block))[..., : block * 2 * block]
+    return repeated.reshape(sections, 2, heads, block, 2 * block)
+
+
+def doc_masks(offsets, start, rows, block, seq_len):
+    positions = start - block + jnp.arange(rows + 2 * block, dtype=jnp.int32)
+    docs = jax.vmap(lambda o: doc_of(positions, o, seq_len))(offsets)
+    groups, blocks = offsets.shape[0], rows // block
+    tiles = docs.reshape(groups, blocks + 2, block)
+    target = tiles[:, 1:-1]
+    before = jnp.concatenate([tiles[:, :-2], target], axis=-1)
+    after = jnp.concatenate([target, tiles[:, 2:]], axis=-1)
+    window = jnp.stack([before, after])
+    return (target[None, :, :, :, None] == window[:, :, :, None, :]).astype(jnp.bfloat16)
+
+
+def paired(
+    fwd_hidden,
+    rev_hidden,
+    bases,
+    complement,
+    offsets,
+    base_embed,
+    norm_gain,
+    in_weight,
+    filters,
+    out_weight,
+):
+    rows, width = fwd_hidden.shape
+    groups, ctx_count, parts = (lax.axis_size(a) for a in ("grp", "ctx", "ch"))
+    mine, here, place = (lax.axis_index(a) for a in ("grp", "ctx", "ch"))
+    sections, heads, block = filters.shape
+    seq_len = rows * ctx_count
+    half = width // groups
+
+    columns = lax.dynamic_slice_in_dim(in_weight, mine * half, half, axis=2)
+    early = lax.all_gather(columns[:sections], "ctx", axis=0)
+    late = lax.all_gather(columns[sections:], "ctx", axis=0)
+    near = lax.all_gather(
+        lax.dynamic_slice_in_dim(out_weight, mine * half, half, axis=0), "ctx", axis=0
+    )
+    far = flip(near, "grp", 1)
+
+    letters = base_embed.shape[0]
+    alphabet = jnp.arange(letters, dtype=jnp.int32)
+    onehot = (bases[:, None] == alphabet[None, :]).astype(jnp.bfloat16)
+    swap_table = (complement[:, None] == alphabet[None, :]).astype(jnp.bfloat16)
+    swapped = jnp.dot(swap_table, base_embed, preferred_element_type=jnp.float32)
+    inputs = []
+    for hidden, table in ((fwd_hidden, base_embed), (rev_hidden, swapped.astype(jnp.bfloat16))):
+        embed = jnp.dot(onehot, table, preferred_element_type=jnp.float32)
+        inputs.append((hidden.astype(jnp.float32) + embed).astype(jnp.bfloat16))
+    other_x = [flip(v, "ch", 2) for v in inputs]
+    other_y = [flip(v, "grp", 1) for v in inputs]
+    other_xy = [flip(other_x[0], "grp", 1), flip(other_y[1], "ch", 2)]
+    pieces = []
+    for s in range(2):
+        own = [inputs[s], flip(inputs[s], "ch", 1), other_x[s], flip(other_x[s], "ch", 1)]
+        far_side = [other_y[s], flip(other_y[s], "ch", 1), other_xy[s], flip(other_xy[s], "ch", 1)]
+        pieces.append([own, far_side])
+    where = place.astype(jnp.int32).reshape(1)
+    normed = norm_all(where, norm_gain, pieces, rows, width, parts)
+
+    both_offsets = jnp.stack([offsets, flip(offsets, "grp", 1)])
+    mask = doc_masks(both_offsets, here * rows, rows, block, seq_len)
+    own_heads = heads // groups
+    taps = lax.dynamic_slice_in_dim(filters, mine * own_heads, own_heads, axis=1)
+    tables = conv_tables(taps.astype(jnp.bfloat16))
+
+    state, *rims = first(normed, early, block)
+    gate = gates(normed, early)
+    for section in range(sections):
+        rims = (shifted(rims[0], "ctx", 1), shifted(rims[1], "ctx", -1))
+        if section + 1 < sections:
+            state, *rims = conv_section(state, rims, tables, mask, section, gate[section])
+        else:
+            (conv,) = conv_section(state, rims, tables, mask, section)
+    mixed_far = mix(normed, late, conv, 1)
+    mixed_near = mix(normed, late, conv, 0)
+    from_y = flip(mixed_far, "grp", 1)
+    from_xy = across(mixed_far, 2)
+    from_x = flip(mixed_near, "ch", 2)
+    near_pieces = [mixed_near, flip(mixed_near, "ch", 1), from_x, flip(from_x, "ch", 1)]
+    far_pieces = [from_y, flip(from_y, "ch", 1), from_xy, flip(from_xy, "ch", 1)]
+    return project_out(where, near, far, near_pieces + far_pieces)
+
+
 def solution(mesh):
     in_specs = (
         P(("grp", "ctx"), "ch"),
@@ -150,4 +558,6 @@
         P("ctx", "ch"),
     )
     out_specs = P(("grp", "ctx"), "ch")
-    return jax.shard_map(local, mesh=mesh, in_specs=in_specs, out_specs=out_specs, check_vma=False)
+    sizes = [mesh.shape[a] for a in ("grp", "ctx", "ch")]
+    body = paired if sizes[0] == 2 and sizes[1] == sizes[2] == 4 else local
+    return jax.shard_map(body, mesh=mesh, in_specs=in_specs, out_specs=out_specs, check_vma=False)

time: 392 us -> 185 us (0.47)
  waiting for transfers between devices: 248 us -> 78.7 us
  matrix products: 36.2 us -> 1.86 us
  Pallas kernels: 0 us -> 30.8 us
  other arithmetic: 20.5 us -> 0.48 us
  local copies, waits for them, and re-layouts: 48.7 us -> 30.9 us
  starting transfers between devices: 23.1 us -> 27.7 us
    all_gather x5 -> x3, waiting for transfers between devices: 188 us -> 36.4 us  [the longest x1 36.3 us: paired(): early = lax.all_gather(columns[:sections], 'ctx', axis=0)]
    dot_general x11 -> x2, matrix products: 36.2 us -> 1.86 us  [paired(): embed = jnp.dot(onehot, table, preferred_element_type=jnp.float32)]
    pallas_call x0 -> x9, Pallas kernels: none -> 30.8 us  [the longest x1 8.78 us: gates(): pl.pallas_call(gates_kernel, grid=(strands, groups, rows // tile), in_spe...]
    ppermute x4 -> x23, waiting for transfers between devices: 51.2 us -> 27.4 us  [the longest x22 27.4 us: flip(): return lax.ppermute(block, axis, [(i, i ^ bit) for i in range(count)])]
    convert_element_type x9 -> x1, other arithmetic: 11.1 us -> 0.24 us  [doc_masks(): (target[None, :, :, :, None] == window[:, :, :, None, :]).astype(jnp.bflo...]
    ppermute x4 -> x23, starting transfers between devices: 5.87 us -> 16.3 us  [the longest x22 14.9 us: flip(): return lax.ppermute(block, axis, [(i, i ^ bit) for i in range(count)])]
    concatenate x14 -> x0, local copies, waits for them, and re-layouts: 10 us -> none  [the longest x12 9.97 us: blockwise_conv(): jnp.concatenate([extended[:rows].reshape(blocks, block, width), extended[...]
    unnamed x33 -> x38, local copies, waits for them, and re-layouts: 5.73 us -> 14.9 us
  transfers between devices with their start and end apart: 15 -> 32, of which waited for: 8 -> 17; matrix products, arithmetic and copies ran while one was open for 24% -> 9% of each run, Pallas kernels for 0% -> 15%
where the time goes in v1:
time: 185 us; the launch traced here: 184 us
  waiting for transfers between devices  78.7 us (43%)
  local copies, waits for them, and re-layouts  30.9 us (17%)
  Pallas kernels  30.8 us (17%)
  starting transfers between devices  27.7 us (15%)
  between operations  13.5 us (7%)
  matrix products  1.86 us (1%)
    all_gather x1, waiting for transfers between devices, paired(): early = lax.all_gather(columns[:sections], 'ctx', axis=0)  36.3 us
    ppermute x22, waiting for transfers between devices, flip(): return lax.ppermute(block, axis, [(i, i ^ bit) for i in range(count)])  27.4 us
    ppermute x6, waiting for transfers between devices, shifted(): return lax.ppermute(value, axis, pairs)  15 us
    ppermute x22, starting transfers between devices, flip(): return lax.ppermute(block, axis, [(i, i ^ bit) for i in range(count)])  14.9 us
    unnamed x38, local copies, waits for them, and re-layouts  14.9 us
    ppermute x6, starting transfers between devices, shifted(): return lax.ppermute(value, axis, pairs)  11.2 us
    pallas_call x1, Pallas kernels, gates(): pl.pallas_call(gates_kernel, grid=(strands, groups, rows // tile), in_spe...  8.78 us
    pallas_call x1, Pallas kernels, norm_all(): pl.pallas_call(norm_kernel, grid_spec=pltpu.PrefetchScalarGridSpec(num_sc...  7.96 us
  transfers between devices with their start and end apart: 32, of which 17 were waited for; matrix products, arithmetic and copies ran while one was open for 9% of the time, Pallas kernels for 15%

profile of v1, /device:TPU:0, one launch (start us, length us, event | category | flops | bytes accessed | tf_op | source)
XLA Modules:
  0.0 183.9 jit_solution(17562841751470006397)
XLA Ops:
  6.6 1.8 constant_dynamic-slice_fusion.2
  8.5 1.0 constant_dynamic-slice_fusion.1
  10.1 3.0 %collective-permute-start.11 = (bf16[512,512]{1,0:T(8,128)(2,1)S(1)}, bf16[512,512]{1,0:T(8,128)(2,1)}, u32[]{:S(2)}, u32[]{:S(2)}) collective-permute-start(bf16[512,512]{1,0:T(8,128)(2,1)S(1)} %fusion.1.refs_8_), channel_id=1, source_target_pairs={{0,16},{16,0},{1,17},{17,1},{2,18},{18,2},{3,19},{19,3},{4,20},{20... | collective-permute-start | bytes 1572872 | tf_op jit(solution)/shard_map/ppermute | solution.py:147
  13.1 1.5 collective-permute-start.9
  14.6 1.4 fusion.refs_0_
  16.7 1.9 %collective-permute-start.17 = (s32[16]{0:T(128)S(1)}, s32[16]{0:T(128)S(1)}, u32[]{:S(2)}, u32[]{:S(2)}) collective-permute-start(s32[16]{0:T(128)S(1)} %copy-done.18), channel_id=1, source_target_pairs={{0,16},{16,0},{1,17},{17,1},{2,18},{18,2},{3,19},{19,3},{4,20},{20... | collective-permute-start | bytes 200 | tf_op jit(solution)/shard_map/ppermute | solution.py:147
  20.3 1.2 tile.4
  21.5 4.7 %tile.10 = bf16[3,2,2,32896]{3,2,1,0:T(2,128)(2,1)} reshape(bf16[3,2,2,128,257]{4,3,2,1,0:T(8,128)(2,1)} %tile.4) | data formatting | bytes 1579008 | tf_op jit(solution)/shard_map/tile | solution.py:460
  26.2 2.6 %slice.24 = bf16[3,2,2,32768]{3,2,1,0:T(2,128)(2,1)} slice(bf16[3,2,2,32896]{3,2,1,0:T(2,128)(2,1)} %tile.10), slice={[0:3], [0:2], [0:2], [0:32768]} | slice | bytes 1572864 | tf_op jit(solution)/shard_map/slice | solution.py:460
  28.8 3.2 %reshape.33.table = bf16[3,2,2,128,256]{4,3,2,1,0:T(8,128)(2,1)} reshape(bf16[3,2,2,32768]{3,2,1,0:T(2,128)(2,1)} %slice.24) | data formatting | bytes 1572864 | tf_op jit(solution)/shard_map/reshape | solution.py:461
  32.0 4.4 %collective-permute-done.17 = s32[16]{0:T(128)S(1)} collective-permute-done((s32[16]{0:T(128)S(1)}, s32[16]{0:T(128)S(1)}, u32[]{:S(2)}, u32[]{:S(2)}) %collective-permute-start.17) | collective-permute-done | bytes 96 | tf_op jit(solution)/shard_map/ppermute | solution.py:147
  37.8 1.5 collective-permute-start.13
  41.0 10.2 %collective-permute-done.13.refs_14_ = bf16[512,512]{1,0:T(8,128)(2,1)} collective-permute-done((bf16[512,512]{1,0:T(8,128)(2,1)}, bf16[512,512]{1,0:T(8,128)(2,1)}, u32[]{:S(2)}, u32[]{:S(2)}) %collective-permute-start.13) | collective-permute-done | bytes 524320 | tf_op jit(solution)/shard_map/ppermute | solution.py:147
  51.2 2.8 %collective-permute-done.6.refs_6_ = bf16[512,512]{1,0:T(8,128)(2,1)} collective-permute-done((bf16[512,512]{1,0:T(8,128)(2,1)}, bf16[512,512]{1,0:T(8,128)(2,1)}, u32[]{:S(2)}, u32[]{:S(2)}) %collective-permute-start.6) | collective-permute-done | bytes 524320 | tf_op jit(solution)/shard_map/ppermute | solution.py:147
  54.8 1.3 collective-permute-done.14.refs_15_
  56.9 1.0 copy-done.9
  57.9 1.0 copy-done.11
  58.9 8.0 %norm.1.normed = bf16[2,2,512,2048]{3,2,1,0:T(8,128)(2,1)} custom-call(s32[1]{0:T(128)} %bitcast.place, f32[1,2048]{1,0:T(1,128)S(1)} %bitcast.25, bf16[512,512]{1,0:T(8,128)(2,1)S(1)} %copy-done.9, bf16[512,512]{1,0:T(8,128)(2,1)} %collective-permute-done.1.refs_1_, bf16[512,512]{1,0:T(8,128)(2,1)} %collective-permute-done.2.refs_2_, ...), custom_call_target="tpu_custom_call" | custom-call | flops 25165824 | bytes 16777216 | tf_op jit(solution)/shard_map/norm/pallas_call | solution.py:185
  66.9 1.0 collective-permute-start
  67.9 36.3 %all-gather.11.cloned.1.call-done = bf16[12,512,256]{2,1,0:T(8,128)(2,1)} async-done(((bf16[3,512,256]{2,1,0:T(8,128)(2,1)}), bf16[12,512,256]{2,1,0:T(8,128)(2,1)}) %all-gather.11.cloned.1.call-update) | async-done | bytes 3145744 | tf_op jit(solution)/shard_map/all_gather | solution.py:496
  104.2 3.4 %copy-done.1 = bf16[2,2,512,2048]{3,2,1,0:T(8,128)(2,1)S(1)} copy-done((bf16[2,2,512,2048]{3,2,1,0:T(8,128)(2,1)S(1)}, bf16[2,2,512,2048]{3,2,1,0:T(8,128)(2,1)}, u32[]{:S(2)}) %copy-start.1) | copy-done | bytes 8388632
  107.6 1.9 %copy-done.7 = bf16[12,512,256]{2,1,0:T(8,128)(2,1)S(1)} copy-done((bf16[12,512,256]{2,1,0:T(8,128)(2,1)S(1)}, bf16[12,512,256]{2,1,0:T(8,128)(2,1)}, u32[]{:S(2)}) %copy-start.7) | copy-done | bytes 3145752
  109.5 3.0 %first.1 = (bf16[2,2,512,256]{3,2,1,0:T(8,128)(2,1)S(1)}, bf16[2,128,256]{2,1,0:T(8,128)(2,1)S(1)}, bf16[2,128,256]{2,1,0:T(8,128)(2,1)S(1)}) custom-call(bf16[2,2,512,2048]{3,2,1,0:T(8,128)(2,1)S(1)} %copy-done.1, bf16[4,3,512,256]{3,2,1,0:T(8,128)(2,1)S(1)} %bitcast.21), custom_call_target="tpu_custom_call" | custom-call | flops 2147483648 | bytes 9437184 | tf_op jit(solution)/shard_map/first/pallas_call | solution.py:244
  112.5 1.3 collective-permute-start.15
  113.8 1.4 collective-permute-start.16
  115.2 8.8 %gates.1 = (f32[2,2,512,256]{3,2,1,0:T(8,128)S(1)}, f32[2,2,512,256]{3,2,1,0:T(8,128)S(1)}) custom-call(bf16[2,2,512,2048]{3,2,1,0:T(8,128)(2,1)} %norm.1.normed, bf16[4,3,512,256]{3,2,1,0:T(8,128)(2,1)S(1)} %bitcast.22), custom_call_target="tpu_custom_call" | custom-call | flops 4294967296 | bytes 11534336 | tf_op jit(solution)/shard_map/gates/pallas_call | solution.py:281
  124.0 4.0 %collective-permute-done.16.rim_rev = bf16[2,128,256]{2,1,0:T(8,128)(2,1)S(1)} collective-permute-done((bf16[2,128,256]{2,1,0:T(8,128)(2,1)S(1)}, bf16[2,128,256]{2,1,0:T(8,128)(2,1)S(1)}, u32[]{:S(2)}, u32[]{:S(2)}) %collective-permute-start.16) | collective-permute-done | bytes 131104 | tf_op jit(solution)/shard_map/ppermute | solution.py:26
  128.0 1.4 conv.3
  129.5 3.8 %collective-permute-start.18 = (bf16[2,128,256]{2,1,0:T(8,128)(2,1)S(1)}, bf16[2,128,256]{2,1,0:T(8,128)(2,1)S(1)}, u32[]{:S(2)}, u32[]{:S(2)}) collective-permute-start(bf16[2,128,256]{2,1,0:T(8,128)(2,1)S(1)} %get-tuple-element.21), channel_id=1, source_target_pairs={{0,4},{4,8},{8,12},{1,5},{5,9},{9,13},{2,6},{6,10},{10,14},{3,7},{... | collective-permute-start | bytes 393224 | tf_op jit(solution)/shard_map/ppermute | solution.py:26
  133.2 1.3 collective-permute-start.19
  134.5 1.2 collective-permute-done.18.rim_fwd
  135.7 4.4 %collective-permute-done.19.rim_rev = bf16[2,128,256]{2,1,0:T(8,128)(2,1)S(1)} collective-permute-done((bf16[2,128,256]{2,1,0:T(8,128)(2,1)S(1)}, bf16[2,128,256]{2,1,0:T(8,128)(2,1)S(1)}, u32[]{:S(2)}, u32[]{:S(2)}) %collective-permute-start.19) | collective-permute-done | bytes 131104 | tf_op jit(solution)/shard_map/ppermute | solution.py:26
  140.1 1.4 conv.4
  141.5 1.9 %collective-permute-start.20 = (bf16[2,128,256]{2,1,0:T(8,128)(2,1)S(1)}, bf16[2,128,256]{2,1,0:T(8,128)(2,1)S(1)}, u32[]{:S(2)}, u32[]{:S(2)}) collective-permute-start(bf16[2,128,256]{2,1,0:T(8,128)(2,1)S(1)} %get-tuple-element.25), channel_id=1, source_target_pairs={{0,4},{4,8},{8,12},{1,5},{5,9},{9,13},{2,6},{6,10},{10,14},{3,7},{... | collective-permute-start | bytes 393224 | tf_op jit(solution)/shard_map/ppermute | solution.py:26
  143.4 1.5 collective-permute-start.21
  144.9 1.0 collective-permute-done.20.rim_fwd
  145.9 4.4 %collective-permute-done.21.rim_rev = bf16[2,128,256]{2,1,0:T(8,128)(2,1)S(1)} collective-permute-done((bf16[2,128,256]{2,1,0:T(8,128)(2,1)S(1)}, bf16[2,128,256]{2,1,0:T(8,128)(2,1)S(1)}, u32[]{:S(2)}, u32[]{:S(2)}) %collective-permute-start.21) | collective-permute-done | bytes 131104 | tf_op jit(solution)/shard_map/ppermute | solution.py:26
  150.3 1.3 conv.5
  151.6 1.3 copy-done.3
  152.9 3.4 %copy-done.2 = bf16[2,2,512,2048]{3,2,1,0:T(8,128)(2,1)S(1)} copy-done((bf16[2,2,512,2048]{3,2,1,0:T(8,128)(2,1)S(1)}, bf16[2,2,512,2048]{3,2,1,0:T(8,128)(2,1)}, u32[]{:S(2)}) %copy-start.2) | copy-done | bytes 8388632
  156.3 1.6 copy-done.4
  157.9 1.2 copy-done.6
  159.1 1.8 mix.3
  161.0 1.4 collective-permute-start.25
  162.4 1.4 collective-permute-start.27
  163.8 1.8 mix.2.refs_0_
  166.4 4.8 %collective-permute-done.25.refs_4_ = bf16[512,256]{1,0:T(8,128)(2,1)S(1)} collective-permute-done((bf16[512,256]{1,0:T(8,128)(2,1)S(1)}, bf16[512,256]{1,0:T(8,128)(2,1)S(1)}, u32[]{:S(2)}, u32[]{:S(2)}) %collective-permute-start.25) | collective-permute-done | bytes 262176 | tf_op jit(solution)/shard_map/ppermute | solution.py:147
  174.0 3.4 %out.1 = bf16[512,512]{1,0:T(8,128)(2,1)} custom-call(s32[1]{0:T(128)} %bitcast.place, bf16[4,256,512]{2,1,0:T(8,128)(2,1)S(1)} %bitcast.24, bf16[4,256,512]{2,1,0:T(8,128)(2,1)} %collective-permute-done.far, bf16[512,256]{1,0:T(8,128)(2,1)S(1)} %mix.2.refs_0_, bf16[512,256]{1,0:T(8,128)(2,1)S(1)} %collective-permute-done.22.refs_1_, ...), custom_call_target="tpu_custom_call" | custom-call | flops 1073741824 | bytes 4194304 | tf_op jit(solution)/shard_map/out/pallas_call | solution.py:429
  (93 shorter events, 11.2 us)
Async XLA Ops:
  6.5 2.0 %copy-start = (bf16[4,512,512]{2,1,0:T(8,128)(2,1)S(1)}, bf16[4,512,512]{2,1,0:T(8,128)(2,1)}, u32[]{:S(2)}) copy-start(bf16[4,512,512]{2,1,0:T(8,128)(2,1)} %param.17) | copy-start | bytes 6291460
  6.5 3.0 %copy-start.14 = (bf16[512,512]{1,0:T(8,128)(2,1)S(1)}, bf16[512,512]{1,0:T(8,128)(2,1)}, u32[]{:S(2)}) copy-start(bf16[512,512]{1,0:T(8,128)(2,1)} %param.11) | copy-start | bytes 1572868
  6.5 3.0 %copy-start.16 = (s32[512]{0:T(512)S(1)}, s32[512]{0:T(512)}, u32[]{:S(2)}) copy-start(s32[512]{0:T(512)} %param.12) | copy-start | bytes 6148
  6.5 3.0 %copy-start.17 = (s32[4]{0:T(128)S(1)}, s32[4]{0:T(128)}, u32[]{:S(2)}) copy-start(s32[4]{0:T(128)} %param.13) | copy-start | bytes 52
  6.5 3.0 %copy-start.15 = (bf16[4,512]{1,0:T(4,128)(2,1)S(1)}, bf16[4,512]{1,0:T(4,128)(2,1)}, u32[]{:S(2)}) copy-start(bf16[4,512]{1,0:T(4,128)(2,1)} %param.15) | copy-start | bytes 12292
  6.5 60.4 %all-gather.7.cloned.1.call-start = ((), (), s32[]{:S(2)}) async-start(), calls=%async_computation | async-start | bytes 1310720 | tf_op jit(solution)/shard_map/all_gather | solution.py:498
  8.4 8.3 %copy-start.18 = (s32[16]{0:T(128)S(1)}, s32[16]{0:T(128)}, u32[]{:S(2)}) copy-start(s32[16]{0:T(128)} %param.14) | copy-start | bytes 196
  8.4 95.8 %all-gather.11.cloned.1.call-start = ((), (), s32[]{:S(2)}) async-start(), calls=%async_computation.2 | async-start | bytes 3932160 | tf_op jit(solution)/shard_map/all_gather | solution.py:496
  9.5 143.4 %all-gather.9.cloned.1.call-start = ((), (), s32[]{:S(2)}) async-start(), calls=%async_computation.1 | async-start | bytes 1310720 | tf_op jit(solution)/shard_map/all_gather | solution.py:497
  10.1 26.3 %copy-start.10 = (bf16[512,512]{1,0:T(8,128)(2,1)}, bf16[512,512]{1,0:T(8,128)(2,1)S(1)}, u32[]{:S(2)}) copy-start(bf16[512,512]{1,0:T(8,128)(2,1)S(1)} %fusion.1.refs_8_) | copy-start | bytes 1572868
  10.1 26.3 %collective-permute-start.11 = (bf16[512,512]{1,0:T(8,128)(2,1)S(1)}, bf16[512,512]{1,0:T(8,128)(2,1)}, u32[]{:S(2)}, u32[]{:S(2)}) collective-permute-start(bf16[512,512]{1,0:T(8,128)(2,1)S(1)} %fusion.1.refs_8_), channel_id=1, source_target_pairs={{0,16},{16,0},{1,17},{17,1},{2,18},{18,2},{3,19},{19,3},{4,20},{20... | collective-permute-start | bytes 1572872 | tf_op jit(solution)/shard_map/ppermute | solution.py:147
  13.1 26.2 %collective-permute-start.9 = (bf16[512,512]{1,0:T(8,128)(2,1)S(1)}, bf16[512,512]{1,0:T(8,128)(2,1)}, u32[]{:S(2)}, u32[]{:S(2)}) collective-permute-start(bf16[512,512]{1,0:T(8,128)(2,1)S(1)} %fusion.1.refs_8_), channel_id=1, source_target_pairs={{0,2},{1,3},{2,0},{3,1},{4,6},{5,7},{6,4},{7,5},{8,10},{9,11},{10,... | collective-permute-start | bytes 1572872 | tf_op jit(solution)/shard_map/ppermute | solution.py:147
  16.0 20.4 %copy-start.8 = (bf16[512,512]{1,0:T(8,128)(2,1)}, bf16[512,512]{1,0:T(8,128)(2,1)S(1)}, u32[]{:S(2)}) copy-start(bf16[512,512]{1,0:T(8,128)(2,1)S(1)} %fusion.refs_0_) | copy-start | bytes 1572868
  16.0 21.8 %collective-permute-start.2 = (bf16[512,512]{1,0:T(8,128)(2,1)S(1)}, bf16[512,512]{1,0:T(8,128)(2,1)}, u32[]{:S(2)}, u32[]{:S(2)}) collective-permute-start(bf16[512,512]{1,0:T(8,128)(2,1)S(1)} %fusion.refs_0_), channel_id=1, source_target_pairs={{0,2},{1,3},{2,0},{3,1},{4,6},{5,7},{6,4},{7,5},{8,10},{9,11},{10,... | collective-permute-start | bytes 1572872 | tf_op jit(solution)/shard_map/ppermute | solution.py:147
  16.6 22.7 %collective-permute-start.4 = (bf16[512,512]{1,0:T(8,128)(2,1)S(1)}, bf16[512,512]{1,0:T(8,128)(2,1)}, u32[]{:S(2)}, u32[]{:S(2)}) collective-permute-start(bf16[512,512]{1,0:T(8,128)(2,1)S(1)} %fusion.refs_0_), channel_id=1, source_target_pairs={{0,16},{16,0},{1,17},{17,1},{2,18},{18,2},{3,19},{19,3},{4,20},{20... | collective-permute-start | bytes 1572872 | tf_op jit(solution)/shard_map/ppermute | solution.py:147
  16.7 19.7 %collective-permute-start.17 = (s32[16]{0:T(128)S(1)}, s32[16]{0:T(128)S(1)}, u32[]{:S(2)}, u32[]{:S(2)}) collective-permute-start(s32[16]{0:T(128)S(1)} %copy-done.18), channel_id=1, source_target_pairs={{0,16},{16,0},{1,17},{17,1},{2,18},{18,2},{3,19},{19,3},{4,20},{20... | collective-permute-start | bytes 200 | tf_op jit(solution)/shard_map/ppermute | solution.py:147
  26.2 30.7 %copy-start.13 = (f32[2048]{0:T(1024)S(1)}, f32[2048]{0:T(1024)}, u32[]{:S(2)}) copy-start(f32[2048]{0:T(1024)} %param.16) | copy-start | bytes 24580
  36.4 4.1 %collective-permute-start.1 = (bf16[512,512]{1,0:T(8,128)(2,1)S(1)}, bf16[512,512]{1,0:T(8,128)(2,1)}, u32[]{:S(2)}, u32[]{:S(2)}) collective-permute-start(bf16[512,512]{1,0:T(8,128)(2,1)S(1)} %fusion.refs_0_), channel_id=1, source_target_pairs={{0,1},{1,0},{2,3},{3,2},{4,5},{5,4},{6,7},{7,6},{8,9},{9,8},{10,11... | collective-permute-start | bytes 1572872 | tf_op jit(solution)/shard_map/ppermute | solution.py:147
  36.4 4.3 %collective-permute-start.8 = (bf16[512,512]{1,0:T(8,128)(2,1)S(1)}, bf16[512,512]{1,0:T(8,128)(2,1)}, u32[]{:S(2)}, u32[]{:S(2)}) collective-permute-start(bf16[512,512]{1,0:T(8,128)(2,1)S(1)} %fusion.1.refs_8_), channel_id=1, source_target_pairs={{0,1},{1,0},{2,3},{3,2},{4,5},{5,4},{6,7},{7,6},{8,9},{9,8},{10,11... | collective-permute-start | bytes 1572872 | tf_op jit(solution)/shard_map/ppermute | solution.py:147
  37.8 13.4 %collective-permute-start.13 = (bf16[512,512]{1,0:T(8,128)(2,1)}, bf16[512,512]{1,0:T(8,128)(2,1)}, u32[]{:S(2)}, u32[]{:S(2)}) collective-permute-start(bf16[512,512]{1,0:T(8,128)(2,1)} %collective-permute-done.11.refs_12_), channel_id=1, source_target_pairs={{0,2},{1,3},{2,0},{3,1},{4,6},{5,7},{6,4},{7,5},{8,10},{9,11},{10,... | collective-permute-start | bytes 1572872 | tf_op jit(solution)/shard_map/ppermute | solution.py:147
  39.3 14.7 %collective-permute-start.12 = (bf16[512,512]{1,0:T(8,128)(2,1)}, bf16[512,512]{1,0:T(8,128)(2,1)}, u32[]{:S(2)}, u32[]{:S(2)}) collective-permute-start(bf16[512,512]{1,0:T(8,128)(2,1)} %collective-permute-done.11.refs_12_), channel_id=1, source_target_pairs={{0,1},{1,0},{2,3},{3,2},{4,5},{5,4},{6,7},{7,6},{8,9},{9,8},{10,11... | collective-permute-start | bytes 1572872 | tf_op jit(solution)/shard_map/ppermute | solution.py:147
  39.3 14.7 %collective-permute-start.6 = (bf16[512,512]{1,0:T(8,128)(2,1)}, bf16[512,512]{1,0:T(8,128)(2,1)}, u32[]{:S(2)}, u32[]{:S(2)}) collective-permute-start(bf16[512,512]{1,0:T(8,128)(2,1)} %collective-permute-done.2.refs_2_), channel_id=1, source_target_pairs={{0,16},{16,0},{1,17},{17,1},{2,18},{18,2},{3,19},{19,3},{4,20},{20... | collective-permute-start | bytes 1572872 | tf_op jit(solution)/shard_map/ppermute | solution.py:147
  40.4 14.3 %collective-permute-start.3 = (bf16[512,512]{1,0:T(8,128)(2,1)}, bf16[512,512]{1,0:T(8,128)(2,1)S(1)}, u32[]{:S(2)}, u32[]{:S(2)}) collective-permute-start(bf16[512,512]{1,0:T(8,128)(2,1)} %collective-permute-done.2.refs_2_), channel_id=1, source_target_pairs={{0,1},{1,0},{2,3},{3,2},{4,5},{5,4},{6,7},{7,6},{8,9},{9,8},{10,11... | collective-permute-start | bytes 1572872 | tf_op jit(solution)/shard_map/ppermute | solution.py:147
  40.7 14.1 %collective-permute-start.10 = (bf16[512,512]{1,0:T(8,128)(2,1)}, bf16[512,512]{1,0:T(8,128)(2,1)S(1)}, u32[]{:S(2)}, u32[]{:S(2)}) collective-permute-start(bf16[512,512]{1,0:T(8,128)(2,1)} %collective-permute-done.9.refs_10_), channel_id=1, source_target_pairs={{0,1},{1,0},{2,3},{3,2},{4,5},{5,4},{6,7},{7,6},{8,9},{9,8},{10,11... | collective-permute-start | bytes 1572872 | tf_op jit(solution)/shard_map/ppermute | solution.py:147
  51.2 3.6 %collective-permute-start.5 = (bf16[512,512]{1,0:T(8,128)(2,1)}, bf16[512,512]{1,0:T(8,128)(2,1)S(1)}, u32[]{:S(2)}, u32[]{:S(2)}) collective-permute-start(bf16[512,512]{1,0:T(8,128)(2,1)} %collective-permute-done.4.refs_4_), channel_id=1, source_target_pairs={{0,1},{1,0},{2,3},{3,2},{4,5},{5,4},{6,7},{7,6},{8,9},{9,8},{10,11... | collective-permute-start | bytes 1572872 | tf_op jit(solution)/shard_map/ppermute | solution.py:147
  54.0 2.1 %collective-permute-start.14 = (bf16[512,512]{1,0:T(8,128)(2,1)}, bf16[512,512]{1,0:T(8,128)(2,1)S(1)}, u32[]{:S(2)}, u32[]{:S(2)}) collective-permute-start(bf16[512,512]{1,0:T(8,128)(2,1)} %collective-permute-done.13.refs_14_), channel_id=1, source_target_pairs={{0,1},{1,0},{2,3},{3,2},{4,5},{5,4},{6,7},{7,6},{8,9},{9,8},{10,11... | collective-permute-start | bytes 1572872 | tf_op jit(solution)/shard_map/ppermute | solution.py:147
  54.0 2.9 %collective-permute-start.7 = (bf16[512,512]{1,0:T(8,128)(2,1)}, bf16[512,512]{1,0:T(8,128)(2,1)S(1)}, u32[]{:S(2)}, u32[]{:S(2)}) collective-permute-start(bf16[512,512]{1,0:T(8,128)(2,1)} %collective-permute-done.6.refs_6_), channel_id=1, source_target_pairs={{0,1},{1,0},{2,3},{3,2},{4,5},{5,4},{6,7},{7,6},{8,9},{9,8},{10,11... | collective-permute-start | bytes 1572872 | tf_op jit(solution)/shard_map/ppermute | solution.py:147
  66.9 105.6 %collective-permute-start = (bf16[4,256,512]{2,1,0:T(8,128)(2,1)}, bf16[4,256,512]{2,1,0:T(8,128)(2,1)}, u32[]{:S(2)}, u32[]{:S(2)}) collective-permute-start(bf16[4,256,512]{2,1,0:T(8,128)(2,1)} %bitcast.23), channel_id=1, source_target_pairs={{0,16},{16,0},{1,17},{17,1},{2,18},{18,2},{3,19},{19,3},{4,20},{20... | collective-permute-start | bytes 3145736 | tf_op jit(solution)/shard_map/ppermute | solution.py:147
  104.2 3.4 %copy-start.1 = (bf16[2,2,512,2048]{3,2,1,0:T(8,128)(2,1)S(1)}, bf16[2,2,512,2048]{3,2,1,0:T(8,128)(2,1)}, u32[]{:S(2)}) copy-start(bf16[2,2,512,2048]{3,2,1,0:T(8,128)(2,1)} %norm.1.normed) | copy-start | bytes 25165828
  107.6 1.9 %copy-start.7 = (bf16[12,512,256]{2,1,0:T(8,128)(2,1)S(1)}, bf16[12,512,256]{2,1,0:T(8,128)(2,1)}, u32[]{:S(2)}) copy-start(bf16[12,512,256]{2,1,0:T(8,128)(2,1)} %all-gather.11.cloned.1.call-done) | copy-start | bytes 9437188
  112.5 11.5 %collective-permute-start.15 = (bf16[2,128,256]{2,1,0:T(8,128)(2,1)S(1)}, bf16[2,128,256]{2,1,0:T(8,128)(2,1)S(1)}, u32[]{:S(2)}, u32[]{:S(2)}) collective-permute-start(bf16[2,128,256]{2,1,0:T(8,128)(2,1)S(1)} %get-tuple-element.17), channel_id=1, source_target_pairs={{0,4},{4,8},{8,12},{1,5},{5,9},{9,13},{2,6},{6,10},{10,14},{3,7},{... | collective-permute-start | bytes 393224 | tf_op jit(solution)/shard_map/ppermute | solution.py:26
  113.8 14.3 %copy-start.5 = (bf16[3,2,2,128,256]{4,3,2,1,0:T(8,128)(2,1)S(1)}, bf16[3,2,2,128,256]{4,3,2,1,0:T(8,128)(2,1)}, u32[]{:S(2)}) copy-start(bf16[3,2,2,128,256]{4,3,2,1,0:T(8,128)(2,1)} %reshape.33.table) | copy-start | bytes 2359300
  113.8 14.2 %collective-permute-start.16 = (bf16[2,128,256]{2,1,0:T(8,128)(2,1)S(1)}, bf16[2,128,256]{2,1,0:T(8,128)(2,1)S(1)}, u32[]{:S(2)}, u32[]{:S(2)}) collective-permute-start(bf16[2,128,256]{2,1,0:T(8,128)(2,1)S(1)} %get-tuple-element.18), channel_id=1, source_target_pairs={{4,0},{8,4},{12,8},{5,1},{9,5},{13,9},{6,2},{10,6},{14,10},{7,3},{... | collective-permute-start | bytes 393224 | tf_op jit(solution)/shard_map/ppermute | solution.py:26
  129.5 6.3 %collective-permute-start.18 = (bf16[2,128,256]{2,1,0:T(8,128)(2,1)S(1)}, bf16[2,128,256]{2,1,0:T(8,128)(2,1)S(1)}, u32[]{:S(2)}, u32[]{:S(2)}) collective-permute-start(bf16[2,128,256]{2,1,0:T(8,128)(2,1)S(1)} %get-tuple-element.21), channel_id=1, source_target_pairs={{0,4},{4,8},{8,12},{1,5},{5,9},{9,13},{2,6},{6,10},{10,14},{3,7},{... | collective-permute-start | bytes 393224 | tf_op jit(solution)/shard_map/ppermute | solution.py:26
  133.2 6.9 %collective-permute-start.19 = (bf16[2,128,256]{2,1,0:T(8,128)(2,1)S(1)}, bf16[2,128,256]{2,1,0:T(8,128)(2,1)S(1)}, u32[]{:S(2)}, u32[]{:S(2)}) collective-permute-start(bf16[2,128,256]{2,1,0:T(8,128)(2,1)S(1)} %get-tuple-element.22), channel_id=1, source_target_pairs={{4,0},{8,4},{12,8},{5,1},{9,5},{13,9},{6,2},{10,6},{14,10},{7,3},{... | collective-permute-start | bytes 393224 | tf_op jit(solution)/shard_map/ppermute | solution.py:26
  141.5 4.4 %collective-permute-start.20 = (bf16[2,128,256]{2,1,0:T(8,128)(2,1)S(1)}, bf16[2,128,256]{2,1,0:T(8,128)(2,1)S(1)}, u32[]{:S(2)}, u32[]{:S(2)}) collective-permute-start(bf16[2,128,256]{2,1,0:T(8,128)(2,1)S(1)} %get-tuple-element.25), channel_id=1, source_target_pairs={{0,4},{4,8},{8,12},{1,5},{5,9},{9,13},{2,6},{6,10},{10,14},{3,7},{... | collective-permute-start | bytes 393224 | tf_op jit(solution)/shard_map/ppermute | solution.py:26
  143.4 6.9 %collective-permute-start.21 = (bf16[2,128,256]{2,1,0:T(8,128)(2,1)S(1)}, bf16[2,128,256]{2,1,0:T(8,128)(2,1)S(1)}, u32[]{:S(2)}, u32[]{:S(2)}) collective-permute-start(bf16[2,128,256]{2,1,0:T(8,128)(2,1)S(1)} %get-tuple-element.26), channel_id=1, source_target_pairs={{4,0},{8,4},{12,8},{5,1},{9,5},{13,9},{6,2},{10,6},{14,10},{7,3},{... | collective-permute-start | bytes 393224 | tf_op jit(solution)/shard_map/ppermute | solution.py:26
  151.6 1.3 copy-start.3
  152.9 3.4 %copy-start.2 = (bf16[2,2,512,2048]{3,2,1,0:T(8,128)(2,1)S(1)}, bf16[2,2,512,2048]{3,2,1,0:T(8,128)(2,1)}, u32[]{:S(2)}) copy-start(bf16[2,2,512,2048]{3,2,1,0:T(8,128)(2,1)} %norm.1.normed) | copy-start | bytes 25165828
  156.3 1.6 copy-start.4
  160.9 13.0 %copy-start.12 = (bf16[1024,512]{1,0:T(8,128)(2,1)S(1)}, bf16[1024,512]{1,0:T(8,128)(2,1)}, u32[]{:S(2)}) copy-start(bf16[1024,512]{1,0:T(8,128)(2,1)} %all-gather.7.cloned.1.call-done) | copy-start | bytes 3145732
  161.0 10.2 %collective-permute-start.25 = (bf16[512,256]{1,0:T(8,128)(2,1)S(1)}, bf16[512,256]{1,0:T(8,128)(2,1)S(1)}, u32[]{:S(2)}, u32[]{:S(2)}) collective-permute-start(bf16[512,256]{1,0:T(8,128)(2,1)S(1)} %mix.3), channel_id=1, source_target_pairs={{0,16},{16,0},{1,17},{17,1},{2,18},{18,2},{3,19},{19,3},{4,20},{20... | collective-permute-start | bytes 786440 | tf_op jit(solution)/shard_map/ppermute | solution.py:147
  162.4 8.8 %collective-permute-start.27 = (bf16[512,256]{1,0:T(8,128)(2,1)S(1)}, bf16[512,256]{1,0:T(8,128)(2,1)S(1)}, u32[]{:S(2)}, u32[]{:S(2)}) collective-permute-start(bf16[512,256]{1,0:T(8,128)(2,1)S(1)} %mix.3), channel_id=1, source_target_pairs={{0,18},{1,19},{2,16},{3,17},{16,2},{17,3},{18,0},{19,1},{4,22},{5,... | collective-permute-start | bytes 786440 | tf_op jit(solution)/shard_map/ppermute | solution.py:155
  165.6 6.8 %collective-permute-start.23 = (bf16[512,256]{1,0:T(8,128)(2,1)S(1)}, bf16[512,256]{1,0:T(8,128)(2,1)S(1)}, u32[]{:S(2)}, u32[]{:S(2)}) collective-permute-start(bf16[512,256]{1,0:T(8,128)(2,1)S(1)} %mix.2.refs_0_), channel_id=1, source_target_pairs={{0,2},{1,3},{2,0},{3,1},{4,6},{5,7},{6,4},{7,5},{8,10},{9,11},{10,... | collective-permute-start | bytes 786440 | tf_op jit(solution)/shard_map/ppermute | solution.py:147
  166.4 6.1 %collective-permute-start.22 = (bf16[512,256]{1,0:T(8,128)(2,1)S(1)}, bf16[512,256]{1,0:T(8,128)(2,1)S(1)}, u32[]{:S(2)}, u32[]{:S(2)}) collective-permute-start(bf16[512,256]{1,0:T(8,128)(2,1)S(1)} %mix.2.refs_0_), channel_id=1, source_target_pairs={{0,1},{1,0},{2,3},{3,2},{4,5},{5,4},{6,7},{7,6},{8,9},{9,8},{10,11... | collective-permute-start | bytes 786440 | tf_op jit(solution)/shard_map/ppermute | solution.py:147
  171.2 1.5 collective-permute-start.26
  171.2 1.9 %collective-permute-start.28 = (bf16[512,256]{1,0:T(8,128)(2,1)S(1)}, bf16[512,256]{1,0:T(8,128)(2,1)S(1)}, u32[]{:S(2)}, u32[]{:S(2)}) collective-permute-start(bf16[512,256]{1,0:T(8,128)(2,1)S(1)} %collective-permute-done.27.refs_6_), channel_id=1, source_target_pairs={{0,1},{1,0},{2,3},{3,2},{4,5},{5,4},{6,7},{7,6},{8,9},{9,8},{10,11... | collective-permute-start | bytes 786440 | tf_op jit(solution)/shard_map/ppermute | solution.py:147
  172.5 1.5 collective-permute-start.24
  (3 other events, 3.3 us)
Sparse Core Ops, SparseCore 0:
  9.0 30.6 all-gather.6
  41.2 62.9 all-gather.10
  105.8 29.3 all-gather.8

commit v2 on v1

--- a/solution.py
+++ b/solution.py
@@ -8,6 +8,8 @@
 from jax.sharding import PartitionSpec as P
 
 VMEM_LIMIT = 40 * 1024 * 1024
+WIDE = 56 * 1024 * 1024
+SMALL = pl.CostEstimate(flops=1, bytes_accessed=1, transcendentals=0)
 
 
 def partner(block, axis, apart):
@@ -155,53 +157,63 @@
     return lax.ppermute(block, ("grp", "ch"), pairs)
 
 
-def params(*semantics):
+def params(*semantics, limit=None):
     return pltpu.CompilerParams(
-        dimension_semantics=semantics, vmem_limit_bytes=VMEM_LIMIT
-    )
-
-
-def norm_kernel(place, gain, *refs):
-    pieces, out = refs[:-1], refs[-1]
-    strands, groups, rows, model = out.shape
-    width = pieces[0].shape[-1]
-    parts = model // width
-    for s in range(strands):
-        for g in range(groups):
-            group = pieces[(s * groups + g) * parts : (s * groups + g + 1) * parts]
-            floats = [p[...].astype(jnp.float32) for p in group]
-            total = sum(jnp.sum(f * f, axis=-1, keepdims=True) for f in floats)
-            scale = lax.rsqrt(total / model + 1e-05)
+        dimension_semantics=semantics, vmem_limit_bytes=limit or VMEM_LIMIT
+    )
+
+
+def gathered(block):
+    two = flip(block, "ctx", 2)
+    return [block, flip(block, "ctx", 1), two, flip(two, "ctx", 1)]
+
+
+def after(value, *others):
+    return lax.optimization_barrier((value,) + others)[0]
+
+
+def norm_kernel(layout, place, gain, *refs):
+    out = refs[-1]
+    for s, strand in enumerate(layout):
+        for g, group in enumerate(strand):
+            blocks = [refs[n][...] if at is None else refs[n][at] for n, at in group]
+            width = blocks[0].shape[-1]
+            model = width * len(blocks)
+            floats = [p.astype(jnp.float32) for p in blocks]
+            total = sum(f * f for f in floats)
+            scale = lax.rsqrt(jnp.sum(total, axis=-1, keepdims=True) / model + 1e-05)
             for j, f in enumerate(floats):
-                at = pl.multiple_of((place[0] ^ j) * width, width)
-                lanes = pl.ds(at, width)
+                lanes = pl.ds(pl.multiple_of((place[0] ^ j) * width, width), width)
                 out[s, g, :, lanes] = (f * scale * gain[:, lanes]).astype(jnp.bfloat16)
 
 
-def norm_all(place, gain, pieces, rows, width, parts):
-    flat = [p for strand in pieces for group in strand for p in group]
-    strands, groups = len(pieces), len(pieces[0])
+def norm_all(place, gain, layout, arrays):
+    strands, groups, parts = len(layout), len(layout[0]), len(layout[0][0])
+    rows, width = arrays[0].shape[-2:]
     tile = 128
+
+    def spec(array):
+        if array.ndim == 2:
+            return pl.BlockSpec((tile, width), lambda i, p: (i, 0))
+        return pl.BlockSpec((strands, tile, width), lambda i, p: (0, i, 0))
+
+    shape = (strands, groups, rows, width * parts)
     return pl.pallas_call(
-        norm_kernel,
+        functools.partial(norm_kernel, layout),
         grid_spec=pltpu.PrefetchScalarGridSpec(
             num_scalar_prefetch=1,
             grid=(rows // tile,),
             in_specs=[pl.BlockSpec((1, width * parts), lambda i, p: (0, 0))]
-            + [pl.BlockSpec((tile, width), lambda i, p: (i, 0)) for _ in flat],
+            + [spec(v) for v in arrays],
             out_specs=pl.BlockSpec(
                 (strands, groups, tile, width * parts), lambda i, p: (0, 0, i, 0)
             ),
         ),
-        out_shape=jax.ShapeDtypeStruct((strands, groups, rows, width * parts), jnp.bfloat16),
+        out_shape=jax.ShapeDtypeStruct(shape, jnp.bfloat16),
         compiler_params=params("arbitrary"),
-        cost_estimate=pl.CostEstimate(
-            flops=6 * strands * groups * rows * width * parts,
-            bytes_accessed=4 * strands * groups * rows * width * parts,
-            transcendentals=0,
-        ),
+        cost_estimate=SMALL,
         name="norm",
-    )(place, gain.reshape(1, -1), *flat)
+    )(place, gain.reshape(1, -1), *arrays)
 
 
 def project(normed, weight, b):
@@ -258,51 +270,46 @@
             rim,
             rim,
         ],
-        compiler_params=params("arbitrary", "arbitrary"),
-        cost_estimate=pl.CostEstimate(
-            flops=2 * strands * groups * rows * model * width,
-            bytes_accessed=2 * strands * groups * rows * model + 2 * model * width,
-            transcendentals=0,
-        ),
+        compiler_params=params("arbitrary", "arbitrary", limit=WIDE),
+        cost_estimate=SMALL,
         name="first",
     )(normed, weight)
 
 
-def gates_kernel(normed, weight, *outs):
-    for i, out in enumerate(outs):
-        out[0, 0] = project(normed[0, 0], weight, 1 + i)
-
-
-def gates(normed, weight):
+def gate_kernel(normed, weight, out):
+    out[0, 0] = project(normed[0, 0], weight, 0)
+
+
+def gate_of(normed, weight, b):
     strands, groups, rows, model = normed.shape
-    count, few, depth, width = weight.shape
-    tile = rows // 2
-    shape = jax.ShapeDtypeStruct((strands, groups, rows, width), jnp.float32)
+    count, _, depth, width = weight.shape
     return pl.pallas_call(
-        gates_kernel,
-        grid=(strands, groups, rows // tile),
+        gate_kernel,
+        grid=(strands, groups),
         in_specs=[
-            pl.BlockSpec((1, 1, tile, model), lambda s, g, i: (s, g, i, 0)),
-            pl.BlockSpec((count, few, depth, width), lambda s, g, i: (0, 0, 0, 0)),
-        ],
-        out_specs=[pl.BlockSpec((1, 1, tile, width), lambda s, g, i: (s, g, i, 0))] * (few - 1),
-        out_shape=[shape] * (few - 1),
-        compiler_params=params("arbitrary", "arbitrary", "arbitrary"),
-        cost_estimate=pl.CostEstimate(
-            flops=2 * (few - 1) * strands * groups * rows * model * width,
-            bytes_accessed=2 * strands * groups * rows * model + 2 * few * model * width,
-            transcendentals=0,
-        ),
-        name="gates",
+            pl.BlockSpec((1, 1, rows, model), lambda s, g: (s, g, 0, 0)),
+            pl.BlockSpec((count, 1, depth, width), lambda s, g: (0, b, 0, 0)),
+        ],
+        out_specs=pl.BlockSpec((1, 1, rows, width), lambda s, g: (s, g, 0, 0)),
+        out_shape=jax.ShapeDtypeStruct((strands, groups, rows, width), jnp.float32),
+        compiler_params=params("arbitrary", "arbitrary"),
+        cost_estimate=SMALL,
+        name="gate",
     )(normed, weight)
 
 
-def conv_kernel(last, state, rim_fwd, rim_rev, table, mask, *refs):
+def toeplitz_of(pattern, block):
+    width = pattern.shape[-1]
+    spread = jnp.broadcast_to(pattern, (block, width))
+    return pltpu.roll(spread, 0, 1, stride=1, stride_axis=0).astype(jnp.bfloat16)
+
+
+def conv_kernel(last, state, rim_fwd, rim_rev, patterns, mask, *refs):
     s, g = pl.program_id(0), pl.program_id(1)
-    extended = refs[-1]
+    extended, table = refs[-2:]
     rows, width = state.shape[2:]
     block = rim_fwd.shape[1]
-    heads = table.shape[2]
+    heads = table.shape[0]
     head = width // heads
 
     @pl.when(s == 0)
@@ -314,14 +321,18 @@
     def _():
         extended[:rows] = state[0, 0]
         extended[rows:] = rim_rev[g]
+
+    @pl.when(g == 0)
+    def _():
+        for h in range(heads):
+            table[h] = toeplitz_of(patterns[0, 0, h], block)
 
     for n in range(rows // block):
         span = slice(n * block, (n + 1) * block)
         for h in range(heads):
             lanes = slice(h * head, (h + 1) * head)
-            kernel = table[0, 0, h] * mask[0, 0, n]
             conv = jnp.dot(
-                kernel,
+                table[h] * mask[0, 0, n],
                 extended[n * block : (n + 2) * block, lanes],
                 preferred_element_type=jnp.float32,
             )
@@ -335,9 +346,10 @@
         keep_rims(refs[1][0, 0], s, g, refs[2], refs[3])
 
 
-def conv_section(state, rims, tables, mask, section, gate=None):
+def conv_section(state, rims, patterns, mask, section, gate=None):
     strands, groups, rows, width = state.shape
-    heads, block = tables.shape[2:4]
+    heads = patterns.shape[2]
+    block = rims[0].shape[1]
     rim = jax.ShapeDtypeStruct((groups, block, width), jnp.bfloat16)
     rim_spec = pl.BlockSpec((groups, block, width), lambda s, g: (0, 0, 0))
     row_spec = pl.BlockSpec((1, 1, rows, width), lambda s, g: (s, g, 0, 0))
@@ -346,12 +358,10 @@
         row_spec,
         rim_spec,
         rim_spec,
-        pl.BlockSpec((1, 1, heads, block, 2 * block), lambda s, g: (section, s, 0, 0, 0)),
-        pl.BlockSpec(
-            (1, 1, rows // block, block, 2 * block), lambda s, g: (s, g, 0, 0, 0)
-        ),
+        pl.BlockSpec((1, 1, heads, 1, 2 * block), lambda s, g: (section, s, 0, 0, 0)),
+        pl.BlockSpec((1, 1, rows // block, block, 2 * block), lambda s, g: (s, g, 0, 0, 0)),
     ]
-    args = [state, rims[0], rims[1], tables, mask]
+    args = [state, rims[0], rims[1], patterns, mask]
     if last:
         out_specs = [row_spec]
         out_shape = [jax.ShapeDtypeStruct(state.shape, jnp.float32)]
@@ -366,99 +376,95 @@
         in_specs=in_specs,
         out_specs=out_specs,
         out_shape=out_shape,
-        scratch_shapes=[pltpu.VMEM((rows + block, width), jnp.bfloat16)],
+        scratch_shapes=[
+            pltpu.VMEM((rows + block, width), jnp.bfloat16),
+            pltpu.VMEM((heads, block, 2 * block), jnp.bfloat16),
+        ],
         compiler_params=params("arbitrary", "arbitrary"),
-        cost_estimate=pl.CostEstimate(
-            flops=4 * strands * groups * rows * block * width,
-            bytes_accessed=10 * strands * groups * rows * width,
-            transcendentals=0,
-        ),
+        cost_estimate=SMALL,
         name="conv",
     )(*args)
 
 
-def mix_kernel(normed, weight, conv, out):
-    strands = normed.shape[0]
+def mix_kernel(normed, weight, conv, near, far):
     total = None
-    for s in range(strands):
+    for s in range(normed.shape[0]):
         gate = project(normed[s, 0], weight, 0)
         state = (gate * conv[s, 0]).astype(jnp.bfloat16).astype(jnp.float32)
         total = state if total is None else total + state
-    out[...] = total.astype(jnp.bfloat16)
-
-
-def mix(normed, weight, conv, group):
+    total = total.astype(jnp.bfloat16)
+
+    @pl.when(pl.program_id(0) == 0)
+    def _():
+        far[...] = total
+
+    @pl.when(pl.program_id(0) == 1)
+    def _():
+        near[...] = total
+
+
+def mix(normed, weight, conv):
     strands, groups, rows, model = normed.shape
     count, _, depth, width = weight.shape
-    tile = rows // 2
+    shape = jax.ShapeDtypeStruct((rows, width), jnp.bfloat16)
     return pl.pallas_call(
         mix_kernel,
-        grid=(rows // tile,),
+        grid=(groups,),
         in_specs=[
-            pl.BlockSpec((strands, 1, tile, model), lambda i: (0, group, i, 0)),
-            pl.BlockSpec((count, 1, depth, width), lambda i: (0, 0, 0, 0)),
-            pl.BlockSpec((strands, 1, tile, width), lambda i: (0, group, i, 0)),
-        ],
-        out_specs=pl.BlockSpec((tile, width), lambda i: (i, 0)),
-        out_shape=jax.ShapeDtypeStruct((rows, width), jnp.bfloat16),
-        compiler_params=params("arbitrary"),
-        cost_estimate=pl.CostEstimate(
-            flops=2 * strands * rows * model * width,
-            bytes_accessed=2 * strands * rows * model + 2 * model * width,
-            transcendentals=0,
-        ),
+            pl.BlockSpec((strands, 1, rows, model), lambda g: (0, 1 - g, 0, 0)),
+            pl.BlockSpec((count, 1, depth, width), lambda g: (0, 0, 0, 0)),
+            pl.BlockSpec((strands, 1, rows, width), lambda g: (0, 1 - g, 0, 0)),
+        ],
+        out_specs=[pl.BlockSpec((rows, width), lambda g: (0, 0))] * 2,
+        out_shape=[shape, shape],
+        compiler_params=params("arbitrary", limit=WIDE),
+        cost_estimate=SMALL,
         name="mix",
     )(normed, weight, conv)
 
 
-def out_kernel(place, near, far, *refs):
+def out_kernel(spots, weight, *refs):
     pieces, out = refs[:-1], refs[-1]
-    half = len(pieces) // 2
+    parts = len(pieces) // 2
+    deep = pieces[0].shape[1]
     total = None
-    for weight, group in ((near, pieces[:half]), (far, pieces[half:])):
-        for j, piece in enumerate(group):
-            term = jnp.dot(piece[...], weight[place[0] ^ j], preferred_element_type=jnp.float32)
-            total = term if total is None else total + term
+    for n, piece in enumerate(pieces):
+        group = spots[1] if n < parts else 1 - spots[1]
+        rows = pl.ds(pl.multiple_of(group * deep, deep), deep)
+        term = jnp.dot(
+            piece[...],
+            weight[spots[0] ^ (n % parts), rows, :],
+            preferred_element_type=jnp.float32,
+        )
+        total = term if total is None else total + term
     out[...] = total.astype(jnp.bfloat16)
 
 
-def project_out(place, near, far, pieces):
-    rows, width = pieces[0].shape
-    whole = pl.BlockSpec(near.shape, lambda i, p: (0, 0, 0))
+def project_out(spots, weight, pieces):
+    rows, deep = pieces[0].shape
+    width = weight.shape[-1]
     tile = rows // 2
     return pl.pallas_call(
         out_kernel,
         grid_spec=pltpu.PrefetchScalarGridSpec(
             num_scalar_prefetch=1,
             grid=(rows // tile,),
-            in_specs=[whole, whole]
-            + [pl.BlockSpec((tile, width), lambda i, p: (i, 0)) for _ in pieces],
-            out_specs=pl.BlockSpec((tile, near.shape[-1]), lambda i, p: (i, 0)),
+            in_specs=[pl.BlockSpec(weight.shape, lambda i, p: (0, 0, 0))]
+            + [pl.BlockSpec((tile, deep), lambda i, p: (i, 0)) for _ in pieces],
+            out_specs=pl.BlockSpec((tile, width), lambda i, p: (i, 0)),
         ),
-        out_shape=jax.ShapeDtypeStruct((rows, near.shape[-1]), jnp.bfloat16),
+        out_shape=jax.ShapeDtypeStruct((rows, width), jnp.bfloat16),
         compiler_params=params("arbitrary"),
-        cost_estimate=pl.CostEstimate(
-            flops=2 * rows * width * len(pieces) * near.shape[-1],
-            bytes_accessed=2 * near.size * 2 + 2 * rows * width * len(pieces),
-            transcendentals=0,
-        ),
+        cost_estimate=SMALL,
         name="out",
-    )(place, near, far, *pieces)
-
-
-def conv_tables(taps):
-    sections, heads, block = taps.shape
-    zero = jnp.zeros((sections, heads, block), taps.dtype)
-    one = jnp.zeros((sections, heads, 1), taps.dtype)
-    patterns = jnp.stack(
-        [
-            jnp.concatenate([one, taps[:, :, ::-1], zero], axis=-1),
-            jnp.concatenate([taps, zero, one], axis=-1),
-        ],
-        axis=1,
-    )
-    repeated = jnp.tile(patterns, (1, 1, 1, block))[..., : block * 2 * block]
-    return repeated.reshape(sections, 2, heads, block, 2 * block)
+    )(spots, weight, *pieces)
+
+
+def conv_patterns(taps):
+    zero = jnp.zeros_like(taps)
+    forward = jnp.concatenate([zero[..., :1], taps[..., ::-1], zero[..., 1:]], axis=-1)
+    reverse = jnp.concatenate([taps, zero], axis=-1)
+    return jnp.stack([forward, reverse], axis=1)[:, :, :, None, :]
 
 
 def doc_masks(offsets, start, rows, block, seq_len):
@@ -494,11 +500,6 @@
 
     columns = lax.dynamic_slice_in_dim(in_weight, mine * half, half, axis=2)
     early = lax.all_gather(columns[:sections], "ctx", axis=0)
-    late = lax.all_gather(columns[sections:], "ctx", axis=0)
-    near = lax.all_gather(
-        lax.dynamic_slice_in_dim(out_weight, mine * half, half, axis=0), "ctx", axis=0
-    )
-    far = flip(near, "grp", 1)
 
     letters = base_embed.shape[0]
     alphabet = jnp.arange(letters, dtype=jnp.int32)
@@ -509,39 +510,53 @@
     for hidden, table in ((fwd_hidden, base_embed), (rev_hidden, swapped.astype(jnp.bfloat16))):
         embed = jnp.dot(onehot, table, preferred_element_type=jnp.float32)
         inputs.append((hidden.astype(jnp.float32) + embed).astype(jnp.bfloat16))
-    other_x = [flip(v, "ch", 2) for v in inputs]
-    other_y = [flip(v, "grp", 1) for v in inputs]
-    other_xy = [flip(other_x[0], "grp", 1), flip(other_y[1], "ch", 2)]
-    pieces = []
-    for s in range(2):
-        own = [inputs[s], flip(inputs[s], "ch", 1), other_x[s], flip(other_x[s], "ch", 1)]
-        far_side = [other_y[s], flip(other_y[s], "ch", 1), other_xy[s], flip(other_xy[s], "ch", 1)]
-        pieces.append([own, far_side])
-    where = place.astype(jnp.int32).reshape(1)
-    normed = norm_all(where, norm_gain, pieces, rows, width, parts)
-
+    own = jnp.stack(inputs)
+    x = flip(own, "ch", 2)
+    y = flip(own, "grp", 1)
+    core = flip(own, "ch", 1)
+    x, y, core = lax.optimization_barrier((x, y, core))
+    xy = [flip(x[0], "grp", 1), flip(y[1], "ch", 2)]
+    arrays = [own, core, x, flip(x, "ch", 1), y, flip(y, "ch", 1)]
+    arrays += [xy[0], flip(xy[0], "ch", 1), xy[1], flip(xy[1], "ch", 1)]
+    layout = [
+        [
+            [(n, s) for n in range(1, 5)],
+            [(5, s), (6, s), (7 + 2 * s, None), (8 + 2 * s, None)],
+        ]
+        for s in range(2)
+    ]
+    layout = [[[(n - 1, at) for n, at in group] for group in strand] for strand in layout]
+    spots = jnp.stack([place, mine]).astype(jnp.int32)
+    normed = norm_all(spots, norm_gain, layout, arrays)
+    late = lax.all_gather(after(columns[sections:], x), "ctx", axis=0)
     both_offsets = jnp.stack([offsets, flip(offsets, "grp", 1)])
     mask = doc_masks(both_offsets, here * rows, rows, block, seq_len)
     own_heads = heads // groups
     taps = lax.dynamic_slice_in_dim(filters, mine * own_heads, own_heads, axis=1)
-    tables = conv_tables(taps.astype(jnp.bfloat16))
-
+    patterns = conv_patterns(taps.astype(jnp.bfloat16).astype(jnp.float32))
+
+    def shift_rims(rims):
+        return shifted(rims[0], "ctx", 1), shifted(rims[1], "ctx", -1)
+
+    early, normed, mask, patterns = lax.optimization_barrier((early, normed, mask, patterns))
+    whole_out = lax.all_gather(after(out_weight, early), "ctx", axis=0)
     state, *rims = first(normed, early, block)
-    gate = gates(normed, early)
-    for section in range(sections):
-        rims = (shifted(rims[0], "ctx", 1), shifted(rims[1], "ctx", -1))
-        if section + 1 < sections:
-            state, *rims = conv_section(state, rims, tables, mask, section, gate[section])
-        else:
-            (conv,) = conv_section(state, rims, tables, mask, section)
-    mixed_far = mix(normed, late, conv, 1)
-    mixed_near = mix(normed, late, conv, 0)
+    rims = shift_rims(rims)
+    gate = gate_of(normed, early, 1)
+    state, *rims = conv_section(state, rims, patterns, mask, 0, gate)
+    state, normed = lax.optimization_barrier((state, normed))
+    rims = shift_rims(rims)
+    gate = gate_of(normed, early, 2)
+    state, *rims = conv_section(state, rims, patterns, mask, 1, gate)
+    rims = shift_rims(rims)
+    (conv,) = conv_section(state, rims, patterns, mask, 2)
+    mixed_near, mixed_far = mix(normed, late, conv)
     from_y = flip(mixed_far, "grp", 1)
     from_xy = across(mixed_far, 2)
     from_x = flip(mixed_near, "ch", 2)
     near_pieces = [mixed_near, flip(mixed_near, "ch", 1), from_x, flip(from_x, "ch", 1)]
     far_pieces = [from_y, flip(from_y, "ch", 1), from_xy, flip(from_xy, "ch", 1)]
-    return project_out(where, near, far, near_pieces + far_pieces)
+    return project_out(spots, whole_out, near_pieces + far_pieces)
 
 
 def solution(mesh):

time: 185 us -> 172 us (0.930)
  waiting for transfers between devices: 78.7 us -> 69.4 us
  local copies, waits for them, and re-layouts: 30.9 us -> 22.3 us
  Pallas kernels: 30.8 us -> 35.5 us
  starting transfers between devices: 27.7 us -> 25.6 us
  other arithmetic: 0.48 us -> 2.54 us
    all_gather x1, waiting for transfers between devices: 36.3 us -> 4.91 us  [paired(): early = lax.all_gather(columns[:sections], 'ctx', axis=0)]
    ppermute x22 -> x16, waiting for transfers between devices: 27.4 us -> 41.7 us  [flip(): return lax.ppermute(block, axis, [(i, i ^ bit) for i in range(count)])]
    another operation x4 -> x0, local copies, waits for them, and re-layouts: 5.88 us -> none  [the longest x2 5.87 us: conv_tables(): repeated = jnp.tile(patterns, (1, 1, 1, block))[..., :block * 2 * block]]
    all_gather x2, waiting for transfers between devices: 0.01 us -> 5.3 us  [the longest x1 5.29 us: paired(): whole_out = lax.all_gather(after(out_weight, early), 'ctx', axis=0)]
    ppermute x22 -> x16, starting transfers between devices: 14.9 us -> 10.5 us  [flip(): return lax.ppermute(block, axis, [(i, i ^ bit) for i in range(count)])]
    pallas_call x1, Pallas kernels: 2.99 us -> 6.87 us  [first(): pl.pallas_call(first_kernel, grid=(strands, groups), in_specs=[pl.BlockSp...]
    squeeze x0 -> x2, local copies, waits for them, and re-layouts: none -> 3.74 us  [paired(): xy = [flip(x[0], 'grp', 1), flip(y[1], 'ch', 2)]]
    reshape x1 -> x0, local copies, waits for them, and re-layouts: 3.22 us -> none  [conv_tables(): return repeated.reshape(sections, 2, heads, block, 2 * block)]
  transfers between devices with their start and end apart: 32 -> 26, of which waited for: 17 -> 12; matrix products, arithmetic and copies ran while one was open for 9% -> 6% of each run, Pallas kernels for 15% -> 19%
where the time goes in v2:
time: 172 us; the launch traced here: 171 us
  waiting for transfers between devices  69.4 us (40%)
  Pallas kernels  35.5 us (21%)
  starting transfers between devices  25.6 us (15%)
  local copies, waits for them, and re-layouts  22.3 us (13%)
  between operations  13.5 us (8%)
  other arithmetic  2.54 us (1%)
  matrix products  2.43 us (1%)
    ppermute x16, waiting for transfers between devices, flip(): return lax.ppermute(block, axis, [(i, i ^ bit) for i in range(count)])  41.7 us
    ppermute x6, waiting for transfers between devices, shifted(): return lax.ppermute(value, axis, pairs)  17.5 us
    unnamed x42, local copies, waits for them, and re-layouts  16.7 us
    ppermute x6, starting transfers between devices, shifted(): return lax.ppermute(value, axis, pairs)  13.8 us
    ppermute x16, starting transfers between devices, flip(): return lax.ppermute(block, axis, [(i, i ^ bit) for i in range(count)])  10.5 us
    pallas_call x1, Pallas kernels, norm_all(): pl.pallas_call(functools.partial(norm_kernel, layout), grid_spec=pltpu.Pr...  8.67 us
    pallas_call x1, Pallas kernels, first(): pl.pallas_call(first_kernel, grid=(strands, groups), in_specs=[pl.BlockSp...  6.87 us
    pallas_call x1, Pallas kernels, mix(): pl.pallas_call(mix_kernel, grid=(groups,), in_specs=[pl.BlockSpec((strand...  6.42 us
  transfers between devices with their start and end apart: 26, of which 12 were waited for; matrix products, arithmetic and copies ran while one was open for 6% of the time, Pallas kernels for 19%

profile of v2, /device:TPU:0, one launch (start us, length us, event | category | flops | bytes accessed | tf_op | source)
XLA Modules:
  0.0 171.2 jit_solution(11420349683171437538)
XLA Ops:
  6.6 1.5 copy-done
  8.1 0.9 constant_dynamic-slice_fusion
  9.2 1.2 fusion.3
  10.4 1.3 fusion.2
  11.6 1.3 pad_maximum_fusion.refs_0_
  12.9 3.0 %collective-permute-start = (bf16[2,512,512]{2,1,0:T(8,128)(2,1)S(1)}, bf16[2,512,512]{2,1,0:T(8,128)(2,1)}, u32[]{:S(2)}, u32[]{:S(2)}) collective-permute-start(bf16[2,512,512]{2,1,0:T(8,128)(2,1)S(1)} %pad_maximum_fusion.refs_0_), channel_id=1, source_target_pairs={{0,2},{1,3},{2,0},{3,1},{4,6},{5,7},{6,4},{7,5},{8,10},{9,11},{10,... | collective-permute-start | bytes 3145736 | tf_op jit(solution)/shard_map/ppermute | solution.py:149
  15.9 1.5 collective-permute-start.1
  19.8 20.9 %collective-permute-done.9 = s32[16]{0:T(128)S(1)} collective-permute-done((s32[16]{0:T(128)S(1)}, s32[16]{0:T(128)S(1)}, u32[]{:S(2)}, u32[]{:S(2)}) %collective-permute-start.9) | collective-permute-done | bytes 96 | tf_op jit(solution)/shard_map/ppermute | solution.py:149
  40.8 1.9 %slice_bitcast_fusion.1 = bf16[512,512]{1,0:T(8,128)(2,1)} fusion(bf16[2,512,512]{2,1,0:T(8,128)(2,1)} %collective-permute-done.refs_2_), kind=kLoop, calls=%fused_computation.10 | loop fusion | bytes 1048576 | tf_op jit(solution)/shard_map/squeeze | solution.py:518
  42.6 1.5 collective-permute-start.5
  44.2 1.9 %slice_bitcast_fusion = bf16[512,512]{1,0:T(8,128)(2,1)} fusion(bf16[2,512,512]{2,1,0:T(8,128)(2,1)} %collective-permute-done.1.refs_4_), kind=kLoop, calls=%fused_computation.9 | loop fusion | bytes 1048576 | tf_op jit(solution)/shard_map/squeeze | solution.py:518
  47.3 8.1 %collective-permute-done.5.refs_6_ = bf16[512,512]{1,0:T(8,128)(2,1)} collective-permute-done((bf16[512,512]{1,0:T(8,128)(2,1)}, bf16[512,512]{1,0:T(8,128)(2,1)}, u32[]{:S(2)}, u32[]{:S(2)}) %collective-permute-start.5) | collective-permute-done | bytes 524320 | tf_op jit(solution)/shard_map/ppermute | solution.py:149
  55.4 3.1 %collective-permute-done.7.refs_8_ = bf16[512,512]{1,0:T(8,128)(2,1)} collective-permute-done((bf16[512,512]{1,0:T(8,128)(2,1)}, bf16[512,512]{1,0:T(8,128)(2,1)}, u32[]{:S(2)}, u32[]{:S(2)}) %collective-permute-start.7) | collective-permute-done | bytes 524320 | tf_op jit(solution)/shard_map/ppermute | solution.py:149
  58.8 1.8 %collective-permute-done.8.refs_9_ = bf16[512,512]{1,0:T(8,128)(2,1)S(1)} collective-permute-done((bf16[512,512]{1,0:T(8,128)(2,1)}, bf16[512,512]{1,0:T(8,128)(2,1)S(1)}, u32[]{:S(2)}, u32[]{:S(2)}) %collective-permute-start.8) | collective-permute-done | bytes 524320 | tf_op jit(solution)/shard_map/ppermute | solution.py:149
  60.7 1.2 copy-done.6
  61.9 8.7 %norm.1.normed = bf16[2,2,512,2048]{3,2,1,0:T(8,128)(2,1)} custom-call(s32[2]{0:T(128)S(1)} %pad_add_fusion.2.place.spots, f32[1,2048]{1,0:T(1,128)S(1)} %bitcast.33, bf16[2,512,512]{2,1,0:T(8,128)(2,1)S(1)} %copy-done.6, bf16[2,512,512]{2,1,0:T(8,128)(2,1)} %collective-permute-done.2.refs_1_, bf16[2,512,512]{2,1,0:T(8,128)(2,1)} %collective-permute-done.refs_2_, ...), custom_call_target="tpu_custom_call" | custom-call | flops 1 | bytes 1 | tf_op jit(solution)/shard_map/norm/pallas_call | solution.py:201
  70.6 4.9 %all-gather.7.cloned.1.call-done = bf16[12,512,256]{2,1,0:T(8,128)(2,1)} async-done(((bf16[3,512,256]{2,1,0:T(8,128)(2,1)}), bf16[12,512,256]{2,1,0:T(8,128)(2,1)}) %all-gather.7.cloned.1.call-update) | async-done | bytes 3145744 | tf_op jit(solution)/shard_map/all_gather | solution.py:502
  75.5 6.9 %first.1 = (bf16[2,2,512,256]{3,2,1,0:T(8,128)(2,1)}, bf16[2,128,256]{2,1,0:T(8,128)(2,1)}, bf16[2,128,256]{2,1,0:T(8,128)(2,1)}) custom-call(bf16[2,2,512,2048]{3,2,1,0:T(8,128)(2,1)} %norm.1.normed, bf16[4,3,512,256]{3,2,1,0:T(8,128)(2,1)} %bitcast.29), custom_call_target="tpu_custom_call" | custom-call | flops 1 | bytes 1 | tf_op jit(solution)/shard_map/first/pallas_call | solution.py:256
  82.4 1.3 collective-permute-start.10
  83.7 1.3 collective-permute-start.11
  85.0 3.4 %copy-done.1 = bf16[2,2,512,2048]{3,2,1,0:T(8,128)(2,1)S(1)} copy-done((bf16[2,2,512,2048]{3,2,1,0:T(8,128)(2,1)S(1)}, bf16[2,2,512,2048]{3,2,1,0:T(8,128)(2,1)}, u32[]{:S(2)}) %copy-start.1) | copy-done | bytes 8388632
  88.4 3.0 %gate.2.refs_0_ = f32[2,2,512,256]{3,2,1,0:T(8,128)S(1)} custom-call(bf16[2,2,512,2048]{3,2,1,0:T(8,128)(2,1)S(1)} %copy-done.1, bf16[4,3,512,256]{3,2,1,0:T(8,128)(2,1)S(1)} %bitcast.30), custom_call_target="tpu_custom_call" | custom-call | flops 1 | bytes 1 | tf_op jit(solution)/shard_map/gate/pallas_call | solution.py:286
  91.4 6.6 %collective-permute-done.11.rim_rev = bf16[2,128,256]{2,1,0:T(8,128)(2,1)S(1)} collective-permute-done((bf16[2,128,256]{2,1,0:T(8,128)(2,1)}, bf16[2,128,256]{2,1,0:T(8,128)(2,1)S(1)}, u32[]{:S(2)}, u32[]{:S(2)}) %collective-permute-start.11) | collective-permute-done | bytes 131104 | tf_op jit(solution)/shard_map/ppermute | solution.py:28
  98.0 1.6 conv.3
  99.6 4.0 %collective-permute-start.12 = (bf16[2,128,256]{2,1,0:T(8,128)(2,1)S(1)}, bf16[2,128,256]{2,1,0:T(8,128)(2,1)S(1)}, u32[]{:S(2)}, u32[]{:S(2)}) collective-permute-start(bf16[2,128,256]{2,1,0:T(8,128)(2,1)S(1)} %get-tuple-element.42), channel_id=1, source_target_pairs={{0,4},{4,8},{8,12},{1,5},{5,9},{9,13},{2,6},{6,10},{10,14},{3,7},{... | collective-permute-start | bytes 393224 | tf_op jit(solution)/shard_map/ppermute | solution.py:28
  103.7 1.3 collective-permute-start.13
  105.0 3.4 %copy-done.2 = bf16[2,2,512,2048]{3,2,1,0:T(8,128)(2,1)S(1)} copy-done((bf16[2,2,512,2048]{3,2,1,0:T(8,128)(2,1)S(1)}, bf16[2,2,512,2048]{3,2,1,0:T(8,128)(2,1)}, u32[]{:S(2)}) %copy-start.2) | copy-done | bytes 8388632
  108.4 3.0 %gate.3.refs_0_ = f32[2,2,512,256]{3,2,1,0:T(8,128)S(1)} custom-call(bf16[2,2,512,2048]{3,2,1,0:T(8,128)(2,1)S(1)} %copy-done.2, bf16[4,3,512,256]{3,2,1,0:T(8,128)(2,1)S(1)} %bitcast.31), custom_call_target="tpu_custom_call" | custom-call | flops 1 | bytes 1 | tf_op jit(solution)/shard_map/gate/pallas_call | solution.py:286
  111.4 1.7 conv.4
  113.1 4.6 %collective-permute-start.14 = (bf16[2,128,256]{2,1,0:T(8,128)(2,1)S(1)}, bf16[2,128,256]{2,1,0:T(8,128)(2,1)S(1)}, u32[]{:S(2)}, u32[]{:S(2)}) collective-permute-start(bf16[2,128,256]{2,1,0:T(8,128)(2,1)S(1)} %get-tuple-element.45), channel_id=1, source_target_pairs={{0,4},{4,8},{8,12},{1,5},{5,9},{9,13},{2,6},{6,10},{10,14},{3,7},{... | collective-permute-start | bytes 393224 | tf_op jit(solution)/shard_map/ppermute | solution.py:28
  117.6 1.3 collective-permute-start.15
  118.9 3.6 %collective-permute-done.14.rim_fwd = bf16[2,128,256]{2,1,0:T(8,128)(2,1)S(1)} collective-permute-done((bf16[2,128,256]{2,1,0:T(8,128)(2,1)S(1)}, bf16[2,128,256]{2,1,0:T(8,128)(2,1)S(1)}, u32[]{:S(2)}, u32[]{:S(2)}) %collective-permute-start.14) | collective-permute-done | bytes 131104 | tf_op jit(solution)/shard_map/ppermute | solution.py:28
  122.5 7.3 %collective-permute-done.15.rim_rev = bf16[2,128,256]{2,1,0:T(8,128)(2,1)S(1)} collective-permute-done((bf16[2,128,256]{2,1,0:T(8,128)(2,1)S(1)}, bf16[2,128,256]{2,1,0:T(8,128)(2,1)S(1)}, u32[]{:S(2)}, u32[]{:S(2)}) %collective-permute-start.15) | collective-permute-done | bytes 131104 | tf_op jit(solution)/shard_map/ppermute | solution.py:28
  129.8 1.5 conv.5
  131.3 1.3 copy-done.4
  132.6 6.4 %mix.1 = (bf16[512,256]{1,0:T(8,128)(2,1)}, bf16[512,256]{1,0:T(8,128)(2,1)}) custom-call(bf16[2,2,512,2048]{3,2,1,0:T(8,128)(2,1)} %norm.1.normed, bf16[4,1,512,256]{3,2,1,0:T(8,128)(2,1)} %bitcast.34, f32[2,2,512,256]{3,2,1,0:T(8,128)} %copy-done.4), custom_call_target="tpu_custom_call" | custom-call | flops 1 | bytes 1 | tf_op jit(solution)/shard_map/mix/pallas_call | solution.py:410
  139.0 0.8 collective-permute-start.17
  139.9 1.5 collective-permute-start.19
  141.4 1.2 collective-permute-start.21
  142.5 3.1 %collective-permute-done.17.refs_2_ = bf16[512,256]{1,0:T(8,128)(2,1)S(1)} collective-permute-done((bf16[512,256]{1,0:T(8,128)(2,1)}, bf16[512,256]{1,0:T(8,128)(2,1)S(1)}, u32[]{:S(2)}, u32[]{:S(2)}) %collective-permute-start.17) | collective-permute-done | bytes 262176 | tf_op jit(solution)/shard_map/ppermute | solution.py:149
  145.6 3.6 %collective-permute-done.19.refs_4_ = bf16[512,256]{1,0:T(8,128)(2,1)S(1)} collective-permute-done((bf16[512,256]{1,0:T(8,128)(2,1)}, bf16[512,256]{1,0:T(8,128)(2,1)S(1)}, u32[]{:S(2)}, u32[]{:S(2)}) %collective-permute-start.19) | collective-permute-done | bytes 262176 | tf_op jit(solution)/shard_map/ppermute | solution.py:149
  149.8 1.0 collective-permute-done.20.refs_5_
  152.2 5.3 %all-gather.9.cloned.1.call-done = bf16[2048,512]{1,0:T(8,128)(2,1)} async-done(((bf16[512,512]{1,0:T(8,128)(2,1)}), bf16[2048,512]{1,0:T(8,128)(2,1)}) %all-gather.9.cloned.1.call-update) | async-done | bytes 2097168 | tf_op jit(solution)/shard_map/all_gather | solution.py:542
  157.5 1.6 copy-done.7
  159.1 0.9 copy-done.9
  160.0 0.9 copy-done.11
  161.0 0.9 copy-done.13
  161.9 2.7 %out.1 = bf16[512,512]{1,0:T(8,128)(2,1)} custom-call(s32[2]{0:T(128)S(1)} %pad_add_fusion.2.place.spots, bf16[4,512,512]{2,1,0:T(8,128)(2,1)S(1)} %bitcast.32, bf16[512,256]{1,0:T(8,128)(2,1)S(1)} %copy-done.9, bf16[512,256]{1,0:T(8,128)(2,1)S(1)} %collective-permute-done.16.refs_1_, bf16[512,256]{1,0:T(8,128)(2,1)S(1)} %collective-permute-done.17.refs_2_, ...), custom_call_target="tpu_custom_call" | custom-call | flops 1 | bytes 1 | tf_op jit(solution)/shard_map/out/pallas_call | solution.py:447
  (85 shorter events, 6.0 us)
Async XLA Ops:
  6.5 1.6 copy-start
  6.5 2.6 %copy-start.18 = (s32[512]{0:T(512)S(1)}, s32[512]{0:T(512)}, u32[]{:S(2)}) copy-start(s32[512]{0:T(512)} %param.12) | copy-start | bytes 6148
  6.5 2.6 %copy-start.17 = (bf16[4,512]{1,0:T(4,128)(2,1)S(1)}, bf16[4,512]{1,0:T(4,128)(2,1)}, u32[]{:S(2)}) copy-start(bf16[4,512]{1,0:T(4,128)(2,1)} %param.15) | copy-start | bytes 12292
  6.5 2.6 %copy-start.15 = (bf16[512,512]{1,0:T(8,128)(2,1)S(1)}, bf16[512,512]{1,0:T(8,128)(2,1)}, u32[]{:S(2)}) copy-start(bf16[512,512]{1,0:T(8,128)(2,1)} %param.10) | copy-start | bytes 1572868
  6.5 3.8 %copy-start.16 = (bf16[512,512]{1,0:T(8,128)(2,1)S(1)}, bf16[512,512]{1,0:T(8,128)(2,1)}, u32[]{:S(2)}) copy-start(bf16[512,512]{1,0:T(8,128)(2,1)} %param.11) | copy-start | bytes 1572868
  6.5 3.8 %copy-start.19 = (s32[4]{0:T(128)S(1)}, s32[4]{0:T(128)}, u32[]{:S(2)}) copy-start(s32[4]{0:T(128)} %param.13) | copy-start | bytes 52
  6.6 68.9 %all-gather.7.cloned.1.call-start = ((), (), s32[]{:S(2)}) async-start(), calls=%async_computation | async-start | bytes 3932160 | tf_op jit(solution)/shard_map/all_gather | solution.py:502
  9.1 8.4 %copy-start.20 = (s32[16]{0:T(128)S(1)}, s32[16]{0:T(128)}, u32[]{:S(2)}) copy-start(s32[16]{0:T(128)} %param.14) | copy-start | bytes 196
  9.1 123.5 %all-gather.11.cloned.1.call-start = ((), (), s32[]{:S(2)}) async-start(), calls=%async_computation.2 | async-start | bytes 1310720 | tf_op jit(solution)/shard_map/all_gather | solution.py:531
  12.9 45.6 %copy-start.5 = (bf16[2,512,512]{2,1,0:T(8,128)(2,1)}, bf16[2,512,512]{2,1,0:T(8,128)(2,1)S(1)}, u32[]{:S(2)}) copy-start(bf16[2,512,512]{2,1,0:T(8,128)(2,1)S(1)} %pad_maximum_fusion.refs_0_) | copy-start | bytes 3145732
  12.9 27.7 %collective-permute-start = (bf16[2,512,512]{2,1,0:T(8,128)(2,1)S(1)}, bf16[2,512,512]{2,1,0:T(8,128)(2,1)}, u32[]{:S(2)}, u32[]{:S(2)}) collective-permute-start(bf16[2,512,512]{2,1,0:T(8,128)(2,1)S(1)} %pad_maximum_fusion.refs_0_), channel_id=1, source_target_pairs={{0,2},{1,3},{2,0},{3,1},{4,6},{5,7},{6,4},{7,5},{8,10},{9,11},{10,... | collective-permute-start | bytes 3145736 | tf_op jit(solution)/shard_map/ppermute | solution.py:149
  15.9 24.7 %collective-permute-start.1 = (bf16[2,512,512]{2,1,0:T(8,128)(2,1)S(1)}, bf16[2,512,512]{2,1,0:T(8,128)(2,1)}, u32[]{:S(2)}, u32[]{:S(2)}) collective-permute-start(bf16[2,512,512]{2,1,0:T(8,128)(2,1)S(1)} %pad_maximum_fusion.refs_0_), channel_id=1, source_target_pairs={{0,16},{16,0},{1,17},{17,1},{2,18},{18,2},{3,19},{19,3},{4,20},{20... | collective-permute-start | bytes 3145736 | tf_op jit(solution)/shard_map/ppermute | solution.py:149
  17.4 23.2 %collective-permute-start.2 = (bf16[2,512,512]{2,1,0:T(8,128)(2,1)S(1)}, bf16[2,512,512]{2,1,0:T(8,128)(2,1)}, u32[]{:S(2)}, u32[]{:S(2)}) collective-permute-start(bf16[2,512,512]{2,1,0:T(8,128)(2,1)S(1)} %pad_maximum_fusion.refs_0_), channel_id=1, source_target_pairs={{0,1},{1,0},{2,3},{3,2},{4,5},{5,4},{6,7},{7,6},{8,9},{9,8},{10,11... | collective-permute-start | bytes 3145736 | tf_op jit(solution)/shard_map/ppermute | solution.py:149
  17.5 23.2 %collective-permute-start.9 = (s32[16]{0:T(128)S(1)}, s32[16]{0:T(128)S(1)}, u32[]{:S(2)}, u32[]{:S(2)}) collective-permute-start(s32[16]{0:T(128)S(1)} %copy-done.20), channel_id=1, source_target_pairs={{0,16},{16,0},{1,17},{17,1},{2,18},{18,2},{3,19},{19,3},{4,20},{20... | collective-permute-start | bytes 200 | tf_op jit(solution)/shard_map/ppermute | solution.py:149
  18.9 41.7 %copy-start.14 = (f32[2048]{0:T(1024)S(1)}, f32[2048]{0:T(1024)}, u32[]{:S(2)}) copy-start(f32[2048]{0:T(1024)} %param.16) | copy-start | bytes 24580
  40.7 116.8 %all-gather.9.cloned.1.call-start = ((), (), s32[]{:S(2)}) async-start(), calls=%async_computation.1 | async-start | bytes 2621440 | tf_op jit(solution)/shard_map/all_gather | solution.py:542
  42.6 12.8 %collective-permute-start.5 = (bf16[512,512]{1,0:T(8,128)(2,1)}, bf16[512,512]{1,0:T(8,128)(2,1)}, u32[]{:S(2)}, u32[]{:S(2)}) collective-permute-start(bf16[512,512]{1,0:T(8,128)(2,1)} %slice_bitcast_fusion.1), channel_id=1, source_target_pairs={{0,16},{16,0},{1,17},{17,1},{2,18},{18,2},{3,19},{19,3},{4,20},{20... | collective-permute-start | bytes 1572872 | tf_op jit(solution)/shard_map/ppermute | solution.py:149
  46.0 12.5 %collective-permute-start.7 = (bf16[512,512]{1,0:T(8,128)(2,1)}, bf16[512,512]{1,0:T(8,128)(2,1)}, u32[]{:S(2)}, u32[]{:S(2)}) collective-permute-start(bf16[512,512]{1,0:T(8,128)(2,1)} %slice_bitcast_fusion), channel_id=1, source_target_pairs={{0,2},{1,3},{2,0},{3,1},{4,6},{5,7},{6,4},{7,5},{8,10},{9,11},{10,... | collective-permute-start | bytes 1572872 | tf_op jit(solution)/shard_map/ppermute | solution.py:149
  46.7 14.0 %collective-permute-start.3 = (bf16[2,512,512]{2,1,0:T(8,128)(2,1)}, bf16[2,512,512]{2,1,0:T(8,128)(2,1)}, u32[]{:S(2)}, u32[]{:S(2)}) collective-permute-start(bf16[2,512,512]{2,1,0:T(8,128)(2,1)} %collective-permute-done.refs_2_), channel_id=1, source_target_pairs={{0,1},{1,0},{2,3},{3,2},{4,5},{5,4},{6,7},{7,6},{8,9},{9,8},{10,11... | collective-permute-start | bytes 3145736 | tf_op jit(solution)/shard_map/ppermute | solution.py:149
  46.8 13.9 %collective-permute-start.4 = (bf16[2,512,512]{2,1,0:T(8,128)(2,1)}, bf16[2,512,512]{2,1,0:T(8,128)(2,1)}, u32[]{:S(2)}, u32[]{:S(2)}) collective-permute-start(bf16[2,512,512]{2,1,0:T(8,128)(2,1)} %collective-permute-done.1.refs_4_), channel_id=1, source_target_pairs={{0,1},{1,0},{2,3},{3,2},{4,5},{5,4},{6,7},{7,6},{8,9},{9,8},{10,11... | collective-permute-start | bytes 3145736 | tf_op jit(solution)/shard_map/ppermute | solution.py:149
  55.4 3.4 %collective-permute-start.6 = (bf16[512,512]{1,0:T(8,128)(2,1)}, bf16[512,512]{1,0:T(8,128)(2,1)S(1)}, u32[]{:S(2)}, u32[]{:S(2)}) collective-permute-start(bf16[512,512]{1,0:T(8,128)(2,1)} %collective-permute-done.5.refs_6_), channel_id=1, source_target_pairs={{0,1},{1,0},{2,3},{3,2},{4,5},{5,4},{6,7},{7,6},{8,9},{9,8},{10,11... | collective-permute-start | bytes 1572872 | tf_op jit(solution)/shard_map/ppermute | solution.py:149
  58.5 2.1 %collective-permute-start.8 = (bf16[512,512]{1,0:T(8,128)(2,1)}, bf16[512,512]{1,0:T(8,128)(2,1)S(1)}, u32[]{:S(2)}, u32[]{:S(2)}) collective-permute-start(bf16[512,512]{1,0:T(8,128)(2,1)} %collective-permute-done.7.refs_8_), channel_id=1, source_target_pairs={{0,1},{1,0},{2,3},{3,2},{4,5},{5,4},{6,7},{7,6},{8,9},{9,8},{10,11... | collective-permute-start | bytes 1572872 | tf_op jit(solution)/shard_map/ppermute | solution.py:149
  60.7 1.2 copy-start.6
  75.5 9.5 %copy-start.3 = (bf16[12,512,256]{2,1,0:T(8,128)(2,1)S(1)}, bf16[12,512,256]{2,1,0:T(8,128)(2,1)}, u32[]{:S(2)}) copy-start(bf16[12,512,256]{2,1,0:T(8,128)(2,1)} %all-gather.7.cloned.1.call-done) | copy-start | bytes 9437188
  82.4 9.0 %collective-permute-start.10 = (bf16[2,128,256]{2,1,0:T(8,128)(2,1)}, bf16[2,128,256]{2,1,0:T(8,128)(2,1)S(1)}, u32[]{:S(2)}, u32[]{:S(2)}) collective-permute-start(bf16[2,128,256]{2,1,0:T(8,128)(2,1)} %get-tuple-element.34), channel_id=1, source_target_pairs={{0,4},{4,8},{8,12},{1,5},{5,9},{9,13},{2,6},{6,10},{10,14},{3,7},{... | collective-permute-start | bytes 393224 | tf_op jit(solution)/shard_map/ppermute | solution.py:28
  83.7 14.3 %collective-permute-start.11 = (bf16[2,128,256]{2,1,0:T(8,128)(2,1)}, bf16[2,128,256]{2,1,0:T(8,128)(2,1)S(1)}, u32[]{:S(2)}, u32[]{:S(2)}) collective-permute-start(bf16[2,128,256]{2,1,0:T(8,128)(2,1)} %get-tuple-element.35), channel_id=1, source_target_pairs={{4,0},{8,4},{12,8},{5,1},{9,5},{13,9},{6,2},{10,6},{14,10},{7,3},{... | collective-permute-start | bytes 393224 | tf_op jit(solution)/shard_map/ppermute | solution.py:28
  85.0 3.4 %copy-start.1 = (bf16[2,2,512,2048]{3,2,1,0:T(8,128)(2,1)S(1)}, bf16[2,2,512,2048]{3,2,1,0:T(8,128)(2,1)}, u32[]{:S(2)}) copy-start(bf16[2,2,512,2048]{3,2,1,0:T(8,128)(2,1)} %norm.1.normed) | copy-start | bytes 25165828
  88.4 9.6 %copy-start.8 = (bf16[2,2,512,256]{3,2,1,0:T(8,128)(2,1)S(1)}, bf16[2,2,512,256]{3,2,1,0:T(8,128)(2,1)}, u32[]{:S(2)}) copy-start(bf16[2,2,512,256]{3,2,1,0:T(8,128)(2,1)} %get-tuple-element.33.state) | copy-start | bytes 3145732
  99.6 11.8 %collective-permute-start.12 = (bf16[2,128,256]{2,1,0:T(8,128)(2,1)S(1)}, bf16[2,128,256]{2,1,0:T(8,128)(2,1)S(1)}, u32[]{:S(2)}, u32[]{:S(2)}) collective-permute-start(bf16[2,128,256]{2,1,0:T(8,128)(2,1)S(1)} %get-tuple-element.42), channel_id=1, source_target_pairs={{0,4},{4,8},{8,12},{1,5},{5,9},{9,13},{2,6},{6,10},{10,14},{3,7},{... | collective-permute-start | bytes 393224 | tf_op jit(solution)/shard_map/ppermute | solution.py:28
  103.7 7.7 %collective-permute-start.13 = (bf16[2,128,256]{2,1,0:T(8,128)(2,1)S(1)}, bf16[2,128,256]{2,1,0:T(8,128)(2,1)S(1)}, u32[]{:S(2)}, u32[]{:S(2)}) collective-permute-start(bf16[2,128,256]{2,1,0:T(8,128)(2,1)S(1)} %get-tuple-element.43), channel_id=1, source_target_pairs={{4,0},{8,4},{12,8},{5,1},{9,5},{13,9},{6,2},{10,6},{14,10},{7,3},{... | collective-permute-start | bytes 393224 | tf_op jit(solution)/shard_map/ppermute | solution.py:28
  105.0 3.4 %copy-start.2 = (bf16[2,2,512,2048]{3,2,1,0:T(8,128)(2,1)S(1)}, bf16[2,2,512,2048]{3,2,1,0:T(8,128)(2,1)}, u32[]{:S(2)}) copy-start(bf16[2,2,512,2048]{3,2,1,0:T(8,128)(2,1)} %norm.1.normed) | copy-start | bytes 25165828
  113.1 9.4 %collective-permute-start.14 = (bf16[2,128,256]{2,1,0:T(8,128)(2,1)S(1)}, bf16[2,128,256]{2,1,0:T(8,128)(2,1)S(1)}, u32[]{:S(2)}, u32[]{:S(2)}) collective-permute-start(bf16[2,128,256]{2,1,0:T(8,128)(2,1)S(1)} %get-tuple-element.45), channel_id=1, source_target_pairs={{0,4},{4,8},{8,12},{1,5},{5,9},{9,13},{2,6},{6,10},{10,14},{3,7},{... | collective-permute-start | bytes 393224 | tf_op jit(solution)/shard_map/ppermute | solution.py:28
  117.6 12.2 %collective-permute-start.15 = (bf16[2,128,256]{2,1,0:T(8,128)(2,1)S(1)}, bf16[2,128,256]{2,1,0:T(8,128)(2,1)S(1)}, u32[]{:S(2)}, u32[]{:S(2)}) collective-permute-start(bf16[2,128,256]{2,1,0:T(8,128)(2,1)S(1)} %get-tuple-element.46), channel_id=1, source_target_pairs={{4,0},{8,4},{12,8},{5,1},{9,5},{13,9},{6,2},{10,6},{14,10},{7,3},{... | collective-permute-start | bytes 393224 | tf_op jit(solution)/shard_map/ppermute | solution.py:28
  131.3 1.3 copy-start.4
  139.0 6.6 %collective-permute-start.17 = (bf16[512,256]{1,0:T(8,128)(2,1)}, bf16[512,256]{1,0:T(8,128)(2,1)S(1)}, u32[]{:S(2)}, u32[]{:S(2)}) collective-permute-start(bf16[512,256]{1,0:T(8,128)(2,1)} %get-tuple-element.47.refs_0_), channel_id=1, source_target_pairs={{0,2},{1,3},{2,0},{3,1},{4,6},{5,7},{6,4},{7,5},{8,10},{9,11},{10,... | collective-permute-start | bytes 786440 | tf_op jit(solution)/shard_map/ppermute | solution.py:149
  139.9 9.4 %collective-permute-start.19 = (bf16[512,256]{1,0:T(8,128)(2,1)}, bf16[512,256]{1,0:T(8,128)(2,1)S(1)}, u32[]{:S(2)}, u32[]{:S(2)}) collective-permute-start(bf16[512,256]{1,0:T(8,128)(2,1)} %get-tuple-element.48), channel_id=1, source_target_pairs={{0,16},{16,0},{1,17},{17,1},{2,18},{18,2},{3,19},{19,3},{4,20},{20... | collective-permute-start | bytes 786440 | tf_op jit(solution)/shard_map/ppermute | solution.py:149
  141.4 7.9 %collective-permute-start.21 = (bf16[512,256]{1,0:T(8,128)(2,1)}, bf16[512,256]{1,0:T(8,128)(2,1)S(1)}, u32[]{:S(2)}, u32[]{:S(2)}) collective-permute-start(bf16[512,256]{1,0:T(8,128)(2,1)} %get-tuple-element.48), channel_id=1, source_target_pairs={{0,18},{1,19},{2,16},{3,17},{16,2},{17,3},{18,0},{19,1},{4,22},{5,... | collective-permute-start | bytes 786440 | tf_op jit(solution)/shard_map/ppermute | solution.py:157
  142.5 7.2 %collective-permute-start.16 = (bf16[512,256]{1,0:T(8,128)(2,1)}, bf16[512,256]{1,0:T(8,128)(2,1)S(1)}, u32[]{:S(2)}, u32[]{:S(2)}) collective-permute-start(bf16[512,256]{1,0:T(8,128)(2,1)} %get-tuple-element.47.refs_0_), channel_id=1, source_target_pairs={{0,1},{1,0},{2,3},{3,2},{4,5},{5,4},{6,7},{7,6},{8,9},{9,8},{10,11... | collective-permute-start | bytes 786440 | tf_op jit(solution)/shard_map/ppermute | solution.py:149
  145.6 4.1 %collective-permute-start.18 = (bf16[512,256]{1,0:T(8,128)(2,1)S(1)}, bf16[512,256]{1,0:T(8,128)(2,1)S(1)}, u32[]{:S(2)}, u32[]{:S(2)}) collective-permute-start(bf16[512,256]{1,0:T(8,128)(2,1)S(1)} %collective-permute-done.17.refs_2_), channel_id=1, source_target_pairs={{0,1},{1,0},{2,3},{3,2},{4,5},{5,4},{6,7},{7,6},{8,9},{9,8},{10,11... | collective-permute-start | bytes 786440 | tf_op jit(solution)/shard_map/ppermute | solution.py:149
  149.3 1.5 collective-permute-start.20
  149.3 2.2 %collective-permute-start.22 = (bf16[512,256]{1,0:T(8,128)(2,1)S(1)}, bf16[512,256]{1,0:T(8,128)(2,1)S(1)}, u32[]{:S(2)}, u32[]{:S(2)}) collective-permute-start(bf16[512,256]{1,0:T(8,128)(2,1)S(1)} %collective-permute-done.21.refs_6_), channel_id=1, source_target_pairs={{0,1},{1,0},{2,3},{3,2},{4,5},{5,4},{6,7},{7,6},{8,9},{9,8},{10,11... | collective-permute-start | bytes 786440 | tf_op jit(solution)/shard_map/ppermute | solution.py:149
  150.8 0.7 copy-start.10
  151.5 0.7 copy-start.12
  157.5 1.6 copy-start.7
  159.1 0.9 copy-start.9
  160.0 0.9 copy-start.11
  161.0 0.9 copy-start.13
Sparse Core Ops, SparseCore 0:
  9.2 66.2 all-gather.6
  77.0 28.9 all-gather.10
  107.6 49.8 all-gather.8

commit v3 on v0

--- a/solution.py
+++ b/solution.py
@@ -1,7 +1,15 @@
+import functools
+
 import jax
 import jax.numpy as jnp
 from jax import lax
+from jax.experimental import pallas as pl
+from jax.experimental.pallas import tpu as pltpu
 from jax.sharding import PartitionSpec as P
+
+VMEM_LIMIT = 40 * 1024 * 1024
+WIDE = 56 * 1024 * 1024
+SMALL = pl.CostEstimate(flops=1, bytes_accessed=1, transcendentals=0)
 
 
 def partner(block, axis, apart):
@@ -136,6 +144,487 @@
     return total.astype(jnp.bfloat16)
 
 
+def flip(block, axis, bit):
+    count = lax.axis_size(axis)
+    return lax.ppermute(block, axis, [(i, i ^ bit) for i in range(count)])
+
+
+def across(block, bit):
+    groups, count = lax.axis_size("grp"), lax.axis_size("ch")
+    pairs = [
+        (g * count + k, (g ^ 1) * count + (k ^ bit)) for g in range(groups) for k in range(count)
+    ]
+    return lax.ppermute(block, ("grp", "ch"), pairs)
+
+
+def params(*semantics, limit=None):
+    return pltpu.CompilerParams(
+        dimension_semantics=semantics, vmem_limit_bytes=limit or VMEM_LIMIT
+    )
+
+
+def gathered(block):
+    two = flip(block, "ctx", 2)
+    return [block, flip(block, "ctx", 1), two, flip(two, "ctx", 1)]
+
+
+def after(value, *others):
+    return lax.optimization_barrier((value,) + others)[0]
+
+
+def norm_kernel(layout, place, gain, *refs):
+    out = refs[-1]
+    for s, strand in enumerate(layout):
+        for g, group in enumerate(strand):
+            blocks = [refs[n][...] if at is None else refs[n][at] for n, at in group]
+            width = blocks[0].shape[-1]
+            model = width * len(blocks)
+            floats = [p.astype(jnp.float32) for p in blocks]
+            total = sum(f * f for f in floats)
+            scale = lax.rsqrt(jnp.sum(total, axis=-1, keepdims=True) / model + 1e-05)
+            for j, f in enumerate(floats):
+                lanes = pl.ds(pl.multiple_of((place[0] ^ j) * width, width), width)
+                out[s, g, :, lanes] = (f * scale * gain[:, lanes]).astype(jnp.bfloat16)
+
+
+def norm_all(place, gain, layout, arrays):
+    strands, groups, parts = len(layout), len(layout[0]), len(layout[0][0])
+    rows, width = arrays[0].shape[-2:]
+    tile = 128
+
+    def spec(array):
+        if array.ndim == 2:
+            return pl.BlockSpec((tile, width), lambda i, p: (i, 0))
+        return pl.BlockSpec((strands, tile, width), lambda i, p: (0, i, 0))
+
+    shape = (strands, groups, rows, width * parts)
+    return pl.pallas_call(
+        functools.partial(norm_kernel, layout),
+        grid_spec=pltpu.PrefetchScalarGridSpec(
+            num_scalar_prefetch=1,
+            grid=(rows // tile,),
+            in_specs=[pl.BlockSpec((1, width * parts), lambda i, p: (0, 0))]
+            + [spec(v) for v in arrays],
+            out_specs=pl.BlockSpec(
+                (strands, groups, tile, width * parts), lambda i, p: (0, 0, i, 0)
+            ),
+        ),
+        out_shape=jax.ShapeDtypeStruct(shape, jnp.bfloat16),
+        compiler_params=params("arbitrary"),
+        cost_estimate=SMALL,
+        name="norm",
+    )(place, gain.reshape(1, -1), *arrays)
+
+
+CUTS = 4
+
+
+def fetch(normed, weight, count, order, held, kept, x_sems, w_sems):
+    depth = weight.shape[2]
+    for b in range(count):
+        for z in range(weight.shape[0]):
+            span = pl.ds(z * depth, depth)
+            pltpu.make_async_copy(
+                weight.at[z, b], kept.at[b, span], w_sems.at[b, z]
+            ).start()
+    groups, rows = normed.shape[1:3]
+    part = rows // CUTS
+    for s, g in order:
+        at = s * groups + g
+        for c in range(CUTS):
+            span = pl.ds(c * part, part)
+            pltpu.make_async_copy(
+                normed.at[s, g, span], held.at[at, span], x_sems.at[at, c]
+            ).start()
+
+
+def wait_weight(weight, count, kept, w_sems):
+    depth = weight.shape[2]
+    for b in range(count):
+        for z in range(weight.shape[0]):
+            span = pl.ds(z * depth, depth)
+            pltpu.make_async_copy(weight.at[z, 0], kept.at[b, span], w_sems.at[b, z]).wait()
+
+
+def wait_rows(normed, at, held, x_sems):
+    part = normed.shape[2] // CUTS
+    for c in range(CUTS):
+        span = pl.ds(c * part, part)
+        pltpu.make_async_copy(normed.at[0, 0, span], held.at[at, span], x_sems.at[at, c]).wait()
+
+
+def product(value, weight):
+    return jnp.dot(value[...], weight[...], preferred_element_type=jnp.float32)
+
+
+def fetch_scratch(normed, weight, count):
+    strands, groups, rows, model = normed.shape
+    blocks, _, depth, width = weight.shape
+    return [
+        pltpu.VMEM((strands * groups, rows, model), jnp.bfloat16),
+        pltpu.VMEM((count, blocks * depth, width), jnp.bfloat16),
+        pltpu.SemaphoreType.DMA((strands * groups, CUTS)),
+        pltpu.SemaphoreType.DMA((count, blocks)),
+    ]
+
+
+def toeplitz_of(pattern, block):
+    width = pattern.shape[-1]
+    spread = jnp.broadcast_to(pattern, (block, width))
+    return pltpu.roll(spread, 0, 1, stride=1, stride_axis=0).astype(jnp.bfloat16)
+
+
+def tables_kernel(patterns, tables):
+    block = tables.shape[-2]
+    for k in range(tables.shape[0]):
+        for h in range(tables.shape[2]):
+            tables[k, 0, h] = toeplitz_of(patterns[k, 0, h], block)
+
+
+def tables_of(patterns):
+    sections, strands, heads, _, width = patterns.shape
+    block = width // 2
+    return pl.pallas_call(
+        tables_kernel,
+        grid=(strands,),
+        in_specs=[pl.BlockSpec((sections, 1, heads, 1, width), lambda s: (0, s, 0, 0, 0))],
+        out_specs=pl.BlockSpec((sections, 1, heads, block, width), lambda s: (0, s, 0, 0, 0)),
+        out_shape=jax.ShapeDtypeStruct((sections, strands, heads, block, width), jnp.bfloat16),
+        compiler_params=params("arbitrary"),
+        cost_estimate=SMALL,
+        name="tables",
+    )(patterns)
+
+
+def gated_block(k, s, n, blocks, window, table, mask, gate, gate_at=None):
+    block = table.shape[-2]
+    place = jnp.where(s == 0, n, blocks - 1 - n)
+    at = pl.multiple_of(place * block, block)
+    heads = table.shape[2]
+    head = gate.shape[-1] // heads
+    gate_at = at if gate_at is None else gate_at
+    out = []
+    for h in range(heads):
+        lanes = slice(h * head, (h + 1) * head)
+        conv = jnp.dot(
+            table[k, 0, h] * mask[0, 0, place],
+            window[pl.ds(at, 2 * block), lanes],
+            preferred_element_type=jnp.float32,
+        )
+        out.append((gate[pl.ds(gate_at, block), lanes] * conv).astype(jnp.bfloat16))
+    return at, jnp.concatenate(out, axis=-1)
+
+
+def shifted_at(at, s, block):
+    return pl.multiple_of(at + jnp.where(s == 0, block, 0), block)
+
+
+def early_kernel(normed, weight, table, mask, *refs):
+    s, g = pl.program_id(0), pl.program_id(1)
+    states, gates_out, rim_fwd, rim_rev = refs[:4]
+    held, kept, x_sems, w_sems, *extended = refs[4:8] + refs[8:10]
+    gates = refs[10:]
+    groups, rows = normed.shape[1:3]
+    block = table.shape[-2]
+    blocks = rows // block
+
+    @pl.when((s == 0) & (g == 0))
+    def _():
+        order = [(i, j) for i in range(normed.shape[0]) for j in range(groups)]
+        fetch(normed, weight, 3, order, held, kept, x_sems, w_sems)
+        wait_weight(weight, 3, kept, w_sems)
+
+    def row_of(n):
+        return pl.multiple_of(jnp.where(s == 0, n, blocks - 1 - n) * block, block)
+
+    def keep_rim(k, value):
+        @pl.when(s == 0)
+        def _():
+            rim_fwd[k, g] = value
+
+        @pl.when(s == 1)
+        def _():
+            rim_rev[k, g] = value
+
+    at = s * groups + g
+    wait_rows(normed, at, held, x_sems)
+    extended[0][pl.ds(shifted_at(0, s, block), rows)] = product(
+        held.at[at], kept.at[0]
+    ).astype(jnp.bfloat16)
+    states[0, 0, 0] = extended[0][pl.ds(shifted_at(row_of(0), s, block), block)]
+    keep_rim(0, extended[0][pl.ds(shifted_at(row_of(blocks - 1), s, block), block)])
+    for k in range(2):
+        gates[k][...] = product(held.at[at], kept.at[k + 1])
+    gates_out[0, 0, 0] = gates[0][pl.ds(row_of(0), block)]
+    for n in range(2):
+        gates_out[0, 0, 1 + n] = gates[1][pl.ds(row_of(n), block)]
+    for n in range(1, blocks):
+        row, value = gated_block(0, s, n, blocks, extended[0], table, mask, gates[0])
+        extended[1][pl.ds(shifted_at(row, s, block), block)] = value
+        if n == 1:
+            states[0, 0, 1] = value
+    keep_rim(1, value)
+    for n in range(2, blocks):
+        row, value = gated_block(1, s, n, blocks, extended[1], table, mask, gates[1])
+        states[0, 0, n] = value
+    keep_rim(2, value)
+
+
+def early_sections(normed, weight, tables, mask):
+    strands, groups, rows, _ = normed.shape
+    width = weight.shape[-1]
+    sections, _, heads, block, _ = tables.shape
+    blocks = rows // block
+    rim = jax.ShapeDtypeStruct((sections, groups, block, width), jnp.bfloat16)
+    rim_spec = pl.BlockSpec(rim.shape, lambda s, g: (0, 0, 0, 0))
+    return pl.pallas_call(
+        early_kernel,
+        grid=(strands, groups),
+        in_specs=[pl.BlockSpec(memory_space=pltpu.HBM)] * 2
+        + [
+            pl.BlockSpec((sections, 1, heads, block, 2 * block), lambda s, g: (0, s, 0, 0, 0)),
+            pl.BlockSpec((1, 1, blocks, block, 2 * block), lambda s, g: (s, g, 0, 0, 0)),
+        ],
+        out_specs=[
+            pl.BlockSpec((1, 1, blocks, block, width), lambda s, g: (s, g, 0, 0, 0)),
+            pl.BlockSpec((1, 1, 3, block, width), lambda s, g: (s, g, 0, 0, 0)),
+            rim_spec,
+            rim_spec,
+        ],
+        out_shape=[
+            jax.ShapeDtypeStruct((strands, groups, blocks, block, width), jnp.bfloat16),
+            jax.ShapeDtypeStruct((strands, groups, 3, block, width), jnp.float32),
+            rim,
+            rim,
+        ],
+        scratch_shapes=fetch_scratch(normed, weight, 3)
+        + [pltpu.VMEM((rows + block, width), jnp.bfloat16)] * 2
+        + [pltpu.VMEM((rows, width), jnp.float32)] * 2,
+        compiler_params=params("arbitrary", "arbitrary", limit=WIDE),
+        cost_estimate=SMALL,
+        name="early_sections",
+    )(normed, weight, tables, mask)
+
+
+def late_kernel(g, normed, weight, states, gates, table, mask, *refs):
+    rims, out = refs[:2], refs[2]
+    held, kept, x_sems, w_sems, last_gate, *extended = refs[3:]
+    s = pl.program_id(0)
+    groups, rows = normed.shape[1:3]
+    block = table.shape[-2]
+    blocks = rows // block
+
+    @pl.when(s == 0)
+    def _():
+        order = [(i, g) for i in range(normed.shape[0])]
+        fetch(normed, weight, 1, order, held, kept, x_sems, w_sems)
+
+    def put(k, n, value):
+        at = jnp.where(s == 0, n, blocks - 1 - n) * block
+        extended[k][pl.ds(shifted_at(at, s, block), block)] = value
+
+    for k in range(3):
+
+        @pl.when(s == 0)
+        def _():
+            extended[k][:block] = rims[0][k, 0]
+
+        @pl.when(s == 1)
+        def _():
+            extended[k][rows:] = rims[1][k, 0]
+
+    put(0, 0, states[0, 0, 0])
+    put(1, 1, states[0, 0, 1])
+    for n in range(2, blocks):
+        put(2, n, states[0, 0, n])
+    for k in range(2):
+        for n in range(k + 1):
+            gate = gates.at[0, 0, k + n]
+            _, value = gated_block(k, s, n, blocks, extended[k], table, mask, gate, 0)
+            put(k + 1, n, value)
+
+    @pl.when(s == 0)
+    def _():
+        wait_weight(weight, 1, kept, w_sems)
+
+    at = s * groups + g
+    wait_rows(normed, at, held, x_sems)
+    last_gate[...] = product(held.at[at], kept.at[0])
+    for n in range(blocks):
+        row, value = gated_block(2, s, n, blocks, extended[2], table, mask, last_gate)
+        span = pl.ds(row, block)
+        before = jnp.where(s == 0, 0.0, out[span].astype(jnp.float32))
+        out[span] = (before + value.astype(jnp.float32)).astype(jnp.bfloat16)
+
+
+def late_sections(normed, weight, states, gates, tables, mask, rims, g):
+    strands, groups, rows, _ = normed.shape
+    blocks, block, width = states.shape[2:]
+    sections, _, heads = tables.shape[:3]
+    return pl.pallas_call(
+        functools.partial(late_kernel, g),
+        grid=(strands,),
+        in_specs=[pl.BlockSpec(memory_space=pltpu.HBM)] * 2
+        + [
+            pl.BlockSpec((1, 1, blocks, block, width), lambda s: (s, g, 0, 0, 0)),
+            pl.BlockSpec((1, 1, 3, block, width), lambda s: (s, g, 0, 0, 0)),
+            pl.BlockSpec((sections, 1, heads, block, 2 * block), lambda s: (0, s, 0, 0, 0)),
+            pl.BlockSpec((1, 1, blocks, block, 2 * block), lambda s: (s, g, 0, 0, 0)),
+        ]
+        + [pl.BlockSpec((sections, 1, block, width), lambda s: (0, g, 0, 0)) for _ in rims],
+        out_specs=pl.BlockSpec((rows, width), lambda s: (0, 0)),
+        out_shape=jax.ShapeDtypeStruct((rows, width), jnp.bfloat16),
+        scratch_shapes=fetch_scratch(normed, weight, 1)
+        + [pltpu.VMEM((rows, width), jnp.float32)]
+        + [pltpu.VMEM((rows + block, width), jnp.bfloat16)] * 3,
+        compiler_params=params("arbitrary", limit=WIDE),
+        cost_estimate=SMALL,
+        name="late_sections",
+    )(normed, weight, states, gates, tables, mask, *rims)
+
+
+def out_kernel(parts, spots, *refs):
+    weights, pieces = refs[: 2 * parts], refs[2 * parts : -2]
+    out, held = refs[-2:]
+
+    @pl.when(pl.program_id(0) == 0)
+    def _():
+        for half in range(2):
+            for i in range(parts):
+                held[half, spots[1] ^ i] = weights[half * parts + i][...]
+
+    total = None
+    for half in range(2):
+        for j in range(parts):
+            piece = pieces[half * parts + j]
+            term = jnp.dot(
+                piece[...], held[half, spots[0] ^ j], preferred_element_type=jnp.float32
+            )
+            total = term if total is None else total + term
+    out[...] = total.astype(jnp.bfloat16)
+
+
+def project_out(spots, near, far, pieces):
+    parts = len(near)
+    rows, depth = pieces[0].shape
+    width = near[0].shape[-1]
+    tile = rows // 2
+    return pl.pallas_call(
+        functools.partial(out_kernel, parts),
+        grid_spec=pltpu.PrefetchScalarGridSpec(
+            num_scalar_prefetch=1,
+            grid=(rows // tile,),
+            in_specs=[pl.BlockSpec(w.shape, lambda i, p: (0, 0)) for w in near + far]
+            + [pl.BlockSpec((tile, depth), lambda i, p: (i, 0)) for _ in pieces],
+            out_specs=pl.BlockSpec((tile, width), lambda i, p: (i, 0)),
+            scratch_shapes=[pltpu.VMEM((2, parts, depth, width), jnp.bfloat16)],
+        ),
+        out_shape=jax.ShapeDtypeStruct((rows, width), jnp.bfloat16),
+        compiler_params=params("arbitrary"),
+        cost_estimate=SMALL,
+        name="out",
+    )(spots, *near, *far, *pieces)
+
+
+def conv_patterns(taps):
+    zero = jnp.zeros_like(taps)
+    forward = jnp.concatenate([zero[..., :1], taps[..., ::-1], zero[..., 1:]], axis=-1)
+    reverse = jnp.concatenate([taps, zero], axis=-1)
+    return jnp.stack([forward, reverse], axis=1)[:, :, :, None, :]
+
+
+def doc_masks(offsets, start, rows, block, seq_len):
+    positions = start - block + jnp.arange(rows + 2 * block, dtype=jnp.int32)
+    docs = jax.vmap(lambda o: doc_of(positions, o, seq_len))(offsets)
+    groups, blocks = offsets.shape[0], rows // block
+    tiles = docs.reshape(groups, blocks + 2, block)
+    target = tiles[:, 1:-1]
+    before = jnp.concatenate([tiles[:, :-2], target], axis=-1)
+    after = jnp.concatenate([target, tiles[:, 2:]], axis=-1)
+    window = jnp.stack([before, after])
+    return (target[None, :, :, :, None] == window[:, :, :, None, :]).astype(jnp.bfloat16)
+
+
+def paired(
+    fwd_hidden,
+    rev_hidden,
+    bases,
+    complement,
+    offsets,
+    base_embed,
+    norm_gain,
+    in_weight,
+    filters,
+    out_weight,
+):
+    rows, width = fwd_hidden.shape
+    groups, ctx_count, parts = (lax.axis_size(a) for a in ("grp", "ctx", "ch"))
+    mine, here, place = (lax.axis_index(a) for a in ("grp", "ctx", "ch"))
+    sections, heads, block = filters.shape
+    seq_len = rows * ctx_count
+    half = width // groups
+
+    columns = lax.dynamic_slice_in_dim(in_weight, mine * half, half, axis=2)
+    early = lax.all_gather(columns[:sections], "ctx", axis=0)
+
+    letters = base_embed.shape[0]
+    alphabet = jnp.arange(letters, dtype=jnp.int32)
+    onehot = (bases[:, None] == alphabet[None, :]).astype(jnp.bfloat16)
+    swap_table = (complement[:, None] == alphabet[None, :]).astype(jnp.bfloat16)
+    swapped = jnp.dot(swap_table, base_embed, preferred_element_type=jnp.float32)
+    inputs = []
+    for hidden, table in ((fwd_hidden, base_embed), (rev_hidden, swapped.astype(jnp.bfloat16))):
+        embed = jnp.dot(onehot, table, preferred_element_type=jnp.float32)
+        inputs.append((hidden.astype(jnp.float32) + embed).astype(jnp.bfloat16))
+    own = jnp.stack(inputs)
+    x = flip(own, "ch", 2)
+    y = flip(own, "grp", 1)
+    core = flip(own, "ch", 1)
+    x, y, core = lax.optimization_barrier((x, y, core))
+    xy = [flip(x[0], "grp", 1), flip(y[1], "ch", 2)]
+    arrays = [own, core, x, flip(x, "ch", 1), y, flip(y, "ch", 1)]
+    arrays += [xy[0], flip(xy[0], "ch", 1), xy[1], flip(xy[1], "ch", 1)]
+    layout = [
+        [
+            [(n, s) for n in range(1, 5)],
+            [(5, s), (6, s), (7 + 2 * s, None), (8 + 2 * s, None)],
+        ]
+        for s in range(2)
+    ]
+    layout = [[[(n - 1, at) for n, at in group] for group in strand] for strand in layout]
+    spots = jnp.stack([place, here]).astype(jnp.int32)
+    normed = norm_all(spots, norm_gain, layout, arrays)
+    late = lax.all_gather(after(columns[sections:], x), "ctx", axis=0)
+
+    both_offsets = jnp.stack([offsets, flip(offsets, "grp", 1)])
+    mask = doc_masks(both_offsets, here * rows, rows, block, seq_len)
+    own_heads = heads // groups
+    taps = lax.dynamic_slice_in_dim(filters, mine * own_heads, own_heads, axis=1)
+    patterns = conv_patterns(taps.astype(jnp.bfloat16).astype(jnp.float32))
+
+    tables = tables_of(patterns)
+    out_near = lax.dynamic_slice_in_dim(out_weight, mine * half, half, axis=0)
+    out_far = lax.dynamic_slice_in_dim(out_weight, (1 - mine) * half, half, axis=0)
+    early, normed, mask, tables, out_near = lax.optimization_barrier(
+        (early, normed, mask, tables, out_near)
+    )
+    one, two = flip(out_near, "ctx", 1), flip(out_near, "ctx", 2)
+    states, gates, rim_fwd, rim_rev = early_sections(normed, early, tables, mask)
+    rims = shifted(rim_fwd, "ctx", 1), shifted(rim_rev, "ctx", -1)
+    one, two, states = lax.optimization_barrier((one, two, states))
+    near = [out_near, one, two, flip(two, "ctx", 1)]
+    far = [out_far] + [flip(w, "grp", 1) for w in near[1:]]
+    work = normed, late, states, gates, tables, mask, rims
+    mixed_far = late_sections(*work, 1)
+    mixed_near = late_sections(*work, 0)
+    from_y = flip(mixed_far, "grp", 1)
+    from_xy = across(mixed_far, 2)
+    from_x = flip(mixed_near, "ch", 2)
+    near_pieces = [mixed_near, flip(mixed_near, "ch", 1), from_x, flip(from_x, "ch", 1)]
+    far_pieces = [from_y, flip(from_y, "ch", 1), from_xy, flip(from_xy, "ch", 1)]
+    return project_out(spots, near, far, near_pieces + far_pieces)
+
+
 def solution(mesh):
     in_specs = (
         P(("grp", "ctx"), "ch"),
@@ -150,4 +639,6 @@
         P("ctx", "ch"),
     )
     out_specs = P(("grp", "ctx"), "ch")
-    return jax.shard_map(local, mesh=mesh, in_specs=in_specs, out_specs=out_specs, check_vma=False)
+    sizes = [mesh.shape[a] for a in ("grp", "ctx", "ch")]
+    body = paired if sizes[0] == 2 and sizes[1] == sizes[2] == 4 else local
+    return jax.shard_map(body, mesh=mesh, in_specs=in_specs, out_specs=out_specs, check_vma=False)

time: 392 us -> 154 us (0.39)
  waiting for transfers between devices: 248 us -> 52.8 us
  Pallas kernels: 0 us -> 44.8 us
  local copies, waits for them, and re-layouts: 48.7 us -> 10.8 us
  matrix products: 36.2 us -> 2.41 us
  other arithmetic: 20.5 us -> 3.53 us
    all_gather x5 -> x2, waiting for transfers between devices: 188 us -> 11.4 us  [the longest x1 6.22 us: paired(): early = lax.all_gather(columns[:sections], 'ctx', axis=0)]
    pallas_call x0 -> x6, Pallas kernels: none -> 44.8 us  [the longest x1 17.8 us: early_sections(): pl.pallas_call(early_kernel, grid=(strands, groups), in_specs=[pl.BlockSp...]
    dot_general x11 -> x2, matrix products: 36.2 us -> 2.41 us  [paired(): embed = jnp.dot(onehot, table, preferred_element_type=jnp.float32)]
    ppermute x4 -> x23, waiting for transfers between devices: 51.2 us -> 36.5 us  [the longest x22 36.5 us: flip(): return lax.ppermute(block, axis, [(i, i ^ bit) for i in range(count)])]
    ppermute x4 -> x23, starting transfers between devices: 5.87 us -> 19.4 us  [the longest x22 17.9 us: flip(): return lax.ppermute(block, axis, [(i, i ^ bit) for i in range(count)])]
    ppermute x6 -> x2, starting transfers between devices: 17.1 us -> 5.77 us  [shifted(): return lax.ppermute(value, axis, pairs)]
    concatenate x14 -> x2, local copies, waits for them, and re-layouts: 10 us -> 0.08 us  [conv_patterns(): jnp.concatenate([zero[..., :1], taps[..., ::-1], zero[..., 1:]], axis=-1)]
    convert_element_type x9 -> x2, other arithmetic: 11.1 us -> 1.93 us  [the longest x1 1.23 us: doc_masks(): (target[None, :, :, :, None] == window[:, :, :, None, :]).astype(jnp.bflo...]
  transfers between devices with their start and end apart: 15 -> 27, of which waited for: 8 -> 11; matrix products, arithmetic and copies ran while one was open for 24% -> 8% of each run, Pallas kernels for 0% -> 27%
where the time goes in v3:
time: 154 us; the launch traced here: 153 us
  waiting for transfers between devices  52.8 us (34%)
  Pallas kernels  44.8 us (29%)
  starting transfers between devices  25.2 us (16%)
  between operations  13.7 us (9%)
  local copies, waits for them, and re-layouts  10.8 us (7%)
  other arithmetic  3.53 us (2%)
  matrix products  2.41 us (2%)
    ppermute x22, waiting for transfers between devices, flip(): return lax.ppermute(block, axis, [(i, i ^ bit) for i in range(count)])  36.5 us
    ppermute x22, starting transfers between devices, flip(): return lax.ppermute(block, axis, [(i, i ^ bit) for i in range(count)])  17.9 us
    pallas_call x1, Pallas kernels, early_sections(): pl.pallas_call(early_kernel, grid=(strands, groups), in_specs=[pl.BlockSp...  17.8 us
    pallas_call x2, Pallas kernels, late_sections(): pl.pallas_call(functools.partial(late_kernel, g), grid=(strands,), in_spe...  14.1 us
    pallas_call x1, Pallas kernels, norm_all(): pl.pallas_call(functools.partial(norm_kernel, layout), grid_spec=pltpu.Pr...  8.68 us
    all_gather x1, waiting for transfers between devices, paired(): early = lax.all_gather(columns[:sections], 'ctx', axis=0)  6.22 us
    ppermute x2, starting transfers between devices, shifted(): return lax.ppermute(value, axis, pairs)  5.77 us
    all_gather x1, waiting for transfers between devices, paired(): late = lax.all_gather(after(columns[sections:], x), 'ctx', axis=0)  5.19 us
  transfers between devices with their start and end apart: 27, of which 11 were waited for; matrix products, arithmetic and copies ran while one was open for 8% of the time, Pallas kernels for 27%

profile of v3, /device:TPU:0, one launch (start us, length us, event | category | flops | bytes accessed | tf_op | source)
XLA Modules:
  0.0 153.2 jit_solution(15316420371938187244)
XLA Ops:
  6.6 1.5 copy-done
  8.1 1.0 constant_dynamic-slice_fusion
  9.2 1.2 fusion.3
  10.4 1.3 fusion.2
  11.6 1.3 pad_maximum_fusion.refs_0_
  12.9 3.0 %collective-permute-start = (bf16[2,512,512]{2,1,0:T(8,128)(2,1)S(1)}, bf16[2,512,512]{2,1,0:T(8,128)(2,1)}, u32[]{:S(2)}, u32[]{:S(2)}) collective-permute-start(bf16[2,512,512]{2,1,0:T(8,128)(2,1)S(1)} %pad_maximum_fusion.refs_0_), channel_id=1, source_target_pairs={{0,2},{1,3},{2,0},{3,1},{4,6},{5,7},{6,4},{7,5},{8,10},{9,11},{10,... | collective-permute-start | bytes 3145736 | tf_op jit(solution)/shard_map/ppermute | solution.py:149
  15.9 1.5 collective-permute-start.1
  17.4 0.5 collective-permute-start.9
  18.0 0.7 fusion.9
  19.0 0.7 constant_dynamic-slice_fusion.3
  19.7 1.8 %constant_dynamic-slice_fusion.1 = (bf16[256,512]{1,0:T(8,128)(2,1)S(1)}, bf16[256,512]{1,0:T(8,128)(2,1)}) fusion(bf16[512,512]{1,0:T(8,128)(2,1)} %param.19, s32[]{:T(128)S(6)} %select_n.18, s32[]{:T(128)S(6)} %select_n.15), kind=kLoop, calls=%fused_computation.32 | loop fusion | bytes 1048584 | tf_op jit(solution)/shard_map/dynamic_slice | solution.py:607
  21.6 0.4 tables.1.table
  22.1 0.9 copy-done.1
  22.9 17.7 %collective-permute-done.9 = s32[16]{0:T(128)S(1)} collective-permute-done((s32[16]{0:T(128)S(1)}, s32[16]{0:T(128)S(1)}, u32[]{:S(2)}, u32[]{:S(2)}) %collective-permute-start.9) | collective-permute-done | bytes 96 | tf_op jit(solution)/shard_map/ppermute | solution.py:149
  40.7 1.9 %slice_bitcast_fusion.1 = bf16[512,512]{1,0:T(8,128)(2,1)} fusion(bf16[2,512,512]{2,1,0:T(8,128)(2,1)} %collective-permute-done.refs_2_), kind=kLoop, calls=%fused_computation.10 | loop fusion | bytes 1048576 | tf_op jit(solution)/shard_map/squeeze | solution.py:584
  42.6 1.5 collective-permute-start.5
  44.1 1.9 %slice_bitcast_fusion = bf16[512,512]{1,0:T(8,128)(2,1)} fusion(bf16[2,512,512]{2,1,0:T(8,128)(2,1)} %collective-permute-done.1.refs_4_), kind=kLoop, calls=%fused_computation.9 | loop fusion | bytes 1048576 | tf_op jit(solution)/shard_map/squeeze | solution.py:584
  45.9 0.5 collective-permute-start.7
  46.5 0.1 convert_reduce_fusion
  46.7 0.5 collective-permute-start.4
  47.2 8.1 %collective-permute-done.5.refs_6_ = bf16[512,512]{1,0:T(8,128)(2,1)} collective-permute-done((bf16[512,512]{1,0:T(8,128)(2,1)}, bf16[512,512]{1,0:T(8,128)(2,1)}, u32[]{:S(2)}, u32[]{:S(2)}) %collective-permute-start.5) | collective-permute-done | bytes 524320 | tf_op jit(solution)/shard_map/ppermute | solution.py:149
  55.3 3.1 %collective-permute-done.7.refs_8_ = bf16[512,512]{1,0:T(8,128)(2,1)} collective-permute-done((bf16[512,512]{1,0:T(8,128)(2,1)}, bf16[512,512]{1,0:T(8,128)(2,1)}, u32[]{:S(2)}, u32[]{:S(2)}) %collective-permute-start.7) | collective-permute-done | bytes 524320 | tf_op jit(solution)/shard_map/ppermute | solution.py:149
  58.5 1.2 compare_convert_fusion.mask
  59.7 0.9 collective-permute-done.8.refs_9_
  60.6 8.7 %norm.1.normed = bf16[2,2,512,2048]{3,2,1,0:T(8,128)(2,1)} custom-call(s32[2]{0:T(128)S(1)} %pad_add_fusion.2.place.spots, f32[1,2048]{1,0:T(1,128)S(1)} %bitcast.28, bf16[2,512,512]{2,1,0:T(8,128)(2,1)S(1)} %pad_maximum_fusion.refs_0_, bf16[2,512,512]{2,1,0:T(8,128)(2,1)} %collective-permute-done.2.refs_1_, ...), custom_call_target="tpu_custom_call" | custom-call | flops 1 | bytes 1 | tf_op jit(solution)/shard_map/norm/pallas_call | solution.py:201
  69.3 6.2 %all-gather.5.cloned.1.call-done = bf16[12,512,256]{2,1,0:T(8,128)(2,1)} async-done(((bf16[3,512,256]{2,1,0:T(8,128)(2,1)}), bf16[12,512,256]{2,1,0:T(8,128)(2,1)}) %all-gather.5.cloned.1.call-update) | async-done | bytes 3145744 | tf_op jit(solution)/shard_map/all_gather | solution.py:568
  75.5 1.3 collective-permute-start.11
  76.8 17.8 %early_sections.1 = (bf16[2,2,4,128,256]{4,3,2,1,0:T(8,128)(2,1)}, f32[2,2,3,128,256]{4,3,2,1,0:T(8,128)}, bf16[3,2,128,256]{3,2,1,0:T(8,128)(2,1)}, bf16[3,2,128,256]{3,2,1,0:T(8,128)(2,1)}) custom-call(bf16[2,2,512,2048]{3,2,1,0:T(8,128)(2,1)} %norm.1.normed, bf16[4,3,512,256]{3,2,1,0:T(8,128)(2,1)} %bitcast.31, bf16[3,2,2,128,256]{4,3,2,1,0:T(8,128)(2,1)} %copy-done.1, ...), custom_call_target="tpu_custom_call" | custom-call | flops 1 | bytes 1 | tf_op jit(solution)/shard_map/early_sections/pallas_call | solution.py:380
  94.6 4.5 %collective-permute-start.16 = (bf16[3,2,128,256]{3,2,1,0:T(8,128)(2,1)}, bf16[3,2,128,256]{3,2,1,0:T(8,128)(2,1)}, u32[]{:S(2)}, u32[]{:S(2)}) collective-permute-start(bf16[3,2,128,256]{3,2,1,0:T(8,128)(2,1)} %get-tuple-element.35), channel_id=1, source_target_pairs={{0,4},{4,8},{8,12},{1,5},{5,9},{9,13},{2,6},{6,10},{10,14},{3,7},{... | collective-permute-start | bytes 1179656 | tf_op jit(solution)/shard_map/ppermute | solution.py:28
  99.1 1.3 collective-permute-start.17
  100.4 2.7 %collective-permute-start.12 = (bf16[256,512]{1,0:T(8,128)(2,1)S(1)}, bf16[256,512]{1,0:T(8,128)(2,1)S(1)}, u32[]{:S(2)}, u32[]{:S(2)}) collective-permute-start(bf16[256,512]{1,0:T(8,128)(2,1)S(1)} %collective-permute-done.11.refs_2_), channel_id=1, source_target_pairs={{0,4},{4,0},{8,12},{12,8},{1,5},{5,1},{9,13},{13,9},{2,6},{6,2},{1... | collective-permute-start | bytes 786440 | tf_op jit(solution)/shard_map/ppermute | solution.py:149
  103.1 1.5 collective-permute-start.14
  104.6 0.6 collective-permute-start.13
  105.1 5.2 %all-gather.7.cloned.1.call-done = bf16[4,512,256]{2,1,0:T(8,128)(2,1)} async-done(((bf16[1,512,256]{2,1,0:T(8,128)(2,1)}), bf16[4,512,256]{2,1,0:T(8,128)(2,1)}) %all-gather.7.cloned.1.call-update) | async-done | bytes 1048592 | tf_op jit(solution)/shard_map/all_gather | solution.py:597
  110.3 2.9 %collective-permute-done.16.refs_0_ = bf16[3,2,128,256]{3,2,1,0:T(8,128)(2,1)} collective-permute-done((bf16[3,2,128,256]{3,2,1,0:T(8,128)(2,1)}, bf16[3,2,128,256]{3,2,1,0:T(8,128)(2,1)}, u32[]{:S(2)}, u32[]{:S(2)}) %collective-permute-start.16) | collective-permute-done | bytes 393248 | tf_op jit(solution)/shard_map/ppermute | solution.py:28
  113.2 1.9 %collective-permute-done.17.refs_1_ = bf16[3,2,128,256]{3,2,1,0:T(8,128)(2,1)} collective-permute-done((bf16[3,2,128,256]{3,2,1,0:T(8,128)(2,1)}, bf16[3,2,128,256]{3,2,1,0:T(8,128)(2,1)}, u32[]{:S(2)}, u32[]{:S(2)}) %collective-permute-start.17) | collective-permute-done | bytes 393248 | tf_op jit(solution)/shard_map/ppermute | solution.py:28
  115.1 7.1 %late_sections.3 = bf16[512,256]{1,0:T(8,128)(2,1)} custom-call(bf16[2,2,512,2048]{3,2,1,0:T(8,128)(2,1)} %norm.1.normed, bf16[4,1,512,256]{3,2,1,0:T(8,128)(2,1)} %bitcast.29, bf16[2,2,4,128,256]{4,3,2,1,0:T(8,128)(2,1)} %get-tuple-element.33.states, f32[2,2,3,128,256]{4,3,2,1,0:T(8,128)} %get-tuple-element.34.gates, ...), custom_call_target="tpu_custom_call" | custom-call | flops 1 | bytes 1 | tf_op jit(solution)/shard_map/late_sections/pallas_call | solution.py:464
  122.2 1.5 %collective-permute-start.21 = (bf16[512,256]{1,0:T(8,128)(2,1)}, bf16[512,256]{1,0:T(8,128)(2,1)S(1)}, u32[]{:S(2)}, u32[]{:S(2)}) collective-permute-start(bf16[512,256]{1,0:T(8,128)(2,1)} %late_sections.3), channel_id=1, source_target_pairs={{0,16},{16,0},{1,17},{17,1},{2,18},{18,2},{3,19},{19,3},{4,20},{20... | collective-permute-start | bytes 786440 | tf_op jit(solution)/shard_map/ppermute | solution.py:149
  123.7 1.5 collective-permute-start.23
  125.2 7.1 %late_sections.2.refs_8_ = bf16[512,256]{1,0:T(8,128)(2,1)} custom-call(bf16[2,2,512,2048]{3,2,1,0:T(8,128)(2,1)} %norm.1.normed, bf16[4,1,512,256]{3,2,1,0:T(8,128)(2,1)} %bitcast.30, bf16[2,2,4,128,256]{4,3,2,1,0:T(8,128)(2,1)} %get-tuple-element.33.states, f32[2,2,3,128,256]{4,3,2,1,0:T(8,128)} %get-tuple-element.34.gates, ...), custom_call_target="tpu_custom_call" | custom-call | flops 1 | bytes 1 | tf_op jit(solution)/shard_map/late_sections/pallas_call | solution.py:464
  132.3 0.6 collective-permute-start.19
  132.9 1.5 %collective-permute-start.15 = (bf16[256,512]{1,0:T(8,128)(2,1)S(1)}, bf16[256,512]{1,0:T(8,128)(2,1)S(1)}, u32[]{:S(2)}, u32[]{:S(2)}) collective-permute-start(bf16[256,512]{1,0:T(8,128)(2,1)S(1)} %collective-permute-done.12.refs_3_), channel_id=1, source_target_pairs={{0,16},{16,0},{1,17},{17,1},{2,18},{18,2},{3,19},{19,3},{4,20},{20... | collective-permute-start | bytes 786440 | tf_op jit(solution)/shard_map/ppermute | solution.py:149
  134.4 1.2 collective-permute-done.21.refs_12_
  135.6 0.5 collective-permute-start.24
  136.1 3.4 %collective-permute-done.19.refs_10_ = bf16[512,256]{1,0:T(8,128)(2,1)S(1)} collective-permute-done((bf16[512,256]{1,0:T(8,128)(2,1)}, bf16[512,256]{1,0:T(8,128)(2,1)S(1)}, u32[]{:S(2)}, u32[]{:S(2)}) %collective-permute-start.19) | collective-permute-done | bytes 262176 | tf_op jit(solution)/shard_map/ppermute | solution.py:149
  139.5 2.1 %collective-permute-done.15.refs_7_ = bf16[256,512]{1,0:T(8,128)(2,1)S(1)} collective-permute-done((bf16[256,512]{1,0:T(8,128)(2,1)S(1)}, bf16[256,512]{1,0:T(8,128)(2,1)S(1)}, u32[]{:S(2)}, u32[]{:S(2)}) %collective-permute-start.15) | collective-permute-done | bytes 262176 | tf_op jit(solution)/shard_map/ppermute | solution.py:149
  141.6 0.9 copy-done.2
  142.6 3.8 %out.1 = bf16[512,512]{1,0:T(8,128)(2,1)} custom-call(s32[2]{0:T(128)S(1)} %pad_add_fusion.2.place.spots, bf16[256,512]{1,0:T(8,128)(2,1)S(1)} %copy-done.3, bf16[256,512]{1,0:T(8,128)(2,1)S(1)} %collective-permute-done.10.refs_1_, bf16[256,512]{1,0:T(8,128)(2,1)S(1)} %collective-permute-done.11.refs_2_, ...), custom_call_target="tpu_custom_call" | custom-call | flops 1 | bytes 1 | tf_op jit(solution)/shard_map/out/pallas_call | solution.py:512
  (64 shorter events, 0.7 us)
Async XLA Ops:
  6.5 1.6 %copy-start = (bf16[4,512,512]{2,1,0:T(8,128)(2,1)S(1)}, bf16[4,512,512]{2,1,0:T(8,128)(2,1)}, u32[]{:S(2)}) copy-start(bf16[4,512,512]{2,1,0:T(8,128)(2,1)} %param.17) | copy-start | bytes 6291460
  6.5 2.6 %copy-start.8 = (s32[512]{0:T(512)S(1)}, s32[512]{0:T(512)}, u32[]{:S(2)}) copy-start(s32[512]{0:T(512)} %param.12) | copy-start | bytes 6148
  6.5 2.6 %copy-start.7 = (bf16[4,512]{1,0:T(4,128)(2,1)S(1)}, bf16[4,512]{1,0:T(4,128)(2,1)}, u32[]{:S(2)}) copy-start(bf16[4,512]{1,0:T(4,128)(2,1)} %param.15) | copy-start | bytes 12292
  6.5 2.6 %copy-start.5 = (bf16[512,512]{1,0:T(8,128)(2,1)S(1)}, bf16[512,512]{1,0:T(8,128)(2,1)}, u32[]{:S(2)}) copy-start(bf16[512,512]{1,0:T(8,128)(2,1)} %param.10) | copy-start | bytes 1572868
  6.5 3.8 %copy-start.6 = (bf16[512,512]{1,0:T(8,128)(2,1)S(1)}, bf16[512,512]{1,0:T(8,128)(2,1)}, u32[]{:S(2)}) copy-start(bf16[512,512]{1,0:T(8,128)(2,1)} %param.11) | copy-start | bytes 1572868
  6.5 3.8 %copy-start.9 = (s32[4]{0:T(128)S(1)}, s32[4]{0:T(128)}, u32[]{:S(2)}) copy-start(s32[4]{0:T(128)} %param.13) | copy-start | bytes 52
  6.6 68.9 %all-gather.5.cloned.1.call-start = ((), (), s32[]{:S(2)}) async-start(), calls=%async_computation | async-start | bytes 3932160 | tf_op jit(solution)/shard_map/all_gather | solution.py:568
  9.1 8.3 %copy-start.10 = (s32[16]{0:T(128)S(1)}, s32[16]{0:T(128)}, u32[]{:S(2)}) copy-start(s32[16]{0:T(128)} %param.14) | copy-start | bytes 196
  9.1 101.2 %all-gather.7.cloned.1.call-start = ((), (), s32[]{:S(2)}) async-start(), calls=%async_computation.1 | async-start | bytes 1310720 | tf_op jit(solution)/shard_map/all_gather | solution.py:597
  12.9 27.7 %collective-permute-start = (bf16[2,512,512]{2,1,0:T(8,128)(2,1)S(1)}, bf16[2,512,512]{2,1,0:T(8,128)(2,1)}, u32[]{:S(2)}, u32[]{:S(2)}) collective-permute-start(bf16[2,512,512]{2,1,0:T(8,128)(2,1)S(1)} %pad_maximum_fusion.refs_0_), channel_id=1, source_target_pairs={{0,2},{1,3},{2,0},{3,1},{4,6},{5,7},{6,4},{7,5},{8,10},{9,11},{10,... | collective-permute-start | bytes 3145736 | tf_op jit(solution)/shard_map/ppermute | solution.py:149
  15.9 24.7 %collective-permute-start.1 = (bf16[2,512,512]{2,1,0:T(8,128)(2,1)S(1)}, bf16[2,512,512]{2,1,0:T(8,128)(2,1)}, u32[]{:S(2)}, u32[]{:S(2)}) collective-permute-start(bf16[2,512,512]{2,1,0:T(8,128)(2,1)S(1)} %pad_maximum_fusion.refs_0_), channel_id=1, source_target_pairs={{0,16},{16,0},{1,17},{17,1},{2,18},{18,2},{3,19},{19,3},{4,20},{20... | collective-permute-start | bytes 3145736 | tf_op jit(solution)/shard_map/ppermute | solution.py:149
  17.4 23.2 %collective-permute-start.2 = (bf16[2,512,512]{2,1,0:T(8,128)(2,1)S(1)}, bf16[2,512,512]{2,1,0:T(8,128)(2,1)}, u32[]{:S(2)}, u32[]{:S(2)}) collective-permute-start(bf16[2,512,512]{2,1,0:T(8,128)(2,1)S(1)} %pad_maximum_fusion.refs_0_), channel_id=1, source_target_pairs={{0,1},{1,0},{2,3},{3,2},{4,5},{5,4},{6,7},{7,6},{8,9},{9,8},{10,11... | collective-permute-start | bytes 3145736 | tf_op jit(solution)/shard_map/ppermute | solution.py:149
  17.4 23.2 %collective-permute-start.9 = (s32[16]{0:T(128)S(1)}, s32[16]{0:T(128)S(1)}, u32[]{:S(2)}, u32[]{:S(2)}) collective-permute-start(s32[16]{0:T(128)S(1)} %copy-done.10), channel_id=1, source_target_pairs={{0,16},{16,0},{1,17},{17,1},{2,18},{18,2},{3,19},{19,3},{4,20},{20... | collective-permute-start | bytes 200 | tf_op jit(solution)/shard_map/ppermute | solution.py:149
  21.6 39.0 %copy-start.4 = (f32[2048]{0:T(1024)S(1)}, f32[2048]{0:T(1024)}, u32[]{:S(2)}) copy-start(f32[2048]{0:T(1024)} %param.16) | copy-start | bytes 24580
  22.0 0.9 copy-start.1
  42.6 12.8 %collective-permute-start.5 = (bf16[512,512]{1,0:T(8,128)(2,1)}, bf16[512,512]{1,0:T(8,128)(2,1)}, u32[]{:S(2)}, u32[]{:S(2)}) collective-permute-start(bf16[512,512]{1,0:T(8,128)(2,1)} %slice_bitcast_fusion.1), channel_id=1, source_target_pairs={{0,16},{16,0},{1,17},{17,1},{2,18},{18,2},{3,19},{19,3},{4,20},{20... | collective-permute-start | bytes 1572872 | tf_op jit(solution)/shard_map/ppermute | solution.py:149
  45.9 12.5 %collective-permute-start.7 = (bf16[512,512]{1,0:T(8,128)(2,1)}, bf16[512,512]{1,0:T(8,128)(2,1)}, u32[]{:S(2)}, u32[]{:S(2)}) collective-permute-start(bf16[512,512]{1,0:T(8,128)(2,1)} %slice_bitcast_fusion), channel_id=1, source_target_pairs={{0,2},{1,3},{2,0},{3,1},{4,6},{5,7},{6,4},{7,5},{8,10},{9,11},{10,... | collective-permute-start | bytes 1572872 | tf_op jit(solution)/shard_map/ppermute | solution.py:149
  46.6 14.0 %collective-permute-start.3 = (bf16[2,512,512]{2,1,0:T(8,128)(2,1)}, bf16[2,512,512]{2,1,0:T(8,128)(2,1)}, u32[]{:S(2)}, u32[]{:S(2)}) collective-permute-start(bf16[2,512,512]{2,1,0:T(8,128)(2,1)} %collective-permute-done.refs_2_), channel_id=1, source_target_pairs={{0,1},{1,0},{2,3},{3,2},{4,5},{5,4},{6,7},{7,6},{8,9},{9,8},{10,11... | collective-permute-start | bytes 3145736 | tf_op jit(solution)/shard_map/ppermute | solution.py:149
  46.7 13.9 %collective-permute-start.4 = (bf16[2,512,512]{2,1,0:T(8,128)(2,1)}, bf16[2,512,512]{2,1,0:T(8,128)(2,1)}, u32[]{:S(2)}, u32[]{:S(2)}) collective-permute-start(bf16[2,512,512]{2,1,0:T(8,128)(2,1)} %collective-permute-done.1.refs_4_), channel_id=1, source_target_pairs={{0,1},{1,0},{2,3},{3,2},{4,5},{5,4},{6,7},{7,6},{8,9},{9,8},{10,11... | collective-permute-start | bytes 3145736 | tf_op jit(solution)/shard_map/ppermute | solution.py:149
  55.3 4.4 %collective-permute-start.6 = (bf16[512,512]{1,0:T(8,128)(2,1)}, bf16[512,512]{1,0:T(8,128)(2,1)S(1)}, u32[]{:S(2)}, u32[]{:S(2)}) collective-permute-start(bf16[512,512]{1,0:T(8,128)(2,1)} %collective-permute-done.5.refs_6_), channel_id=1, source_target_pairs={{0,1},{1,0},{2,3},{3,2},{4,5},{5,4},{6,7},{7,6},{8,9},{9,8},{10,11... | collective-permute-start | bytes 1572872 | tf_op jit(solution)/shard_map/ppermute | solution.py:149
  58.4 2.1 %collective-permute-start.8 = (bf16[512,512]{1,0:T(8,128)(2,1)}, bf16[512,512]{1,0:T(8,128)(2,1)S(1)}, u32[]{:S(2)}, u32[]{:S(2)}) collective-permute-start(bf16[512,512]{1,0:T(8,128)(2,1)} %collective-permute-done.7.refs_8_), channel_id=1, source_target_pairs={{0,1},{1,0},{2,3},{3,2},{4,5},{5,4},{6,7},{7,6},{8,9},{9,8},{10,11... | collective-permute-start | bytes 1572872 | tf_op jit(solution)/shard_map/ppermute | solution.py:149
  75.5 24.9 %collective-permute-start.10 = (bf16[256,512]{1,0:T(8,128)(2,1)}, bf16[256,512]{1,0:T(8,128)(2,1)S(1)}, u32[]{:S(2)}, u32[]{:S(2)}) collective-permute-start(bf16[256,512]{1,0:T(8,128)(2,1)} %get-tuple-element.24.refs_0_), channel_id=1, source_target_pairs={{0,4},{4,0},{8,12},{12,8},{1,5},{5,1},{9,13},{13,9},{2,6},{6,2},{1... | collective-permute-start | bytes 786440 | tf_op jit(solution)/shard_map/ppermute | solution.py:149
  75.5 24.9 %collective-permute-start.11 = (bf16[256,512]{1,0:T(8,128)(2,1)}, bf16[256,512]{1,0:T(8,128)(2,1)S(1)}, u32[]{:S(2)}, u32[]{:S(2)}) collective-permute-start(bf16[256,512]{1,0:T(8,128)(2,1)} %get-tuple-element.24.refs_0_), channel_id=1, source_target_pairs={{0,8},{4,12},{8,0},{12,4},{1,9},{5,13},{9,1},{13,5},{2,10},{6,14},... | collective-permute-start | bytes 786440 | tf_op jit(solution)/shard_map/ppermute | solution.py:149
  94.6 18.6 %collective-permute-start.16 = (bf16[3,2,128,256]{3,2,1,0:T(8,128)(2,1)}, bf16[3,2,128,256]{3,2,1,0:T(8,128)(2,1)}, u32[]{:S(2)}, u32[]{:S(2)}) collective-permute-start(bf16[3,2,128,256]{3,2,1,0:T(8,128)(2,1)} %get-tuple-element.35), channel_id=1, source_target_pairs={{0,4},{4,8},{8,12},{1,5},{5,9},{9,13},{2,6},{6,10},{10,14},{3,7},{... | collective-permute-start | bytes 1179656 | tf_op jit(solution)/shard_map/ppermute | solution.py:28
  99.1 16.0 %collective-permute-start.17 = (bf16[3,2,128,256]{3,2,1,0:T(8,128)(2,1)}, bf16[3,2,128,256]{3,2,1,0:T(8,128)(2,1)}, u32[]{:S(2)}, u32[]{:S(2)}) collective-permute-start(bf16[3,2,128,256]{3,2,1,0:T(8,128)(2,1)} %get-tuple-element.36), channel_id=1, source_target_pairs={{4,0},{8,4},{12,8},{5,1},{9,5},{13,9},{6,2},{10,6},{14,10},{7,3},{... | collective-permute-start | bytes 1179656 | tf_op jit(solution)/shard_map/ppermute | solution.py:28
  100.4 31.9 %collective-permute-start.12 = (bf16[256,512]{1,0:T(8,128)(2,1)S(1)}, bf16[256,512]{1,0:T(8,128)(2,1)S(1)}, u32[]{:S(2)}, u32[]{:S(2)}) collective-permute-start(bf16[256,512]{1,0:T(8,128)(2,1)S(1)} %collective-permute-done.11.refs_2_), channel_id=1, source_target_pairs={{0,4},{4,0},{8,12},{12,8},{1,5},{5,1},{9,13},{13,9},{2,6},{6,2},{1... | collective-permute-start | bytes 786440 | tf_op jit(solution)/shard_map/ppermute | solution.py:149
  103.1 29.8 %collective-permute-start.14 = (bf16[256,512]{1,0:T(8,128)(2,1)S(1)}, bf16[256,512]{1,0:T(8,128)(2,1)S(1)}, u32[]{:S(2)}, u32[]{:S(2)}) collective-permute-start(bf16[256,512]{1,0:T(8,128)(2,1)S(1)} %collective-permute-done.11.refs_2_), channel_id=1, source_target_pairs={{0,16},{16,0},{1,17},{17,1},{2,18},{18,2},{3,19},{19,3},{4,20},{20... | collective-permute-start | bytes 786440 | tf_op jit(solution)/shard_map/ppermute | solution.py:149
  104.6 28.3 %collective-permute-start.13 = (bf16[256,512]{1,0:T(8,128)(2,1)S(1)}, bf16[256,512]{1,0:T(8,128)(2,1)}, u32[]{:S(2)}, u32[]{:S(2)}) collective-permute-start(bf16[256,512]{1,0:T(8,128)(2,1)S(1)} %collective-permute-done.10.refs_1_), channel_id=1, source_target_pairs={{0,16},{16,0},{1,17},{17,1},{2,18},{18,2},{3,19},{19,3},{4,20},{20... | collective-permute-start | bytes 786440 | tf_op jit(solution)/shard_map/ppermute | solution.py:149
  122.2 19.5 %copy-start.3 = (bf16[256,512]{1,0:T(8,128)(2,1)S(1)}, bf16[256,512]{1,0:T(8,128)(2,1)}, u32[]{:S(2)}) copy-start(bf16[256,512]{1,0:T(8,128)(2,1)} %get-tuple-element.24.refs_0_) | copy-start | bytes 786436
  122.2 13.4 %collective-permute-start.21 = (bf16[512,256]{1,0:T(8,128)(2,1)}, bf16[512,256]{1,0:T(8,128)(2,1)S(1)}, u32[]{:S(2)}, u32[]{:S(2)}) collective-permute-start(bf16[512,256]{1,0:T(8,128)(2,1)} %late_sections.3), channel_id=1, source_target_pairs={{0,16},{16,0},{1,17},{17,1},{2,18},{18,2},{3,19},{19,3},{4,20},{20... | collective-permute-start | bytes 786440 | tf_op jit(solution)/shard_map/ppermute | solution.py:149
  123.7 11.9 %collective-permute-start.23 = (bf16[512,256]{1,0:T(8,128)(2,1)}, bf16[512,256]{1,0:T(8,128)(2,1)S(1)}, u32[]{:S(2)}, u32[]{:S(2)}) collective-permute-start(bf16[512,256]{1,0:T(8,128)(2,1)} %late_sections.3), channel_id=1, source_target_pairs={{0,18},{1,19},{2,16},{3,17},{16,2},{17,3},{18,0},{19,1},{4,22},{5,... | collective-permute-start | bytes 786440 | tf_op jit(solution)/shard_map/ppermute | solution.py:157
  132.3 7.2 %collective-permute-start.19 = (bf16[512,256]{1,0:T(8,128)(2,1)}, bf16[512,256]{1,0:T(8,128)(2,1)S(1)}, u32[]{:S(2)}, u32[]{:S(2)}) collective-permute-start(bf16[512,256]{1,0:T(8,128)(2,1)} %late_sections.2.refs_8_), channel_id=1, source_target_pairs={{0,2},{1,3},{2,0},{3,1},{4,6},{5,7},{6,4},{7,5},{8,10},{9,11},{10,... | collective-permute-start | bytes 786440 | tf_op jit(solution)/shard_map/ppermute | solution.py:149
  132.9 6.6 %collective-permute-start.18 = (bf16[512,256]{1,0:T(8,128)(2,1)}, bf16[512,256]{1,0:T(8,128)(2,1)S(1)}, u32[]{:S(2)}, u32[]{:S(2)}) collective-permute-start(bf16[512,256]{1,0:T(8,128)(2,1)} %late_sections.2.refs_8_), channel_id=1, source_target_pairs={{0,1},{1,0},{2,3},{3,2},{4,5},{5,4},{6,7},{7,6},{8,9},{9,8},{10,11... | collective-permute-start | bytes 786440 | tf_op jit(solution)/shard_map/ppermute | solution.py:149
  132.9 8.7 %collective-permute-start.15 = (bf16[256,512]{1,0:T(8,128)(2,1)S(1)}, bf16[256,512]{1,0:T(8,128)(2,1)S(1)}, u32[]{:S(2)}, u32[]{:S(2)}) collective-permute-start(bf16[256,512]{1,0:T(8,128)(2,1)S(1)} %collective-permute-done.12.refs_3_), channel_id=1, source_target_pairs={{0,16},{16,0},{1,17},{17,1},{2,18},{18,2},{3,19},{19,3},{4,20},{20... | collective-permute-start | bytes 786440 | tf_op jit(solution)/shard_map/ppermute | solution.py:149
  135.6 6.0 %collective-permute-start.22 = (bf16[512,256]{1,0:T(8,128)(2,1)S(1)}, bf16[512,256]{1,0:T(8,128)(2,1)S(1)}, u32[]{:S(2)}, u32[]{:S(2)}) collective-permute-start(bf16[512,256]{1,0:T(8,128)(2,1)S(1)} %collective-permute-done.21.refs_12_), channel_id=1, source_target_pairs={{0,1},{1,0},{2,3},{3,2},{4,5},{5,4},{6,7},{7,6},{8,9},{9,8},{10,11... | collective-permute-start | bytes 786440 | tf_op jit(solution)/shard_map/ppermute | solution.py:149
  135.6 6.0 %collective-permute-start.24 = (bf16[512,256]{1,0:T(8,128)(2,1)S(1)}, bf16[512,256]{1,0:T(8,128)(2,1)S(1)}, u32[]{:S(2)}, u32[]{:S(2)}) collective-permute-start(bf16[512,256]{1,0:T(8,128)(2,1)S(1)} %collective-permute-done.23.refs_14_), channel_id=1, source_target_pairs={{0,1},{1,0},{2,3},{3,2},{4,5},{5,4},{6,7},{7,6},{8,9},{9,8},{10,11... | collective-permute-start | bytes 786440 | tf_op jit(solution)/shard_map/ppermute | solution.py:149
  139.5 2.1 %collective-permute-start.20 = (bf16[512,256]{1,0:T(8,128)(2,1)S(1)}, bf16[512,256]{1,0:T(8,128)(2,1)S(1)}, u32[]{:S(2)}, u32[]{:S(2)}) collective-permute-start(bf16[512,256]{1,0:T(8,128)(2,1)S(1)} %collective-permute-done.19.refs_10_), channel_id=1, source_target_pairs={{0,1},{1,0},{2,3},{3,2},{4,5},{5,4},{6,7},{7,6},{8,9},{9,8},{10,11... | collective-permute-start | bytes 786440 | tf_op jit(solution)/shard_map/ppermute | solution.py:149
  141.6 1.0 copy-start.2
Sparse Core Ops, SparseCore 0:
  9.2 66.2 all-gather.4
  77.1 33.2 all-gather.6

commit v4 on v3

--- a/solution.py
+++ b/solution.py
@@ -483,6 +483,99 @@
     )(normed, weight, states, gates, tables, mask, *rims)
 
 
+def last_gate_kernel(g, normed, weight, out, held, kept, x_sems, w_sems):
+    s = pl.program_id(0)
+
+    @pl.when(s == 0)
+    def _():
+        order = [(i, g) for i in range(normed.shape[0])]
+        fetch(normed, weight, 1, order, held, kept, x_sems, w_sems)
+        wait_weight(weight, 1, kept, w_sems)
+
+    at = s * normed.shape[1] + g
+    wait_rows(normed, at, held, x_sems)
+    out[0] = product(held.at[at], kept.at[0])
+
+
+def last_gate_of(normed, weight, g):
+    strands, _, rows, _ = normed.shape
+    width = weight.shape[-1]
+    return pl.pallas_call(
+        functools.partial(last_gate_kernel, g),
+        grid=(strands,),
+        in_specs=[pl.BlockSpec(memory_space=pltpu.HBM)] * 2,
+        out_specs=pl.BlockSpec((1, rows, width), lambda s: (s, 0, 0)),
+        out_shape=jax.ShapeDtypeStruct((strands, rows, width), jnp.float32),
+        scratch_shapes=fetch_scratch(normed, weight, 1),
+        compiler_params=params("arbitrary", limit=WIDE),
+        cost_estimate=SMALL,
+        name="last_gate",
+    )(normed, weight)
+
+
+def gated_kernel(last_gate, states, gates, table, mask, *refs):
+    rims, out = refs[:2], refs[2]
+    extended = refs[3:]
+    s = pl.program_id(0)
+    block = table.shape[-2]
+    rows = out.shape[0]
+    blocks = rows // block
+
+    def put(k, n, value):
+        at = jnp.where(s == 0, n, blocks - 1 - n) * block
+        extended[k][pl.ds(shifted_at(at, s, block), block)] = value
+
+    for k in range(3):
+
+        @pl.when(s == 0)
+        def _():
+            extended[k][:block] = rims[0][k, 0]
+
+        @pl.when(s == 1)
+        def _():
+            extended[k][rows:] = rims[1][k, 0]
+
+    put(0, 0, states[0, 0, 0])
+    put(1, 1, states[0, 0, 1])
+    for n in range(2, blocks):
+        put(2, n, states[0, 0, n])
+    for k in range(2):
+        for n in range(k + 1):
+            gate = gates.at[0, 0, k + n]
+            _, value = gated_block(k, s, n, blocks, extended[k], table, mask, gate, 0)
+            put(k + 1, n, value)
+
+    for n in range(blocks):
+        row, value = gated_block(2, s, n, blocks, extended[2], table, mask, last_gate.at[0])
+        span = pl.ds(row, block)
+        before = jnp.where(s == 0, 0.0, out[span].astype(jnp.float32))
+        out[span] = (before + value.astype(jnp.float32)).astype(jnp.bfloat16)
+
+
+def gated_sections(last_gate, states, gates, tables, mask, rims, g):
+    strands, rows, _ = last_gate.shape
+    blocks, block, width = states.shape[2:]
+    sections, _, heads = tables.shape[:3]
+    return pl.pallas_call(
+        gated_kernel,
+        grid=(strands,),
+        in_specs=[pl.BlockSpec((1, rows, width), lambda s: (s, 0, 0))]
+        + [
+            pl.BlockSpec((1, 1, blocks, block, width), lambda s: (s, g, 0, 0, 0)),
+            pl.BlockSpec((1, 1, 3, block, width), lambda s: (s, g, 0, 0, 0)),
+            pl.BlockSpec((sections, 1, heads, block, 2 * block), lambda s: (0, s, 0, 0, 0)),
+            pl.BlockSpec((1, 1, blocks, block, 2 * block), lambda s: (s, g, 0, 0, 0)),
+        ]
+        + [pl.BlockSpec((sections, 1, block, width), lambda s: (0, g, 0, 0)) for _ in rims],
+        out_specs=pl.BlockSpec((rows, width), lambda s: (0, 0)),
+        out_shape=jax.ShapeDtypeStruct((rows, width), jnp.bfloat16),
+        scratch_shapes=[pltpu.VMEM((rows + block, width), jnp.bfloat16)] * 3,
+        compiler_params=params("arbitrary", limit=WIDE),
+        cost_estimate=SMALL,
+        name="gated_sections",
+    )(last_gate, states, gates, tables, mask, *rims)
+
+
 def out_kernel(parts, spots, *refs):
     weights, pieces = refs[: 2 * parts], refs[2 * parts : -2]
     out, held = refs[-2:]
@@ -508,7 +601,7 @@
     parts = len(near)
     rows, depth = pieces[0].shape
     width = near[0].shape[-1]
-    tile = rows // 2
+    tile = rows
     return pl.pallas_call(
         functools.partial(out_kernel, parts),
         grid_spec=pltpu.PrefetchScalarGridSpec(
@@ -613,9 +706,12 @@
     rims = shifted(rim_fwd, "ctx", 1), shifted(rim_rev, "ctx", -1)
     one, two, states = lax.optimization_barrier((one, two, states))
     near = [out_near, one, two, flip(two, "ctx", 1)]
-    far = [out_far] + [flip(w, "grp", 1) for w in near[1:]]
+    far = [out_far, flip(one, "grp", 1), flip(two, "grp", 1)]
+    late, far[2] = lax.optimization_barrier((late, far[2]))
+    far.append(flip(near[3], "grp", 1))
     work = normed, late, states, gates, tables, mask, rims
-    mixed_far = late_sections(*work, 1)
+    last_gate = last_gate_of(normed, late, 1)
+    mixed_far = gated_sections(last_gate, states, gates, tables, mask, rims, 1)
     mixed_near = late_sections(*work, 0)
     from_y = flip(mixed_far, "grp", 1)
     from_xy = across(mixed_far, 2)

time: 154 us -> 150 us (0.974)
  waiting for transfers between devices: 52.8 us -> 48 us
    pallas_call x0 -> x2, Pallas kernels: none -> 8.57 us  [the longest x1 4.77 us: last_gate_of(): pl.pallas_call(functools.partial(last_gate_kernel, g), grid=(strands,), i...]
    pallas_call x2 -> x1, Pallas kernels: 14.1 us -> 7.06 us  [late_sections(): pl.pallas_call(functools.partial(late_kernel, g), grid=(strands,), in_spe...]
    ppermute x2, waiting for transfers between devices: 4.8 us -> 0.01 us  [shifted(): return lax.ppermute(value, axis, pairs)]
  transfers between devices with their start and end apart: 27 -> 27, of which waited for: 11 -> 9; matrix products, arithmetic and copies ran while one was open for 8% -> 8% of each run, Pallas kernels for 27% -> 28%
where the time goes in v4:
time: 150 us
  waiting for transfers between devices  48 us (32%)
  Pallas kernels  46.2 us (31%)
  starting transfers between devices  25.1 us (17%)
  between operations  13.7 us (9%)
  local copies, waits for them, and re-layouts  10.8 us (7%)
  other arithmetic  3.53 us (2%)
  matrix products  2.41 us (2%)
    ppermute x22, waiting for transfers between devices, flip(): return lax.ppermute(block, axis, [(i, i ^ bit) for i in range(count)])  36.5 us
    ppermute x22, starting transfers between devices, flip(): return lax.ppermute(block, axis, [(i, i ^ bit) for i in range(count)])  17.9 us
    pallas_call x1, Pallas kernels, early_sections(): pl.pallas_call(early_kernel, grid=(strands, groups), in_specs=[pl.BlockSp...  17.8 us
    pallas_call x1, Pallas kernels, norm_all(): pl.pallas_call(functools.partial(norm_kernel, layout), grid_spec=pltpu.Pr...  8.68 us
    pallas_call x1, Pallas kernels, late_sections(): pl.pallas_call(functools.partial(late_kernel, g), grid=(strands,), in_spe...  7.06 us
    all_gather x1, waiting for transfers between devices, paired(): early = lax.all_gather(columns[:sections], 'ctx', axis=0)  6.23 us
    ppermute x2, starting transfers between devices, shifted(): return lax.ppermute(value, axis, pairs)  5.74 us
    all_gather x1, waiting for transfers between devices, paired(): late = lax.all_gather(after(columns[sections:], x), 'ctx', axis=0)  5.22 us
  transfers between devices with their start and end apart: 27, of which 9 were waited for; matrix products, arithmetic and copies ran while one was open for 8% of the time, Pallas kernels for 28%

profile of v4, /device:TPU:0, one launch (start us, length us, event | category | flops | bytes accessed | tf_op | source)
XLA Modules:
  0.0 149.7 jit_solution(15767179759619170758)
XLA Ops:
  6.6 1.5 %copy-done = bf16[4,512,512]{2,1,0:T(8,128)(2,1)S(1)} copy-done((bf16[4,512,512]{2,1,0:T(8,128)(2,1)S(1)}, bf16[4,512,512]{2,1,0:T(8,128)(2,1)}, u32[]{:S(2)}) %copy-start) | copy-done | bytes 2097176
  8.1 0.9 constant_dynamic-slice_fusion
  9.2 1.2 fusion.3
  10.3 1.3 fusion.2
  11.6 1.3 pad_maximum_fusion.refs_0_
  12.9 3.0 %collective-permute-start = (bf16[2,512,512]{2,1,0:T(8,128)(2,1)S(1)}, bf16[2,512,512]{2,1,0:T(8,128)(2,1)}, u32[]{:S(2)}, u32[]{:S(2)}) collective-permute-start(bf16[2,512,512]{2,1,0:T(8,128)(2,1)S(1)} %pad_maximum_fusion.refs_0_), channel_id=1, source_target_pairs={{0,2},{1,3},{2,0},{3,1},{4,6},{5,7},{6,4},{7,5},{8,10},{9,11},{10,... | collective-permute-start | bytes 3145736 | tf_op jit(solution)/shard_map/ppermute | solution.py:149
  15.9 1.5 %collective-permute-start.1 = (bf16[2,512,512]{2,1,0:T(8,128)(2,1)S(1)}, bf16[2,512,512]{2,1,0:T(8,128)(2,1)}, u32[]{:S(2)}, u32[]{:S(2)}) collective-permute-start(bf16[2,512,512]{2,1,0:T(8,128)(2,1)S(1)} %pad_maximum_fusion.refs_0_), channel_id=1, source_target_pairs={{0,16},{16,0},{1,17},{17,1},{2,18},{18,2},{3,19},{19,3},{4,20},{20... | collective-permute-start | bytes 3145736 | tf_op jit(solution)/shard_map/ppermute | solution.py:149
  17.4 0.5 collective-permute-start.9
  17.9 0.7 fusion.9
  18.6 0.1 rev.3
  18.9 0.7 constant_dynamic-slice_fusion.3
  19.7 1.8 %constant_dynamic-slice_fusion.1 = (bf16[256,512]{1,0:T(8,128)(2,1)S(1)}, bf16[256,512]{1,0:T(8,128)(2,1)}) fusion(bf16[512,512]{1,0:T(8,128)(2,1)} %param.19, s32[]{:T(128)S(6)} %select_n.18, s32[]{:T(128)S(6)} %select_n.15), kind=kLoop, calls=%fused_computation.32 | loop fusion | bytes 1048584 | tf_op jit(solution)/shard_map/dynamic_slice | solution.py:700
  21.6 0.4 tables.1.table
  22.0 0.9 copy-done.1
  22.9 17.7 %collective-permute-done.9 = s32[16]{0:T(128)S(1)} collective-permute-done((s32[16]{0:T(128)S(1)}, s32[16]{0:T(128)S(1)}, u32[]{:S(2)}, u32[]{:S(2)}) %collective-permute-start.9) | collective-permute-done | bytes 96 | tf_op jit(solution)/shard_map/ppermute | solution.py:149
  40.7 1.9 %slice_bitcast_fusion.1 = bf16[512,512]{1,0:T(8,128)(2,1)} fusion(bf16[2,512,512]{2,1,0:T(8,128)(2,1)} %collective-permute-done.refs_2_), kind=kLoop, calls=%fused_computation.10 | loop fusion | bytes 1048576 | tf_op jit(solution)/shard_map/squeeze | solution.py:677
  42.5 1.5 %collective-permute-start.5 = (bf16[512,512]{1,0:T(8,128)(2,1)}, bf16[512,512]{1,0:T(8,128)(2,1)}, u32[]{:S(2)}, u32[]{:S(2)}) collective-permute-start(bf16[512,512]{1,0:T(8,128)(2,1)} %slice_bitcast_fusion.1), channel_id=1, source_target_pairs={{0,16},{16,0},{1,17},{17,1},{2,18},{18,2},{3,19},{19,3},{4,20},{20... | collective-permute-start | bytes 1572872 | tf_op jit(solution)/shard_map/ppermute | solution.py:149
  44.0 1.9 %slice_bitcast_fusion = bf16[512,512]{1,0:T(8,128)(2,1)} fusion(bf16[2,512,512]{2,1,0:T(8,128)(2,1)} %collective-permute-done.1.refs_4_), kind=kLoop, calls=%fused_computation.9 | loop fusion | bytes 1048576 | tf_op jit(solution)/shard_map/squeeze | solution.py:677
  45.9 0.5 collective-permute-start.7
  46.4 0.1 convert_reduce_fusion
  46.6 0.5 collective-permute-start.4
  47.2 8.1 %collective-permute-done.5.refs_6_ = bf16[512,512]{1,0:T(8,128)(2,1)} collective-permute-done((bf16[512,512]{1,0:T(8,128)(2,1)}, bf16[512,512]{1,0:T(8,128)(2,1)}, u32[]{:S(2)}, u32[]{:S(2)}) %collective-permute-start.5) | collective-permute-done | bytes 524320 | tf_op jit(solution)/shard_map/ppermute | solution.py:149
  55.3 3.1 %collective-permute-done.7.refs_8_ = bf16[512,512]{1,0:T(8,128)(2,1)} collective-permute-done((bf16[512,512]{1,0:T(8,128)(2,1)}, bf16[512,512]{1,0:T(8,128)(2,1)}, u32[]{:S(2)}, u32[]{:S(2)}) %collective-permute-start.7) | collective-permute-done | bytes 524320 | tf_op jit(solution)/shard_map/ppermute | solution.py:149
  58.4 1.2 compare_convert_fusion.mask
  59.7 0.9 collective-permute-done.8.refs_9_
  60.5 8.7 %norm.1.normed = bf16[2,2,512,2048]{3,2,1,0:T(8,128)(2,1)} custom-call(s32[2]{0:T(128)S(1)} %pad_add_fusion.2.place.spots, f32[1,2048]{1,0:T(1,128)S(1)} %bitcast.28, bf16[2,512,512]{2,1,0:T(8,128)(2,1)S(1)} %pad_maximum_fusion.refs_0_, bf16[2,512,512]{2,1,0:T(8,128)(2,1)} %collective-permute-done.2.refs_1_, ...), custom_call_target="tpu_custom_call" | custom-call | flops 1 | bytes 1 | tf_op jit(solution)/shard_map/norm/pallas_call | solution.py:201
  69.2 6.2 %all-gather.5.cloned.1.call-done = bf16[12,512,256]{2,1,0:T(8,128)(2,1)} async-done(((bf16[3,512,256]{2,1,0:T(8,128)(2,1)}), bf16[12,512,256]{2,1,0:T(8,128)(2,1)}) %all-gather.5.cloned.1.call-update) | async-done | bytes 3145744 | tf_op jit(solution)/shard_map/all_gather | solution.py:661
  75.5 1.3 collective-permute-start.11
  76.7 17.8 %early_sections.1 = (bf16[2,2,4,128,256]{4,3,2,1,0:T(8,128)(2,1)}, f32[2,2,3,128,256]{4,3,2,1,0:T(8,128)}, bf16[3,2,128,256]{3,2,1,0:T(8,128)(2,1)}, bf16[3,2,128,256]{3,2,1,0:T(8,128)(2,1)}) custom-call(bf16[2,2,512,2048]{3,2,1,0:T(8,128)(2,1)} %norm.1.normed, bf16[4,3,512,256]{3,2,1,0:T(8,128)(2,1)} %bitcast.31, bf16[3,2,2,128,256]{4,3,2,1,0:T(8,128)(2,1)} %copy-done.1, ...), custom_call_target="tpu_custom_call" | custom-call | flops 1 | bytes 1 | tf_op jit(solution)/shard_map/early_sections/pallas_call | solution.py:380
  94.6 4.5 %collective-permute-start.16 = (bf16[3,2,128,256]{3,2,1,0:T(8,128)(2,1)}, bf16[3,2,128,256]{3,2,1,0:T(8,128)(2,1)}, u32[]{:S(2)}, u32[]{:S(2)}) collective-permute-start(bf16[3,2,128,256]{3,2,1,0:T(8,128)(2,1)} %get-tuple-element.39), channel_id=1, source_target_pairs={{0,4},{4,8},{8,12},{1,5},{5,9},{9,13},{2,6},{6,10},{10,14},{3,7},{... | collective-permute-start | bytes 1179656 | tf_op jit(solution)/shard_map/ppermute | solution.py:28
  99.0 1.3 collective-permute-start.17
  100.3 1.5 %collective-permute-start.14 = (bf16[256,512]{1,0:T(8,128)(2,1)S(1)}, bf16[256,512]{1,0:T(8,128)(2,1)S(1)}, u32[]{:S(2)}, u32[]{:S(2)}) collective-permute-start(bf16[256,512]{1,0:T(8,128)(2,1)S(1)} %collective-permute-done.11.refs_2_), channel_id=1, source_target_pairs={{0,16},{16,0},{1,17},{17,1},{2,18},{18,2},{3,19},{19,3},{4,20},{20... | collective-permute-start | bytes 786440 | tf_op jit(solution)/shard_map/ppermute | solution.py:149
  101.9 2.6 %collective-permute-start.12 = (bf16[256,512]{1,0:T(8,128)(2,1)S(1)}, bf16[256,512]{1,0:T(8,128)(2,1)S(1)}, u32[]{:S(2)}, u32[]{:S(2)}) collective-permute-start(bf16[256,512]{1,0:T(8,128)(2,1)S(1)} %collective-permute-done.11.refs_2_), channel_id=1, source_target_pairs={{0,4},{4,0},{8,12},{12,8},{1,5},{5,1},{9,13},{13,9},{2,6},{6,2},{1... | collective-permute-start | bytes 786440 | tf_op jit(solution)/shard_map/ppermute | solution.py:149
  104.5 0.6 collective-permute-start.13
  105.1 5.2 %all-gather.7.cloned.1.call-done = bf16[4,512,256]{2,1,0:T(8,128)(2,1)} async-done(((bf16[1,512,256]{2,1,0:T(8,128)(2,1)}), bf16[4,512,256]{2,1,0:T(8,128)(2,1)}) %all-gather.7.cloned.1.call-update) | async-done | bytes 1048592 | tf_op jit(solution)/shard_map/all_gather | solution.py:690
  110.3 4.8 %last_gate.1 = f32[2,512,256]{2,1,0:T(8,128)} custom-call(bf16[2,2,512,2048]{3,2,1,0:T(8,128)(2,1)} %norm.1.normed, bf16[4,1,512,256]{3,2,1,0:T(8,128)(2,1)} %bitcast.29), custom_call_target="tpu_custom_call" | custom-call | flops 1 | bytes 1 | tf_op jit(solution)/shard_map/last_gate/pallas_call | solution.py:503
  115.1 3.8 %gated_sections.1 = bf16[512,256]{1,0:T(8,128)(2,1)} custom-call(f32[2,512,256]{2,1,0:T(8,128)} %last_gate.1, bf16[2,2,4,128,256]{4,3,2,1,0:T(8,128)(2,1)} %get-tuple-element.37.states, f32[2,2,3,128,256]{4,3,2,1,0:T(8,128)} %get-tuple-element.38.gates, bf16[3,2,2,128,256]{4,3,2,1,0:T(8,128)(2,1)} %copy-done.1, ...), custom_call_target="tpu_custom_call" | custom-call | flops 1 | bytes 1 | tf_op jit(solution)/shard_map/gated_sections/pallas_call | solution.py:559
  118.9 1.5 collective-permute-start.21
  120.4 1.4 collective-permute-start.23
  121.8 7.1 %late_sections.1.refs_8_ = bf16[512,256]{1,0:T(8,128)(2,1)} custom-call(bf16[2,2,512,2048]{3,2,1,0:T(8,128)(2,1)} %norm.1.normed, bf16[4,1,512,256]{3,2,1,0:T(8,128)(2,1)} %bitcast.30, bf16[2,2,4,128,256]{4,3,2,1,0:T(8,128)(2,1)} %get-tuple-element.37.states, f32[2,2,3,128,256]{4,3,2,1,0:T(8,128)} %get-tuple-element.38.gates, ...), custom_call_target="tpu_custom_call" | custom-call | flops 1 | bytes 1 | tf_op jit(solution)/shard_map/late_sections/pallas_call | solution.py:464
  128.9 0.6 collective-permute-start.19
  129.5 1.6 %collective-permute-start.15 = (bf16[256,512]{1,0:T(8,128)(2,1)S(1)}, bf16[256,512]{1,0:T(8,128)(2,1)S(1)}, u32[]{:S(2)}, u32[]{:S(2)}) collective-permute-start(bf16[256,512]{1,0:T(8,128)(2,1)S(1)} %collective-permute-done.12.refs_3_), channel_id=1, source_target_pairs={{0,16},{16,0},{1,17},{17,1},{2,18},{18,2},{3,19},{19,3},{4,20},{20... | collective-permute-start | bytes 786440 | tf_op jit(solution)/shard_map/ppermute | solution.py:149
  131.1 1.1 collective-permute-done.21.refs_12_
  132.2 0.5 collective-permute-start.24
  132.7 3.4 %collective-permute-done.19.refs_10_ = bf16[512,256]{1,0:T(8,128)(2,1)S(1)} collective-permute-done((bf16[512,256]{1,0:T(8,128)(2,1)}, bf16[512,256]{1,0:T(8,128)(2,1)S(1)}, u32[]{:S(2)}, u32[]{:S(2)}) %collective-permute-start.19) | collective-permute-done | bytes 262176 | tf_op jit(solution)/shard_map/ppermute | solution.py:149
  136.1 2.1 %collective-permute-done.15.refs_7_ = bf16[256,512]{1,0:T(8,128)(2,1)S(1)} collective-permute-done((bf16[256,512]{1,0:T(8,128)(2,1)S(1)}, bf16[256,512]{1,0:T(8,128)(2,1)S(1)}, u32[]{:S(2)}, u32[]{:S(2)}) %collective-permute-start.15) | collective-permute-done | bytes 262176 | tf_op jit(solution)/shard_map/ppermute | solution.py:149
  138.3 0.9 copy-done.2
  139.2 3.7 %out.1 = bf16[512,512]{1,0:T(8,128)(2,1)} custom-call(s32[2]{0:T(128)S(1)} %pad_add_fusion.2.place.spots, bf16[256,512]{1,0:T(8,128)(2,1)S(1)} %copy-done.3, bf16[256,512]{1,0:T(8,128)(2,1)S(1)} %collective-permute-done.10.refs_1_, bf16[256,512]{1,0:T(8,128)(2,1)S(1)} %collective-permute-done.11.refs_2_, ...), custom_call_target="tpu_custom_call" | custom-call | flops 1 | bytes 1 | tf_op jit(solution)/shard_map/out/pallas_call | solution.py:605
  (65 shorter events, 0.6 us)
Async XLA Ops:
  6.5 1.6 %copy-start = (bf16[4,512,512]{2,1,0:T(8,128)(2,1)S(1)}, bf16[4,512,512]{2,1,0:T(8,128)(2,1)}, u32[]{:S(2)}) copy-start(bf16[4,512,512]{2,1,0:T(8,128)(2,1)} %param.17) | copy-start | bytes 6291460
  6.5 2.6 %copy-start.8 = (s32[512]{0:T(512)S(1)}, s32[512]{0:T(512)}, u32[]{:S(2)}) copy-start(s32[512]{0:T(512)} %param.12) | copy-start | bytes 6148
  6.5 2.6 %copy-start.7 = (bf16[4,512]{1,0:T(4,128)(2,1)S(1)}, bf16[4,512]{1,0:T(4,128)(2,1)}, u32[]{:S(2)}) copy-start(bf16[4,512]{1,0:T(4,128)(2,1)} %param.15) | copy-start | bytes 12292
  6.5 2.6 %copy-start.5 = (bf16[512,512]{1,0:T(8,128)(2,1)S(1)}, bf16[512,512]{1,0:T(8,128)(2,1)}, u32[]{:S(2)}) copy-start(bf16[512,512]{1,0:T(8,128)(2,1)} %param.10) | copy-start | bytes 1572868
  6.5 3.8 %copy-start.6 = (bf16[512,512]{1,0:T(8,128)(2,1)S(1)}, bf16[512,512]{1,0:T(8,128)(2,1)}, u32[]{:S(2)}) copy-start(bf16[512,512]{1,0:T(8,128)(2,1)} %param.11) | copy-start | bytes 1572868
  6.5 3.8 %copy-start.9 = (s32[4]{0:T(128)S(1)}, s32[4]{0:T(128)}, u32[]{:S(2)}) copy-start(s32[4]{0:T(128)} %param.13) | copy-start | bytes 52
  6.6 68.9 %all-gather.5.cloned.1.call-start = ((), (), s32[]{:S(2)}) async-start(), calls=%async_computation | async-start | bytes 3932160 | tf_op jit(solution)/shard_map/all_gather | solution.py:661
  9.1 8.3 %copy-start.10 = (s32[16]{0:T(128)S(1)}, s32[16]{0:T(128)}, u32[]{:S(2)}) copy-start(s32[16]{0:T(128)} %param.14) | copy-start | bytes 196
  9.1 101.2 %all-gather.7.cloned.1.call-start = ((), (), s32[]{:S(2)}) async-start(), calls=%async_computation.1 | async-start | bytes 1310720 | tf_op jit(solution)/shard_map/all_gather | solution.py:690
  12.9 27.7 %collective-permute-start = (bf16[2,512,512]{2,1,0:T(8,128)(2,1)S(1)}, bf16[2,512,512]{2,1,0:T(8,128)(2,1)}, u32[]{:S(2)}, u32[]{:S(2)}) collective-permute-start(bf16[2,512,512]{2,1,0:T(8,128)(2,1)S(1)} %pad_maximum_fusion.refs_0_), channel_id=1, source_target_pairs={{0,2},{1,3},{2,0},{3,1},{4,6},{5,7},{6,4},{7,5},{8,10},{9,11},{10,... | collective-permute-start | bytes 3145736 | tf_op jit(solution)/shard_map/ppermute | solution.py:149
  15.9 24.7 %collective-permute-start.1 = (bf16[2,512,512]{2,1,0:T(8,128)(2,1)S(1)}, bf16[2,512,512]{2,1,0:T(8,128)(2,1)}, u32[]{:S(2)}, u32[]{:S(2)}) collective-permute-start(bf16[2,512,512]{2,1,0:T(8,128)(2,1)S(1)} %pad_maximum_fusion.refs_0_), channel_id=1, source_target_pairs={{0,16},{16,0},{1,17},{17,1},{2,18},{18,2},{3,19},{19,3},{4,20},{20... | collective-permute-start | bytes 3145736 | tf_op jit(solution)/shard_map/ppermute | solution.py:149
  17.4 23.2 %collective-permute-start.2 = (bf16[2,512,512]{2,1,0:T(8,128)(2,1)S(1)}, bf16[2,512,512]{2,1,0:T(8,128)(2,1)}, u32[]{:S(2)}, u32[]{:S(2)}) collective-permute-start(bf16[2,512,512]{2,1,0:T(8,128)(2,1)S(1)} %pad_maximum_fusion.refs_0_), channel_id=1, source_target_pairs={{0,1},{1,0},{2,3},{3,2},{4,5},{5,4},{6,7},{7,6},{8,9},{9,8},{10,11... | collective-permute-start | bytes 3145736 | tf_op jit(solution)/shard_map/ppermute | solution.py:149
  17.4 23.2 %collective-permute-start.9 = (s32[16]{0:T(128)S(1)}, s32[16]{0:T(128)S(1)}, u32[]{:S(2)}, u32[]{:S(2)}) collective-permute-start(s32[16]{0:T(128)S(1)} %copy-done.10), channel_id=1, source_target_pairs={{0,16},{16,0},{1,17},{17,1},{2,18},{18,2},{3,19},{19,3},{4,20},{20... | collective-permute-start | bytes 200 | tf_op jit(solution)/shard_map/ppermute | solution.py:149
  21.6 39.0 %copy-start.4 = (f32[2048]{0:T(1024)S(1)}, f32[2048]{0:T(1024)}, u32[]{:S(2)}) copy-start(f32[2048]{0:T(1024)} %param.16) | copy-start | bytes 24580
  22.0 0.9 copy-start.1
  42.5 12.8 %collective-permute-start.5 = (bf16[512,512]{1,0:T(8,128)(2,1)}, bf16[512,512]{1,0:T(8,128)(2,1)}, u32[]{:S(2)}, u32[]{:S(2)}) collective-permute-start(bf16[512,512]{1,0:T(8,128)(2,1)} %slice_bitcast_fusion.1), channel_id=1, source_target_pairs={{0,16},{16,0},{1,17},{17,1},{2,18},{18,2},{3,19},{19,3},{4,20},{20... | collective-permute-start | bytes 1572872 | tf_op jit(solution)/shard_map/ppermute | solution.py:149
  45.9 12.5 %collective-permute-start.7 = (bf16[512,512]{1,0:T(8,128)(2,1)}, bf16[512,512]{1,0:T(8,128)(2,1)}, u32[]{:S(2)}, u32[]{:S(2)}) collective-permute-start(bf16[512,512]{1,0:T(8,128)(2,1)} %slice_bitcast_fusion), channel_id=1, source_target_pairs={{0,2},{1,3},{2,0},{3,1},{4,6},{5,7},{6,4},{7,5},{8,10},{9,11},{10,... | collective-permute-start | bytes 1572872 | tf_op jit(solution)/shard_map/ppermute | solution.py:149
  46.5 14.0 %collective-permute-start.3 = (bf16[2,512,512]{2,1,0:T(8,128)(2,1)}, bf16[2,512,512]{2,1,0:T(8,128)(2,1)}, u32[]{:S(2)}, u32[]{:S(2)}) collective-permute-start(bf16[2,512,512]{2,1,0:T(8,128)(2,1)} %collective-permute-done.refs_2_), channel_id=1, source_target_pairs={{0,1},{1,0},{2,3},{3,2},{4,5},{5,4},{6,7},{7,6},{8,9},{9,8},{10,11... | collective-permute-start | bytes 3145736 | tf_op jit(solution)/shard_map/ppermute | solution.py:149
  46.6 13.9 %collective-permute-start.4 = (bf16[2,512,512]{2,1,0:T(8,128)(2,1)}, bf16[2,512,512]{2,1,0:T(8,128)(2,1)}, u32[]{:S(2)}, u32[]{:S(2)}) collective-permute-start(bf16[2,512,512]{2,1,0:T(8,128)(2,1)} %collective-permute-done.1.refs_4_), channel_id=1, source_target_pairs={{0,1},{1,0},{2,3},{3,2},{4,5},{5,4},{6,7},{7,6},{8,9},{9,8},{10,11... | collective-permute-start | bytes 3145736 | tf_op jit(solution)/shard_map/ppermute | solution.py:149
  55.3 4.4 %collective-permute-start.6 = (bf16[512,512]{1,0:T(8,128)(2,1)}, bf16[512,512]{1,0:T(8,128)(2,1)S(1)}, u32[]{:S(2)}, u32[]{:S(2)}) collective-permute-start(bf16[512,512]{1,0:T(8,128)(2,1)} %collective-permute-done.5.refs_6_), channel_id=1, source_target_pairs={{0,1},{1,0},{2,3},{3,2},{4,5},{5,4},{6,7},{7,6},{8,9},{9,8},{10,11... | collective-permute-start | bytes 1572872 | tf_op jit(solution)/shard_map/ppermute | solution.py:149
  58.4 2.1 %collective-permute-start.8 = (bf16[512,512]{1,0:T(8,128)(2,1)}, bf16[512,512]{1,0:T(8,128)(2,1)S(1)}, u32[]{:S(2)}, u32[]{:S(2)}) collective-permute-start(bf16[512,512]{1,0:T(8,128)(2,1)} %collective-permute-done.7.refs_8_), channel_id=1, source_target_pairs={{0,1},{1,0},{2,3},{3,2},{4,5},{5,4},{6,7},{7,6},{8,9},{9,8},{10,11... | collective-permute-start | bytes 1572872 | tf_op jit(solution)/shard_map/ppermute | solution.py:149
  75.5 24.9 %collective-permute-start.10 = (bf16[256,512]{1,0:T(8,128)(2,1)}, bf16[256,512]{1,0:T(8,128)(2,1)S(1)}, u32[]{:S(2)}, u32[]{:S(2)}) collective-permute-start(bf16[256,512]{1,0:T(8,128)(2,1)} %get-tuple-element.26.refs_0_), channel_id=1, source_target_pairs={{0,4},{4,0},{8,12},{12,8},{1,5},{5,1},{9,13},{13,9},{2,6},{6,2},{1... | collective-permute-start | bytes 786440 | tf_op jit(solution)/shard_map/ppermute | solution.py:149
  75.5 24.9 %collective-permute-start.11 = (bf16[256,512]{1,0:T(8,128)(2,1)}, bf16[256,512]{1,0:T(8,128)(2,1)S(1)}, u32[]{:S(2)}, u32[]{:S(2)}) collective-permute-start(bf16[256,512]{1,0:T(8,128)(2,1)} %get-tuple-element.26.refs_0_), channel_id=1, source_target_pairs={{0,8},{4,12},{8,0},{12,4},{1,9},{5,13},{9,1},{13,5},{2,10},{6,14},... | collective-permute-start | bytes 786440 | tf_op jit(solution)/shard_map/ppermute | solution.py:149
  94.6 20.5 %collective-permute-start.16 = (bf16[3,2,128,256]{3,2,1,0:T(8,128)(2,1)}, bf16[3,2,128,256]{3,2,1,0:T(8,128)(2,1)}, u32[]{:S(2)}, u32[]{:S(2)}) collective-permute-start(bf16[3,2,128,256]{3,2,1,0:T(8,128)(2,1)} %get-tuple-element.39), channel_id=1, source_target_pairs={{0,4},{4,8},{8,12},{1,5},{5,9},{9,13},{2,6},{6,10},{10,14},{3,7},{... | collective-permute-start | bytes 1179656 | tf_op jit(solution)/shard_map/ppermute | solution.py:28
  99.0 16.1 %collective-permute-start.17 = (bf16[3,2,128,256]{3,2,1,0:T(8,128)(2,1)}, bf16[3,2,128,256]{3,2,1,0:T(8,128)(2,1)}, u32[]{:S(2)}, u32[]{:S(2)}) collective-permute-start(bf16[3,2,128,256]{3,2,1,0:T(8,128)(2,1)} %get-tuple-element.40), channel_id=1, source_target_pairs={{4,0},{8,4},{12,8},{5,1},{9,5},{13,9},{6,2},{10,6},{14,10},{7,3},{... | collective-permute-start | bytes 1179656 | tf_op jit(solution)/shard_map/ppermute | solution.py:28
  100.3 10.0 %collective-permute-start.14 = (bf16[256,512]{1,0:T(8,128)(2,1)S(1)}, bf16[256,512]{1,0:T(8,128)(2,1)S(1)}, u32[]{:S(2)}, u32[]{:S(2)}) collective-permute-start(bf16[256,512]{1,0:T(8,128)(2,1)S(1)} %collective-permute-done.11.refs_2_), channel_id=1, source_target_pairs={{0,16},{16,0},{1,17},{17,1},{2,18},{18,2},{3,19},{19,3},{4,20},{20... | collective-permute-start | bytes 786440 | tf_op jit(solution)/shard_map/ppermute | solution.py:149
  101.9 27.6 %collective-permute-start.12 = (bf16[256,512]{1,0:T(8,128)(2,1)S(1)}, bf16[256,512]{1,0:T(8,128)(2,1)S(1)}, u32[]{:S(2)}, u32[]{:S(2)}) collective-permute-start(bf16[256,512]{1,0:T(8,128)(2,1)S(1)} %collective-permute-done.11.refs_2_), channel_id=1, source_target_pairs={{0,4},{4,0},{8,12},{12,8},{1,5},{5,1},{9,13},{13,9},{2,6},{6,2},{1... | collective-permute-start | bytes 786440 | tf_op jit(solution)/shard_map/ppermute | solution.py:149
  104.5 25.0 %collective-permute-start.13 = (bf16[256,512]{1,0:T(8,128)(2,1)S(1)}, bf16[256,512]{1,0:T(8,128)(2,1)}, u32[]{:S(2)}, u32[]{:S(2)}) collective-permute-start(bf16[256,512]{1,0:T(8,128)(2,1)S(1)} %collective-permute-done.10.refs_1_), channel_id=1, source_target_pairs={{0,16},{16,0},{1,17},{17,1},{2,18},{18,2},{3,19},{19,3},{4,20},{20... | collective-permute-start | bytes 786440 | tf_op jit(solution)/shard_map/ppermute | solution.py:149
  118.9 19.4 %copy-start.3 = (bf16[256,512]{1,0:T(8,128)(2,1)S(1)}, bf16[256,512]{1,0:T(8,128)(2,1)}, u32[]{:S(2)}) copy-start(bf16[256,512]{1,0:T(8,128)(2,1)} %get-tuple-element.26.refs_0_) | copy-start | bytes 786436
  118.9 13.3 %collective-permute-start.21 = (bf16[512,256]{1,0:T(8,128)(2,1)}, bf16[512,256]{1,0:T(8,128)(2,1)S(1)}, u32[]{:S(2)}, u32[]{:S(2)}) collective-permute-start(bf16[512,256]{1,0:T(8,128)(2,1)} %gated_sections.1), channel_id=1, source_target_pairs={{0,16},{16,0},{1,17},{17,1},{2,18},{18,2},{3,19},{19,3},{4,20},{20... | collective-permute-start | bytes 786440 | tf_op jit(solution)/shard_map/ppermute | solution.py:149
  120.4 11.8 %collective-permute-start.23 = (bf16[512,256]{1,0:T(8,128)(2,1)}, bf16[512,256]{1,0:T(8,128)(2,1)S(1)}, u32[]{:S(2)}, u32[]{:S(2)}) collective-permute-start(bf16[512,256]{1,0:T(8,128)(2,1)} %gated_sections.1), channel_id=1, source_target_pairs={{0,18},{1,19},{2,16},{3,17},{16,2},{17,3},{18,0},{19,1},{4,22},{5,... | collective-permute-start | bytes 786440 | tf_op jit(solution)/shard_map/ppermute | solution.py:157
  128.9 7.2 %collective-permute-start.19 = (bf16[512,256]{1,0:T(8,128)(2,1)}, bf16[512,256]{1,0:T(8,128)(2,1)S(1)}, u32[]{:S(2)}, u32[]{:S(2)}) collective-permute-start(bf16[512,256]{1,0:T(8,128)(2,1)} %late_sections.1.refs_8_), channel_id=1, source_target_pairs={{0,2},{1,3},{2,0},{3,1},{4,6},{5,7},{6,4},{7,5},{8,10},{9,11},{10,... | collective-permute-start | bytes 786440 | tf_op jit(solution)/shard_map/ppermute | solution.py:149
  129.5 6.6 %collective-permute-start.18 = (bf16[512,256]{1,0:T(8,128)(2,1)}, bf16[512,256]{1,0:T(8,128)(2,1)S(1)}, u32[]{:S(2)}, u32[]{:S(2)}) collective-permute-start(bf16[512,256]{1,0:T(8,128)(2,1)} %late_sections.1.refs_8_), channel_id=1, source_target_pairs={{0,1},{1,0},{2,3},{3,2},{4,5},{5,4},{6,7},{7,6},{8,9},{9,8},{10,11... | collective-permute-start | bytes 786440 | tf_op jit(solution)/shard_map/ppermute | solution.py:149
  129.5 8.7 %collective-permute-start.15 = (bf16[256,512]{1,0:T(8,128)(2,1)S(1)}, bf16[256,512]{1,0:T(8,128)(2,1)S(1)}, u32[]{:S(2)}, u32[]{:S(2)}) collective-permute-start(bf16[256,512]{1,0:T(8,128)(2,1)S(1)} %collective-permute-done.12.refs_3_), channel_id=1, source_target_pairs={{0,16},{16,0},{1,17},{17,1},{2,18},{18,2},{3,19},{19,3},{4,20},{20... | collective-permute-start | bytes 786440 | tf_op jit(solution)/shard_map/ppermute | solution.py:149
  132.2 6.0 %collective-permute-start.22 = (bf16[512,256]{1,0:T(8,128)(2,1)S(1)}, bf16[512,256]{1,0:T(8,128)(2,1)S(1)}, u32[]{:S(2)}, u32[]{:S(2)}) collective-permute-start(bf16[512,256]{1,0:T(8,128)(2,1)S(1)} %collective-permute-done.21.refs_12_), channel_id=1, source_target_pairs={{0,1},{1,0},{2,3},{3,2},{4,5},{5,4},{6,7},{7,6},{8,9},{9,8},{10,11... | collective-permute-start | bytes 786440 | tf_op jit(solution)/shard_map/ppermute | solution.py:149
  132.2 6.0 %collective-permute-start.24 = (bf16[512,256]{1,0:T(8,128)(2,1)S(1)}, bf16[512,256]{1,0:T(8,128)(2,1)S(1)}, u32[]{:S(2)}, u32[]{:S(2)}) collective-permute-start(bf16[512,256]{1,0:T(8,128)(2,1)S(1)} %collective-permute-done.23.refs_14_), channel_id=1, source_target_pairs={{0,1},{1,0},{2,3},{3,2},{4,5},{5,4},{6,7},{7,6},{8,9},{9,8},{10,11... | collective-permute-start | bytes 786440 | tf_op jit(solution)/shard_map/ppermute | solution.py:149
  136.1 2.1 %collective-permute-start.20 = (bf16[512,256]{1,0:T(8,128)(2,1)S(1)}, bf16[512,256]{1,0:T(8,128)(2,1)S(1)}, u32[]{:S(2)}, u32[]{:S(2)}) collective-permute-start(bf16[512,256]{1,0:T(8,128)(2,1)S(1)} %collective-permute-done.19.refs_10_), channel_id=1, source_target_pairs={{0,1},{1,0},{2,3},{3,2},{4,5},{5,4},{6,7},{7,6},{8,9},{9,8},{10,11... | collective-permute-start | bytes 786440 | tf_op jit(solution)/shard_map/ppermute | solution.py:149
  138.3 1.0 copy-start.2
Sparse Core Ops, SparseCore 0:
  9.2 66.2 all-gather.4
  77.0 33.2 all-gather.6

commit v5 on v4

--- a/solution.py
+++ b/solution.py
@@ -8,7 +8,7 @@
 from jax.sharding import PartitionSpec as P
 
 VMEM_LIMIT = 40 * 1024 * 1024
-WIDE = 56 * 1024 * 1024
+WIDE = 50 * 1024 * 1024
 SMALL = pl.CostEstimate(flops=1, bytes_accessed=1, transcendentals=0)
 
 
@@ -216,7 +216,7 @@
     )(place, gain.reshape(1, -1), *arrays)
 
 
-CUTS = 4
+CUTS = 2
 
 
 def fetch(normed, weight, count, order, held, kept, x_sems, w_sems):

time: 150 us -> 148 us (0.987)
  Pallas kernels: 46.2 us -> 40.7 us
  local copies, waits for them, and re-layouts: 10.8 us -> 14.4 us
    unnamed x22 -> x38, local copies, waits for them, and re-layouts: 3.39 us -> 6.97 us
    ppermute x22, waiting for transfers between devices: 36.5 us -> 39.2 us  [flip(): return lax.ppermute(block, axis, [(i, i ^ bit) for i in range(count)])]
    pallas_call x1, Pallas kernels: 7.06 us -> 5.26 us  [late_sections(): pl.pallas_call(functools.partial(late_kernel, g), grid=(strands,), in_spe...]
  transfers between devices with their start and end apart: 27 -> 27, of which waited for: 9 -> 11; matrix products, arithmetic and copies ran while one was open for 8% -> 8% of each run, Pallas kernels for 28% -> 25%
where the time goes in v5:
time: 148 us; the launch traced here: 147 us
  waiting for transfers between devices  49.1 us (33%)
  Pallas kernels  40.7 us (28%)
  starting transfers between devices  24.5 us (17%)
  local copies, waits for them, and re-layouts  14.4 us (10%)
  between operations  13.7 us (9%)
  other arithmetic  2.54 us (2%)
  matrix products  2.43 us (2%)
    ppermute x22, waiting for transfers between devices, flip(): return lax.ppermute(block, axis, [(i, i ^ bit) for i in range(count)])  39.2 us
    ppermute x22, starting transfers between devices, flip(): return lax.ppermute(block, axis, [(i, i ^ bit) for i in range(count)])  17.9 us
    pallas_call x1, Pallas kernels, early_sections(): pl.pallas_call(early_kernel, grid=(strands, groups), in_specs=[pl.BlockSp...  16.5 us
    pallas_call x1, Pallas kernels, norm_all(): pl.pallas_call(functools.partial(norm_kernel, layout), grid_spec=pltpu.Pr...  8.66 us
    unnamed x38, local copies, waits for them, and re-layouts  6.97 us
    pallas_call x1, Pallas kernels, late_sections(): pl.pallas_call(functools.partial(late_kernel, g), grid=(strands,), in_spe...  5.26 us
    ppermute x2, starting transfers between devices, shifted(): return lax.ppermute(value, axis, pairs)  5.02 us
    all_gather x1, waiting for transfers between devices, paired(): early = lax.all_gather(columns[:sections], 'ctx', axis=0)  4.99 us
  transfers between devices with their start and end apart: 27, of which 11 were waited for; matrix products, arithmetic and copies ran while one was open for 8% of the time, Pallas kernels for 25%

profile of v5, /device:TPU:0, one launch (start us, length us, event | category | flops | bytes accessed | tf_op | source)
XLA Modules:
  0.0 147.4 jit_solution(11501092012501949538)
XLA Ops:
  6.6 1.5 %copy-done = bf16[4,512,512]{2,1,0:T(8,128)(2,1)S(1)} copy-done((bf16[4,512,512]{2,1,0:T(8,128)(2,1)S(1)}, bf16[4,512,512]{2,1,0:T(8,128)(2,1)}, u32[]{:S(2)}) %copy-start) | copy-done | bytes 2097176
  8.1 1.0 constant_dynamic-slice_fusion
  9.2 1.2 fusion.3
  10.4 1.3 fusion.2
  11.6 1.3 pad_maximum_fusion.refs_0_
  12.9 3.0 %collective-permute-start = (bf16[2,512,512]{2,1,0:T(8,128)(2,1)S(1)}, bf16[2,512,512]{2,1,0:T(8,128)(2,1)}, u32[]{:S(2)}, u32[]{:S(2)}) collective-permute-start(bf16[2,512,512]{2,1,0:T(8,128)(2,1)S(1)} %pad_maximum_fusion.refs_0_), channel_id=1, source_target_pairs={{0,2},{1,3},{2,0},{3,1},{4,6},{5,7},{6,4},{7,5},{8,10},{9,11},{10,... | collective-permute-start | bytes 3145736 | tf_op jit(solution)/shard_map/ppermute | solution.py:149
  16.0 1.5 %collective-permute-start.1 = (bf16[2,512,512]{2,1,0:T(8,128)(2,1)S(1)}, bf16[2,512,512]{2,1,0:T(8,128)(2,1)}, u32[]{:S(2)}, u32[]{:S(2)}) collective-permute-start(bf16[2,512,512]{2,1,0:T(8,128)(2,1)S(1)} %pad_maximum_fusion.refs_0_), channel_id=1, source_target_pairs={{0,16},{16,0},{1,17},{17,1},{2,18},{18,2},{3,19},{19,3},{4,20},{20... | collective-permute-start | bytes 3145736 | tf_op jit(solution)/shard_map/ppermute | solution.py:149
  17.5 0.5 collective-permute-start.9
  18.0 0.7 fusion.9
  19.0 0.7 constant_dynamic-slice_fusion.3
  19.7 1.8 %constant_dynamic-slice_fusion.1 = (bf16[256,512]{1,0:T(8,128)(2,1)S(1)}, bf16[256,512]{1,0:T(8,128)(2,1)}) fusion(bf16[512,512]{1,0:T(8,128)(2,1)} %param.19, s32[]{:T(128)S(6)} %select_n.18, s32[]{:T(128)S(6)} %select_n.15), kind=kLoop, calls=%fused_computation.32 | loop fusion | bytes 1048584 | tf_op jit(solution)/shard_map/dynamic_slice | solution.py:700
  22.1 0.9 copy-done.2
  22.9 17.8 %collective-permute-done.9 = s32[16]{0:T(128)S(1)} collective-permute-done((s32[16]{0:T(128)S(1)}, s32[16]{0:T(128)S(1)}, u32[]{:S(2)}, u32[]{:S(2)}) %collective-permute-start.9) | collective-permute-done | bytes 96 | tf_op jit(solution)/shard_map/ppermute | solution.py:149
  40.7 1.9 %slice_bitcast_fusion.1 = bf16[512,512]{1,0:T(8,128)(2,1)} fusion(bf16[2,512,512]{2,1,0:T(8,128)(2,1)} %collective-permute-done.refs_2_), kind=kLoop, calls=%fused_computation.10 | loop fusion | bytes 1048576 | tf_op jit(solution)/shard_map/squeeze | solution.py:677
  42.6 1.5 %collective-permute-start.5 = (bf16[512,512]{1,0:T(8,128)(2,1)}, bf16[512,512]{1,0:T(8,128)(2,1)}, u32[]{:S(2)}, u32[]{:S(2)}) collective-permute-start(bf16[512,512]{1,0:T(8,128)(2,1)} %slice_bitcast_fusion.1), channel_id=1, source_target_pairs={{0,16},{16,0},{1,17},{17,1},{2,18},{18,2},{3,19},{19,3},{4,20},{20... | collective-permute-start | bytes 1572872 | tf_op jit(solution)/shard_map/ppermute | solution.py:149
  44.1 1.9 %slice_bitcast_fusion = bf16[512,512]{1,0:T(8,128)(2,1)} fusion(bf16[2,512,512]{2,1,0:T(8,128)(2,1)} %collective-permute-done.1.refs_4_), kind=kLoop, calls=%fused_computation.9 | loop fusion | bytes 1048576 | tf_op jit(solution)/shard_map/squeeze | solution.py:677
  46.0 0.5 collective-permute-start.7
  46.7 0.5 collective-permute-start.4
  47.3 8.1 %collective-permute-done.5.refs_6_ = bf16[512,512]{1,0:T(8,128)(2,1)} collective-permute-done((bf16[512,512]{1,0:T(8,128)(2,1)}, bf16[512,512]{1,0:T(8,128)(2,1)}, u32[]{:S(2)}, u32[]{:S(2)}) %collective-permute-start.5) | collective-permute-done | bytes 524320 | tf_op jit(solution)/shard_map/ppermute | solution.py:149
  55.4 3.1 %collective-permute-done.7.refs_8_ = bf16[512,512]{1,0:T(8,128)(2,1)} collective-permute-done((bf16[512,512]{1,0:T(8,128)(2,1)}, bf16[512,512]{1,0:T(8,128)(2,1)}, u32[]{:S(2)}, u32[]{:S(2)}) %collective-permute-start.7) | collective-permute-done | bytes 524320 | tf_op jit(solution)/shard_map/ppermute | solution.py:149
  58.8 1.8 %collective-permute-done.8.refs_9_ = bf16[512,512]{1,0:T(8,128)(2,1)S(1)} collective-permute-done((bf16[512,512]{1,0:T(8,128)(2,1)}, bf16[512,512]{1,0:T(8,128)(2,1)S(1)}, u32[]{:S(2)}, u32[]{:S(2)}) %collective-permute-start.8) | collective-permute-done | bytes 524320 | tf_op jit(solution)/shard_map/ppermute | solution.py:149
  60.6 1.2 copy-done.10
  61.9 8.7 %norm.1.normed = bf16[2,2,512,2048]{3,2,1,0:T(8,128)(2,1)} custom-call(s32[2]{0:T(128)S(1)} %pad_add_fusion.2.place.spots, f32[1,2048]{1,0:T(1,128)S(1)} %bitcast.30, bf16[2,512,512]{2,1,0:T(8,128)(2,1)S(1)} %copy-done.10, bf16[2,512,512]{2,1,0:T(8,128)(2,1)} %collective-permute-done.2.refs_1_, bf16[2,512,512]{2,1,0:T(8,128)(2,1)} %collective-permute-done.refs_2_, ...), custom_call_target="tpu_custom_call" | custom-call | flops 1 | bytes 1 | tf_op jit(solution)/shard_map/norm/pallas_call | solution.py:201
  70.5 5.0 %all-gather.5.cloned.1.call-done = bf16[12,512,256]{2,1,0:T(8,128)(2,1)} async-done(((bf16[3,512,256]{2,1,0:T(8,128)(2,1)}), bf16[12,512,256]{2,1,0:T(8,128)(2,1)}) %all-gather.5.cloned.1.call-update) | async-done | bytes 3145744 | tf_op jit(solution)/shard_map/all_gather | solution.py:661
  75.5 1.3 collective-permute-start.11
  76.8 1.1 copy-done.3
  77.9 16.5 %early_sections.1 = (bf16[2,2,4,128,256]{4,3,2,1,0:T(8,128)(2,1)S(1)}, f32[2,2,3,128,256]{4,3,2,1,0:T(8,128)}, bf16[3,2,128,256]{3,2,1,0:T(8,128)(2,1)}, bf16[3,2,128,256]{3,2,1,0:T(8,128)(2,1)}) custom-call(bf16[2,2,512,2048]{3,2,1,0:T(8,128)(2,1)} %norm.1.normed, bf16[4,3,512,256]{3,2,1,0:T(8,128)(2,1)} %bitcast.31, ...), custom_call_target="tpu_custom_call" | custom-call | flops 1 | bytes 1 | tf_op jit(solution)/shard_map/early_sections/pallas_call | solution.py:380
  94.4 0.9 copy-done.7
  95.3 3.7 %collective-permute-start.16 = (bf16[3,2,128,256]{3,2,1,0:T(8,128)(2,1)}, bf16[3,2,128,256]{3,2,1,0:T(8,128)(2,1)S(1)}, u32[]{:S(2)}, u32[]{:S(2)}) collective-permute-start(bf16[3,2,128,256]{3,2,1,0:T(8,128)(2,1)} %get-tuple-element.39), channel_id=1, source_target_pairs={{0,4},{4,8},{8,12},{1,5},{5,9},{9,13},{2,6},{6,10},{10,14},{3,7},{... | collective-permute-start | bytes 1179656 | tf_op jit(solution)/shard_map/ppermute | solution.py:28
  99.1 1.3 collective-permute-start.17
  100.4 1.5 %collective-permute-start.14 = (bf16[256,512]{1,0:T(8,128)(2,1)}, bf16[256,512]{1,0:T(8,128)(2,1)S(1)}, u32[]{:S(2)}, u32[]{:S(2)}) collective-permute-start(bf16[256,512]{1,0:T(8,128)(2,1)} %collective-permute-done.11.refs_2_), channel_id=1, source_target_pairs={{0,16},{16,0},{1,17},{17,1},{2,18},{18,2},{3,19},{19,3},{4,20},{20... | collective-permute-start | bytes 786440 | tf_op jit(solution)/shard_map/ppermute | solution.py:149
  101.9 2.6 %collective-permute-start.12 = (bf16[256,512]{1,0:T(8,128)(2,1)}, bf16[256,512]{1,0:T(8,128)(2,1)}, u32[]{:S(2)}, u32[]{:S(2)}) collective-permute-start(bf16[256,512]{1,0:T(8,128)(2,1)} %collective-permute-done.11.refs_2_), channel_id=1, source_target_pairs={{0,4},{4,0},{8,12},{12,8},{1,5},{5,1},{9,13},{13,9},{2,6},{6,2},{1... | collective-permute-start | bytes 786440 | tf_op jit(solution)/shard_map/ppermute | solution.py:149
  104.6 0.6 collective-permute-start.13
  105.1 4.3 %all-gather.7.cloned.1.call-done = bf16[4,512,256]{2,1,0:T(8,128)(2,1)} async-done(((bf16[1,512,256]{2,1,0:T(8,128)(2,1)}), bf16[4,512,256]{2,1,0:T(8,128)(2,1)}) %all-gather.7.cloned.1.call-update) | async-done | bytes 1048592 | tf_op jit(solution)/shard_map/all_gather | solution.py:690
  109.9 1.2 copy-done.5
  111.2 3.3 %last_gate.1 = f32[2,512,256]{2,1,0:T(8,128)S(1)} custom-call(bf16[2,2,512,2048]{3,2,1,0:T(8,128)(2,1)} %norm.1.normed, bf16[4,1,512,256]{3,2,1,0:T(8,128)(2,1)S(1)} %bitcast.28), custom_call_target="tpu_custom_call" | custom-call | flops 1 | bytes 1 | tf_op jit(solution)/shard_map/last_gate/pallas_call | solution.py:503
  114.5 0.5 collective-permute-done.17.refs_1_
  115.0 2.7 %gated_sections.1 = bf16[512,256]{1,0:T(8,128)(2,1)S(1)} custom-call(f32[2,512,256]{2,1,0:T(8,128)S(1)} %last_gate.1, bf16[2,2,4,128,256]{4,3,2,1,0:T(8,128)(2,1)S(1)} %copy-done.8, f32[2,2,3,128,256]{4,3,2,1,0:T(8,128)} %get-tuple-element.38.gates, bf16[3,2,2,128,256]{4,3,2,1,0:T(8,128)(2,1)S(1)} %copy-done.4, bf16[2,2,4,128,256]{4,3,2,1,0:T(8,128)(2,1)} %copy-done.1, ...), custom_call_target="tpu_custom_call" | custom-call | flops 1 | bytes 1 | tf_op jit(solution)/shard_map/gated_sections/pallas_call | solution.py:559
  117.7 1.5 %collective-permute-start.21 = (bf16[512,256]{1,0:T(8,128)(2,1)S(1)}, bf16[512,256]{1,0:T(8,128)(2,1)S(1)}, u32[]{:S(2)}, u32[]{:S(2)}) collective-permute-start(bf16[512,256]{1,0:T(8,128)(2,1)S(1)} %gated_sections.1), channel_id=1, source_target_pairs={{0,16},{16,0},{1,17},{17,1},{2,18},{18,2},{3,19},{19,3},{4,20},{20... | collective-permute-start | bytes 786440 | tf_op jit(solution)/shard_map/ppermute | solution.py:149
  119.3 1.5 collective-permute-start.23
  120.7 5.3 %late_sections.1.refs_8_ = bf16[512,256]{1,0:T(8,128)(2,1)S(1)} custom-call(bf16[2,2,512,2048]{3,2,1,0:T(8,128)(2,1)} %norm.1.normed, bf16[4,1,512,256]{3,2,1,0:T(8,128)(2,1)S(1)} %bitcast.29, bf16[2,2,4,128,256]{4,3,2,1,0:T(8,128)(2,1)S(1)} %copy-done.8, f32[2,2,3,128,256]{4,3,2,1,0:T(8,128)} %get-tuple-element.38.gates, ...), custom_call_target="tpu_custom_call" | custom-call | flops 1 | bytes 1 | tf_op jit(solution)/shard_map/late_sections/pallas_call | solution.py:464
  126.0 0.6 collective-permute-start.19
  126.6 1.5 %collective-permute-start.15 = (bf16[256,512]{1,0:T(8,128)(2,1)}, bf16[256,512]{1,0:T(8,128)(2,1)S(1)}, u32[]{:S(2)}, u32[]{:S(2)}) collective-permute-start(bf16[256,512]{1,0:T(8,128)(2,1)} %collective-permute-done.12.refs_3_), channel_id=1, source_target_pairs={{0,16},{16,0},{1,17},{17,1},{2,18},{18,2},{3,19},{19,3},{4,20},{20... | collective-permute-start | bytes 786440 | tf_op jit(solution)/shard_map/ppermute | solution.py:149
  128.2 3.8 %collective-permute-done.21.refs_12_ = bf16[512,256]{1,0:T(8,128)(2,1)S(1)} collective-permute-done((bf16[512,256]{1,0:T(8,128)(2,1)S(1)}, bf16[512,256]{1,0:T(8,128)(2,1)S(1)}, u32[]{:S(2)}, u32[]{:S(2)}) %collective-permute-start.21) | collective-permute-done | bytes 262176 | tf_op jit(solution)/shard_map/ppermute | solution.py:149
  131.9 0.5 collective-permute-start.24
  132.5 0.6 collective-permute-done.19.refs_10_
  133.1 3.5 %collective-permute-done.15.refs_7_ = bf16[256,512]{1,0:T(8,128)(2,1)S(1)} collective-permute-done((bf16[256,512]{1,0:T(8,128)(2,1)}, bf16[256,512]{1,0:T(8,128)(2,1)S(1)}, u32[]{:S(2)}, u32[]{:S(2)}) %collective-permute-start.15) | collective-permute-done | bytes 262176 | tf_op jit(solution)/shard_map/ppermute | solution.py:149
  136.6 3.9 %out.1 = bf16[512,512]{1,0:T(8,128)(2,1)} custom-call(s32[2]{0:T(128)S(1)} %pad_add_fusion.2.place.spots, bf16[256,512]{1,0:T(8,128)(2,1)S(1)} %copy-done.11, bf16[256,512]{1,0:T(8,128)(2,1)} %collective-permute-done.10.refs_1_, bf16[256,512]{1,0:T(8,128)(2,1)} %collective-permute-done.11.refs_2_, bf16[256,512]{1,0:T(8,128)(2,1)} %collective-permute-done.12.refs_3_, ...), custom_call_target="tpu_custom_call" | custom-call | flops 1 | bytes 1 | tf_op jit(solution)/shard_map/out/pallas_call | solution.py:605
  (81 shorter events, 1.9 us)
Async XLA Ops:
  6.5 1.6 %copy-start = (bf16[4,512,512]{2,1,0:T(8,128)(2,1)S(1)}, bf16[4,512,512]{2,1,0:T(8,128)(2,1)}, u32[]{:S(2)}) copy-start(bf16[4,512,512]{2,1,0:T(8,128)(2,1)} %param.17) | copy-start | bytes 6291460
  6.5 2.6 %copy-start.16 = (s32[512]{0:T(512)S(1)}, s32[512]{0:T(512)}, u32[]{:S(2)}) copy-start(s32[512]{0:T(512)} %param.12) | copy-start | bytes 6148
  6.5 2.6 %copy-start.15 = (bf16[4,512]{1,0:T(4,128)(2,1)S(1)}, bf16[4,512]{1,0:T(4,128)(2,1)}, u32[]{:S(2)}) copy-start(bf16[4,512]{1,0:T(4,128)(2,1)} %param.15) | copy-start | bytes 12292
  6.5 2.6 %copy-start.13 = (bf16[512,512]{1,0:T(8,128)(2,1)S(1)}, bf16[512,512]{1,0:T(8,128)(2,1)}, u32[]{:S(2)}) copy-start(bf16[512,512]{1,0:T(8,128)(2,1)} %param.10) | copy-start | bytes 1572868
  6.5 3.8 %copy-start.14 = (bf16[512,512]{1,0:T(8,128)(2,1)S(1)}, bf16[512,512]{1,0:T(8,128)(2,1)}, u32[]{:S(2)}) copy-start(bf16[512,512]{1,0:T(8,128)(2,1)} %param.11) | copy-start | bytes 1572868
  6.5 3.8 %copy-start.17 = (s32[4]{0:T(128)S(1)}, s32[4]{0:T(128)}, u32[]{:S(2)}) copy-start(s32[4]{0:T(128)} %param.13) | copy-start | bytes 52
  6.6 68.9 %all-gather.5.cloned.1.call-start = ((), (), s32[]{:S(2)}) async-start(), calls=%async_computation | async-start | bytes 3932160 | tf_op jit(solution)/shard_map/all_gather | solution.py:661
  9.1 8.4 %copy-start.18 = (s32[16]{0:T(128)S(1)}, s32[16]{0:T(128)}, u32[]{:S(2)}) copy-start(s32[16]{0:T(128)} %param.14) | copy-start | bytes 196
  9.1 100.3 %all-gather.7.cloned.1.call-start = ((), (), s32[]{:S(2)}) async-start(), calls=%async_computation.1 | async-start | bytes 1310720 | tf_op jit(solution)/shard_map/all_gather | solution.py:690
  12.9 33.0 %copy-start.9 = (bf16[2,512,512]{2,1,0:T(8,128)(2,1)}, bf16[2,512,512]{2,1,0:T(8,128)(2,1)S(1)}, u32[]{:S(2)}) copy-start(bf16[2,512,512]{2,1,0:T(8,128)(2,1)S(1)} %pad_maximum_fusion.refs_0_) | copy-start | bytes 3145732
  12.9 27.7 %collective-permute-start = (bf16[2,512,512]{2,1,0:T(8,128)(2,1)S(1)}, bf16[2,512,512]{2,1,0:T(8,128)(2,1)}, u32[]{:S(2)}, u32[]{:S(2)}) collective-permute-start(bf16[2,512,512]{2,1,0:T(8,128)(2,1)S(1)} %pad_maximum_fusion.refs_0_), channel_id=1, source_target_pairs={{0,2},{1,3},{2,0},{3,1},{4,6},{5,7},{6,4},{7,5},{8,10},{9,11},{10,... | collective-permute-start | bytes 3145736 | tf_op jit(solution)/shard_map/ppermute | solution.py:149
  16.0 24.7 %collective-permute-start.1 = (bf16[2,512,512]{2,1,0:T(8,128)(2,1)S(1)}, bf16[2,512,512]{2,1,0:T(8,128)(2,1)}, u32[]{:S(2)}, u32[]{:S(2)}) collective-permute-start(bf16[2,512,512]{2,1,0:T(8,128)(2,1)S(1)} %pad_maximum_fusion.refs_0_), channel_id=1, source_target_pairs={{0,16},{16,0},{1,17},{17,1},{2,18},{18,2},{3,19},{19,3},{4,20},{20... | collective-permute-start | bytes 3145736 | tf_op jit(solution)/shard_map/ppermute | solution.py:149
  17.5 23.2 %collective-permute-start.2 = (bf16[2,512,512]{2,1,0:T(8,128)(2,1)S(1)}, bf16[2,512,512]{2,1,0:T(8,128)(2,1)}, u32[]{:S(2)}, u32[]{:S(2)}) collective-permute-start(bf16[2,512,512]{2,1,0:T(8,128)(2,1)S(1)} %pad_maximum_fusion.refs_0_), channel_id=1, source_target_pairs={{0,1},{1,0},{2,3},{3,2},{4,5},{5,4},{6,7},{7,6},{8,9},{9,8},{10,11... | collective-permute-start | bytes 3145736 | tf_op jit(solution)/shard_map/ppermute | solution.py:149
  17.5 23.2 %collective-permute-start.9 = (s32[16]{0:T(128)S(1)}, s32[16]{0:T(128)S(1)}, u32[]{:S(2)}, u32[]{:S(2)}) collective-permute-start(s32[16]{0:T(128)S(1)} %copy-done.18), channel_id=1, source_target_pairs={{0,16},{16,0},{1,17},{17,1},{2,18},{18,2},{3,19},{19,3},{4,20},{20... | collective-permute-start | bytes 200 | tf_op jit(solution)/shard_map/ppermute | solution.py:149
  21.6 39.0 %copy-start.12 = (f32[2048]{0:T(1024)S(1)}, f32[2048]{0:T(1024)}, u32[]{:S(2)}) copy-start(f32[2048]{0:T(1024)} %param.16) | copy-start | bytes 24580
  22.0 0.9 copy-start.2
  42.6 12.8 %collective-permute-start.5 = (bf16[512,512]{1,0:T(8,128)(2,1)}, bf16[512,512]{1,0:T(8,128)(2,1)}, u32[]{:S(2)}, u32[]{:S(2)}) collective-permute-start(bf16[512,512]{1,0:T(8,128)(2,1)} %slice_bitcast_fusion.1), channel_id=1, source_target_pairs={{0,16},{16,0},{1,17},{17,1},{2,18},{18,2},{3,19},{19,3},{4,20},{20... | collective-permute-start | bytes 1572872 | tf_op jit(solution)/shard_map/ppermute | solution.py:149
  46.0 12.5 %collective-permute-start.7 = (bf16[512,512]{1,0:T(8,128)(2,1)}, bf16[512,512]{1,0:T(8,128)(2,1)}, u32[]{:S(2)}, u32[]{:S(2)}) collective-permute-start(bf16[512,512]{1,0:T(8,128)(2,1)} %slice_bitcast_fusion), channel_id=1, source_target_pairs={{0,2},{1,3},{2,0},{3,1},{4,6},{5,7},{6,4},{7,5},{8,10},{9,11},{10,... | collective-permute-start | bytes 1572872 | tf_op jit(solution)/shard_map/ppermute | solution.py:149
  46.6 14.0 %collective-permute-start.3 = (bf16[2,512,512]{2,1,0:T(8,128)(2,1)}, bf16[2,512,512]{2,1,0:T(8,128)(2,1)}, u32[]{:S(2)}, u32[]{:S(2)}) collective-permute-start(bf16[2,512,512]{2,1,0:T(8,128)(2,1)} %collective-permute-done.refs_2_), channel_id=1, source_target_pairs={{0,1},{1,0},{2,3},{3,2},{4,5},{5,4},{6,7},{7,6},{8,9},{9,8},{10,11... | collective-permute-start | bytes 3145736 | tf_op jit(solution)/shard_map/ppermute | solution.py:149
  46.7 13.9 %collective-permute-start.4 = (bf16[2,512,512]{2,1,0:T(8,128)(2,1)}, bf16[2,512,512]{2,1,0:T(8,128)(2,1)}, u32[]{:S(2)}, u32[]{:S(2)}) collective-permute-start(bf16[2,512,512]{2,1,0:T(8,128)(2,1)} %collective-permute-done.1.refs_4_), channel_id=1, source_target_pairs={{0,1},{1,0},{2,3},{3,2},{4,5},{5,4},{6,7},{7,6},{8,9},{9,8},{10,11... | collective-permute-start | bytes 3145736 | tf_op jit(solution)/shard_map/ppermute | solution.py:149
  55.4 3.4 %collective-permute-start.6 = (bf16[512,512]{1,0:T(8,128)(2,1)}, bf16[512,512]{1,0:T(8,128)(2,1)S(1)}, u32[]{:S(2)}, u32[]{:S(2)}) collective-permute-start(bf16[512,512]{1,0:T(8,128)(2,1)} %collective-permute-done.5.refs_6_), channel_id=1, source_target_pairs={{0,1},{1,0},{2,3},{3,2},{4,5},{5,4},{6,7},{7,6},{8,9},{9,8},{10,11... | collective-permute-start | bytes 1572872 | tf_op jit(solution)/shard_map/ppermute | solution.py:149
  58.5 2.1 %collective-permute-start.8 = (bf16[512,512]{1,0:T(8,128)(2,1)}, bf16[512,512]{1,0:T(8,128)(2,1)S(1)}, u32[]{:S(2)}, u32[]{:S(2)}) collective-permute-start(bf16[512,512]{1,0:T(8,128)(2,1)} %collective-permute-done.7.refs_8_), channel_id=1, source_target_pairs={{0,1},{1,0},{2,3},{3,2},{4,5},{5,4},{6,7},{7,6},{8,9},{9,8},{10,11... | collective-permute-start | bytes 1572872 | tf_op jit(solution)/shard_map/ppermute | solution.py:149
  58.8 18.0 %copy-start.1 = (bf16[2,2,4,128,256]{4,3,2,1,0:T(8,128)(2,1)}, bf16[2,2,4,128,256]{4,3,2,1,0:T(8,128)(2,1)S(1)}, u32[]{:S(2)}) copy-start(bf16[2,2,4,128,256]{4,3,2,1,0:T(8,128)(2,1)S(1)} %compare_convert_fusion.mask) | copy-start | bytes 3145732
  60.6 1.2 copy-start.10
  75.5 24.9 %collective-permute-start.10 = (bf16[256,512]{1,0:T(8,128)(2,1)}, bf16[256,512]{1,0:T(8,128)(2,1)}, u32[]{:S(2)}, u32[]{:S(2)}) collective-permute-start(bf16[256,512]{1,0:T(8,128)(2,1)} %get-tuple-element.26.refs_0_), channel_id=1, source_target_pairs={{0,4},{4,0},{8,12},{12,8},{1,5},{5,1},{9,13},{13,9},{2,6},{6,2},{1... | collective-permute-start | bytes 786440 | tf_op jit(solution)/shard_map/ppermute | solution.py:149
  75.5 24.9 %collective-permute-start.11 = (bf16[256,512]{1,0:T(8,128)(2,1)}, bf16[256,512]{1,0:T(8,128)(2,1)}, u32[]{:S(2)}, u32[]{:S(2)}) collective-permute-start(bf16[256,512]{1,0:T(8,128)(2,1)} %get-tuple-element.26.refs_0_), channel_id=1, source_target_pairs={{0,8},{4,12},{8,0},{12,4},{1,9},{5,13},{9,1},{13,5},{2,10},{6,14},... | collective-permute-start | bytes 786440 | tf_op jit(solution)/shard_map/ppermute | solution.py:149
  76.8 1.1 copy-start.3
  94.4 1.0 copy-start.7
  95.3 19.1 %collective-permute-start.16 = (bf16[3,2,128,256]{3,2,1,0:T(8,128)(2,1)}, bf16[3,2,128,256]{3,2,1,0:T(8,128)(2,1)S(1)}, u32[]{:S(2)}, u32[]{:S(2)}) collective-permute-start(bf16[3,2,128,256]{3,2,1,0:T(8,128)(2,1)} %get-tuple-element.39), channel_id=1, source_target_pairs={{0,4},{4,8},{8,12},{1,5},{5,9},{9,13},{2,6},{6,10},{10,14},{3,7},{... | collective-permute-start | bytes 1179656 | tf_op jit(solution)/shard_map/ppermute | solution.py:28
  99.1 15.9 %collective-permute-start.17 = (bf16[3,2,128,256]{3,2,1,0:T(8,128)(2,1)}, bf16[3,2,128,256]{3,2,1,0:T(8,128)(2,1)S(1)}, u32[]{:S(2)}, u32[]{:S(2)}) collective-permute-start(bf16[3,2,128,256]{3,2,1,0:T(8,128)(2,1)} %get-tuple-element.40), channel_id=1, source_target_pairs={{4,0},{8,4},{12,8},{5,1},{9,5},{13,9},{6,2},{10,6},{14,10},{7,3},{... | collective-permute-start | bytes 1179656 | tf_op jit(solution)/shard_map/ppermute | solution.py:28
  100.4 9.5 %collective-permute-start.14 = (bf16[256,512]{1,0:T(8,128)(2,1)}, bf16[256,512]{1,0:T(8,128)(2,1)S(1)}, u32[]{:S(2)}, u32[]{:S(2)}) collective-permute-start(bf16[256,512]{1,0:T(8,128)(2,1)} %collective-permute-done.11.refs_2_), channel_id=1, source_target_pairs={{0,16},{16,0},{1,17},{17,1},{2,18},{18,2},{3,19},{19,3},{4,20},{20... | collective-permute-start | bytes 786440 | tf_op jit(solution)/shard_map/ppermute | solution.py:149
  101.9 24.7 %collective-permute-start.12 = (bf16[256,512]{1,0:T(8,128)(2,1)}, bf16[256,512]{1,0:T(8,128)(2,1)}, u32[]{:S(2)}, u32[]{:S(2)}) collective-permute-start(bf16[256,512]{1,0:T(8,128)(2,1)} %collective-permute-done.11.refs_2_), channel_id=1, source_target_pairs={{0,4},{4,0},{8,12},{12,8},{1,5},{5,1},{9,13},{13,9},{2,6},{6,2},{1... | collective-permute-start | bytes 786440 | tf_op jit(solution)/shard_map/ppermute | solution.py:149
  104.6 22.0 %collective-permute-start.13 = (bf16[256,512]{1,0:T(8,128)(2,1)}, bf16[256,512]{1,0:T(8,128)(2,1)}, u32[]{:S(2)}, u32[]{:S(2)}) collective-permute-start(bf16[256,512]{1,0:T(8,128)(2,1)} %collective-permute-done.10.refs_1_), channel_id=1, source_target_pairs={{0,16},{16,0},{1,17},{17,1},{2,18},{18,2},{3,19},{19,3},{4,20},{20... | collective-permute-start | bytes 786440 | tf_op jit(solution)/shard_map/ppermute | solution.py:149
  109.9 1.2 copy-start.5
  111.2 3.8 %copy-start.4 = (bf16[3,2,2,128,256]{4,3,2,1,0:T(8,128)(2,1)S(1)}, bf16[3,2,2,128,256]{4,3,2,1,0:T(8,128)(2,1)}, u32[]{:S(2)}) copy-start(bf16[3,2,2,128,256]{4,3,2,1,0:T(8,128)(2,1)} %copy-done.2) | copy-start | bytes 2359300
  111.2 3.8 %copy-start.8 = (bf16[2,2,4,128,256]{4,3,2,1,0:T(8,128)(2,1)S(1)}, bf16[2,2,4,128,256]{4,3,2,1,0:T(8,128)(2,1)}, u32[]{:S(2)}) copy-start(bf16[2,2,4,128,256]{4,3,2,1,0:T(8,128)(2,1)} %copy-done.7) | copy-start | bytes 3145732
  115.0 5.7 %copy-start.6 = (bf16[4,512,256]{2,1,0:T(8,128)(2,1)S(1)}, bf16[4,512,256]{2,1,0:T(8,128)(2,1)}, u32[]{:S(2)}) copy-start(bf16[4,512,256]{2,1,0:T(8,128)(2,1)} %all-gather.7.cloned.1.call-done) | copy-start | bytes 3145732
  117.7 18.9 %copy-start.11 = (bf16[256,512]{1,0:T(8,128)(2,1)S(1)}, bf16[256,512]{1,0:T(8,128)(2,1)}, u32[]{:S(2)}) copy-start(bf16[256,512]{1,0:T(8,128)(2,1)} %get-tuple-element.26.refs_0_) | copy-start | bytes 786436
  117.7 14.2 %collective-permute-start.21 = (bf16[512,256]{1,0:T(8,128)(2,1)S(1)}, bf16[512,256]{1,0:T(8,128)(2,1)S(1)}, u32[]{:S(2)}, u32[]{:S(2)}) collective-permute-start(bf16[512,256]{1,0:T(8,128)(2,1)S(1)} %gated_sections.1), channel_id=1, source_target_pairs={{0,16},{16,0},{1,17},{17,1},{2,18},{18,2},{3,19},{19,3},{4,20},{20... | collective-permute-start | bytes 786440 | tf_op jit(solution)/shard_map/ppermute | solution.py:149
  119.3 12.7 %collective-permute-start.23 = (bf16[512,256]{1,0:T(8,128)(2,1)S(1)}, bf16[512,256]{1,0:T(8,128)(2,1)S(1)}, u32[]{:S(2)}, u32[]{:S(2)}) collective-permute-start(bf16[512,256]{1,0:T(8,128)(2,1)S(1)} %gated_sections.1), channel_id=1, source_target_pairs={{0,18},{1,19},{2,16},{3,17},{16,2},{17,3},{18,0},{19,1},{4,22},{5,... | collective-permute-start | bytes 786440 | tf_op jit(solution)/shard_map/ppermute | solution.py:157
  126.0 7.1 %collective-permute-start.19 = (bf16[512,256]{1,0:T(8,128)(2,1)S(1)}, bf16[512,256]{1,0:T(8,128)(2,1)S(1)}, u32[]{:S(2)}, u32[]{:S(2)}) collective-permute-start(bf16[512,256]{1,0:T(8,128)(2,1)S(1)} %late_sections.1.refs_8_), channel_id=1, source_target_pairs={{0,2},{1,3},{2,0},{3,1},{4,6},{5,7},{6,4},{7,5},{8,10},{9,11},{10,... | collective-permute-start | bytes 786440 | tf_op jit(solution)/shard_map/ppermute | solution.py:149
  126.6 6.5 %collective-permute-start.18 = (bf16[512,256]{1,0:T(8,128)(2,1)S(1)}, bf16[512,256]{1,0:T(8,128)(2,1)S(1)}, u32[]{:S(2)}, u32[]{:S(2)}) collective-permute-start(bf16[512,256]{1,0:T(8,128)(2,1)S(1)} %late_sections.1.refs_8_), channel_id=1, source_target_pairs={{0,1},{1,0},{2,3},{3,2},{4,5},{5,4},{6,7},{7,6},{8,9},{9,8},{10,11... | collective-permute-start | bytes 786440 | tf_op jit(solution)/shard_map/ppermute | solution.py:149
  126.6 10.0 %collective-permute-start.15 = (bf16[256,512]{1,0:T(8,128)(2,1)}, bf16[256,512]{1,0:T(8,128)(2,1)S(1)}, u32[]{:S(2)}, u32[]{:S(2)}) collective-permute-start(bf16[256,512]{1,0:T(8,128)(2,1)} %collective-permute-done.12.refs_3_), channel_id=1, source_target_pairs={{0,16},{16,0},{1,17},{17,1},{2,18},{18,2},{3,19},{19,3},{4,20},{20... | collective-permute-start | bytes 786440 | tf_op jit(solution)/shard_map/ppermute | solution.py:149
  131.9 4.7 %collective-permute-start.22 = (bf16[512,256]{1,0:T(8,128)(2,1)S(1)}, bf16[512,256]{1,0:T(8,128)(2,1)S(1)}, u32[]{:S(2)}, u32[]{:S(2)}) collective-permute-start(bf16[512,256]{1,0:T(8,128)(2,1)S(1)} %collective-permute-done.21.refs_12_), channel_id=1, source_target_pairs={{0,1},{1,0},{2,3},{3,2},{4,5},{5,4},{6,7},{7,6},{8,9},{9,8},{10,11... | collective-permute-start | bytes 786440 | tf_op jit(solution)/shard_map/ppermute | solution.py:149
  131.9 4.7 %collective-permute-start.24 = (bf16[512,256]{1,0:T(8,128)(2,1)S(1)}, bf16[512,256]{1,0:T(8,128)(2,1)S(1)}, u32[]{:S(2)}, u32[]{:S(2)}) collective-permute-start(bf16[512,256]{1,0:T(8,128)(2,1)S(1)} %collective-permute-done.23.refs_14_), channel_id=1, source_target_pairs={{0,1},{1,0},{2,3},{3,2},{4,5},{5,4},{6,7},{7,6},{8,9},{9,8},{10,11... | collective-permute-start | bytes 786440 | tf_op jit(solution)/shard_map/ppermute | solution.py:149
  133.1 3.5 %collective-permute-start.20 = (bf16[512,256]{1,0:T(8,128)(2,1)S(1)}, bf16[512,256]{1,0:T(8,128)(2,1)S(1)}, u32[]{:S(2)}, u32[]{:S(2)}) collective-permute-start(bf16[512,256]{1,0:T(8,128)(2,1)S(1)} %collective-permute-done.19.refs_10_), channel_id=1, source_target_pairs={{0,1},{1,0},{2,3},{3,2},{4,5},{5,4},{6,7},{7,6},{8,9},{9,8},{10,11... | collective-permute-start | bytes 786440 | tf_op jit(solution)/shard_map/ppermute | solution.py:149
Sparse Core Ops, SparseCore 0:
  9.2 66.2 all-gather.4
  77.1 32.3 all-gather.6
